TPU v7x, 32 devices: a whole 2x2x4 slice. The times are simulated.
32 devices in a mesh: view: 4 (over y, core), slab: 8 (over z, x).
Axes of the slice: x: 2, y: 2, z: 4, core: 2. Of those that a mesh axis runs over, the one named last changes fastest.
Arguments:
- estimate: float32 [2, 128, 128, 1024], P(None, 'slab', 'view'), may hold values from 0.2 to 5
- recorded: bfloat16 [2, 2, 128, 128, 1024], P(None, None, None, 'view', 'slab'), may hold values from 0.19921875 to 5
- psf_lateral: float32 [2, 2, 31], replicated, may hold values from 0.0007 to 1.5, as said below
- psf_axial: float32 [2, 127], replicated, may hold values from 0.0007 to 1.5, as said below
- offsets: int32 [2, 2], replicated, may hold values from -8 to 8, as said below
Outputs:
- updated: float32 [2, 128, 128, 1024], P(None, 'slab', 'view')
Inputs may be any that keep to these rules, and one draw needn't show every extreme that they name: offsets[v] is imaging direction v's voxel shift along x and along y; the magnitude 8 occurs with both signs. `psf_lateral`: positive lateral taps. `psf_axial`: positive axial taps.
All inputs are finite; a program needn't handle non-finite values.
Results may differ from a plain program's by a relative error of at most 0.0003.
Values sent between devices are 32-bit elements; how exact they have to be, the bound alone decides.
No kernel may reach another device: no remote copies, remote signals or barrier semaphores. Data moves between devices by JAX's collectives and lax.ppermute only.
A program may use at most 128 MiB of HBM per device.

v0:
```python
import jax
import jax.numpy as jnp
from jax import lax
from jax.sharding import PartitionSpec as P

Z = 128
YBLK = 128
HALO = 23


BACKGROUND = 0.05
HIGHEST = lax.Precision.HIGHEST


def with_halo(value, sides, width):
    for axis, dim in sides:
        peers, length = (lax.axis_size(axis), value.shape[dim])
        up = [(i, (i + 1) % peers) for i in range(peers - 1)]
        down = [(j, i) for i, j in up]
        last = lax.slice_in_dim(value, length - width, length, axis=dim)
        leading = lax.slice_in_dim(value, 0, width, axis=dim)
        before = lax.ppermute(last, axis, up)
        after = lax.ppermute(leading, axis, down)
        value = jnp.concatenate([before, value, after], axis=dim)
    return value


def unit_taps(weights):
    return weights / jnp.sum(weights)


def band_table(weights, places):
    levels = jnp.arange(weights.shape[0], dtype=jnp.int32)
    return jnp.sum(jnp.where(places[..., None] == levels, weights, 0.0), axis=-1)


def margin_matrix(weights, offset, length, margin, adjoint):
    centre = (weights.shape[0] - 1) // 2
    outputs = jnp.arange(length, dtype=jnp.int32)[:, None]
    sources = jnp.arange(length + 2 * margin, dtype=jnp.int32)[None, :] - margin
    apart = sources - outputs
    if adjoint:
        apart = -apart
    return band_table(weights, apart - offset + centre)


def blocked_rows(field, weights, offset, width_blk, adjoint):
    extent = field.shape
    blocks = extent[3] // width_blk
    pieces = field.reshape(extent[0], extent[1], extent[2], blocks, width_blk)
    padded = jnp.pad(pieces, ((0, 0), (0, 0), (0, 0), (1, 1), (0, 0)))
    centre = (weights.shape[0] - 1) // 2
    sources = jnp.arange(width_blk, dtype=jnp.int32)[:, None]
    outputs = jnp.arange(width_blk, dtype=jnp.int32)[None, :]
    result = jnp.zeros(pieces.shape, jnp.float32)
    for shifted in range(3):
        apart = (shifted - 1) * width_blk + sources - outputs
        if adjoint:
            apart = -apart
        matrix = band_table(weights, apart - offset + centre)
        result = result + jnp.einsum(
            "czxkj,ji->czxki",
            padded[:, :, :, shifted : shifted + blocks],
            matrix,
            precision=HIGHEST,
        )
    return result.reshape(extent)


def shards(estimate, recorded, psf_lateral, psf_axial, offsets):
    views_n = recorded.shape[0]
    along_x = [unit_taps(psf_lateral[which, 0]) for which in range(views_n)]
    along_y = [unit_taps(psf_lateral[which, 1]) for which in range(views_n)]
    rows_at = jnp.arange(Z, dtype=jnp.int32)[:, None]
    cols_at = jnp.arange(Z, dtype=jnp.int32)[None, :]
    axial_places = cols_at - rows_at + (psf_axial.shape[1] - 1) // 2
    axial = [band_table(unit_taps(psf_axial[which]), axial_places) for which in range(views_n)]
    x_rows = estimate.shape[2]
    widened = with_halo(estimate, (("view", 2),), HALO)
    blurred = []
    for which in range(views_n):
        across = margin_matrix(along_x[which], offsets[which, 0], x_rows, HALO, False)
        sectioned = jnp.einsum("ab,czby->czay", across, widened, precision=HIGHEST)
        blurred.append(blocked_rows(sectioned, along_y[which], offsets[which, 1], YBLK, False))
    columns = lax.all_to_all(jnp.stack(blurred), "slab", split_axis=4, concat_axis=2, tiled=True)
    spread = []
    for which in range(views_n):
        imaged = jnp.einsum("oi,cixy->coxy", axial[which], columns[which], precision=HIGHEST)
        quotient = recorded[which].astype(jnp.float32) / (imaged + BACKGROUND)
        spread.append(jnp.einsum("oi,coxy->cixy", axial[which], quotient, precision=HIGHEST))
    planes = lax.all_to_all(jnp.stack(spread), "slab", split_axis=2, concat_axis=4, tiled=True)
    returned = [
        blocked_rows(planes[which], along_y[which], offsets[which, 1], YBLK, True)
        for which in range(views_n)
    ]
    fringe = with_halo(jnp.stack(returned), (("view", 3),), HALO)
    summed = jnp.zeros(estimate.shape, jnp.float32)
    for which in range(views_n):
        across = margin_matrix(along_x[which], offsets[which, 0], x_rows, HALO, True)
        summed = summed + jnp.einsum("ab,czby->czay", across, fringe[which], precision=HIGHEST)
    return estimate * (summed / views_n)


def solution(mesh):
    in_specs = (P(None, "slab", "view", None), P(None, None, None, "view", "slab"), P(), P(), P())
    out_specs = P(None, "slab", "view", None)
    return jax.shard_map(shards, mesh=mesh, in_specs=in_specs, out_specs=out_specs, check_vma=False)
```

profile of v0, /device:TPU:1, one launch (start us, length us, event | category | flops | bytes accessed | tf_op | source)
XLA Modules:
  0.0 831.5 jit_solution(896550517628313579)
XLA Ops:
  30.3 12.5 %collective-permute-done = f32[2,16,23,1024]{3,1,2,0:T(8,128)S(1)} collective-permute-done((f32[2,16,23,1024]{3,1,2,0:T(8,128)S(1)}, f32[2,16,23,1024]{3,1,2,0:T(8,128)S(1)}, u32[]{:S(2)}, u32[]{:S(2)}) %collective-permute-start) | collective-permute-done | bytes 3014688 | tf_op jit(solution)/shard_map/ppermute | solution.py:22
  50.7 11.1 %fusion.3 = f32[2,16,1024,32]{2,3,1,0:T(8,128)S(1)} fusion(f32[2,16,23,1024]{3,2,1,0:T(8,128)S(1)} %copy.64, f32[2,16,32,1024]{3,2,1,0:T(8,128)S(1)} %copy-done, f32[2,16,23,1024]{3,2,1,0:T(8,128)S(1)} %copy.63, f32[32,78]{1,0:T(8,128)S(1)} %get-tuple-element.61), kind=kOutput, calls=%fused_computation.21 | convolution fusion | flops 986578944 | bytes 14427904 | tf_op jit(solution)/shard_map/ab,czby->czay/dot_general | solution.py:83
  79.9 13.7 %fusion.2 = f32[2,16,1024,32]{2,3,1,0:T(8,128)S(1)} fusion(f32[2,16,23,1024]{3,2,1,0:T(8,128)} %copy-done.4, f32[2,16,32,1024]{3,2,1,0:T(8,128)} %param.5, f32[2,16,23,1024]{3,2,1,0:T(8,128)S(1)} %copy.63, f32[32,78]{1,0:T(8,128)S(1)} %get-tuple-element.16), kind=kOutput, calls=%fused_computation.20 | convolution fusion | flops 986578944 | bytes 14427904 | tf_op jit(solution)/shard_map/ab,czby->czay/dot_general | solution.py:83
  111.2 8.3 %pad_maximum_fusion.2 = f32[2,2,16,32,1024]{4,3,2,1,0:T(8,128)} fusion(f32[1,2,16,32,1024]{4,3,2,1,0:T(8,128)} %stack_reshape.13, f32[1,2,16,32,1024]{4,3,2,1,0:T(8,128)} %stack_reshape.12), kind=kLoop, calls=%fused_computation.14 | loop fusion | flops 2097152 | bytes 16777216 | tf_op jit(solution)/shard_map/stack | solution.py:85
  119.6 26.6 %copy.65 = f32[2,2,16,32,1024]{3,2,1,0,4:T(8,128)} copy(f32[2,2,16,32,1024]{4,3,2,1,0:T(8,128)} %pad_maximum_fusion.2) | data formatting | bytes 16777216 | tf_op jit(solution)/shard_map/stack | solution.py:85
  146.1 20.5 %reshape.373 = f32[8,1,262144]{2,1,0:T(1,128)} reshape(f32[1024,2,2,16,32]{4,3,2,1,0:T(8,128)} %bitcast.192) | data formatting | bytes 16777216
  166.6 5.5 all-to-all-start
  187.9 150.7 %all-to-all-done = f32[8,1,262144]{2,1,0:T(1,128)} async-done(((f32[8,1,262144]{2,1,0:T(1,128)}), f32[8,1,262144]{2,1,0:T(1,128)}, u32[]{:S(2)}, u32[]{:S(2)}) %all-to-all-start) | async-done | bytes 8388640 | tf_op jit(solution)/shard_map/all_to_all | solution.py:85
  339.1 26.4 %reduce.6 = f32[8,262144]{1,0:T(8,128)} reduce(f32[8,1,262144]{2,1,0:T(1,128)} %all-to-all-done, f32[]{:T(128)} %broadcast.385), dimensions={1}, to_apply=%all_to_all.22.reduce_sub_computation | reduce | bytes 16777220 | tf_op jit(solution)/shard_map/all_to_all | solution.py:85
  365.5 25.3 %reshape.374 = f32[1024,2,2,16,32]{4,3,2,1,0:T(8,128)} reshape(f32[8,262144]{1,0:T(8,128)} %reduce.6) | data formatting | bytes 16777216
  390.7 18.4 %copy.97 = f32[2,2,16,32,8,128]{5,4,3,2,1,0:T(8,128)} copy(f32[2,2,16,32,8,128]{3,2,1,0,5,4:T(8,128)} %bitcast.193) | data formatting | bytes 16777216 | tf_op jit(solution)/shard_map/all_to_all | solution.py:85
  414.8 8.4 %fusion.18 = f32[2,32,128,128]{3,2,1,0:T(8,128)S(1)} fusion(f32[2,128,32,128]{3,2,1,0:T(8,128)S(1)} %bitcast.206, f32[128,128]{1,0:T(8,128)S(1)} %get-tuple-element.5), kind=kOutput, calls=%fused_computation.41 | convolution fusion | flops 1610612736 | bytes 8454144 | tf_op jit(solution)/shard_map/oi,cixy->coxy/dot_general | solution.py:88
  427.3 8.4 %fusion.16 = f32[2,32,128,128]{3,2,1,0:T(8,128)S(1)} fusion(f32[2,128,32,128]{3,2,1,0:T(8,128)S(1)} %bitcast.205, f32[128,128]{1,0:T(8,128)S(1)} %get-tuple-element.6), kind=kOutput, calls=%fused_computation.39 | convolution fusion | flops 1610612736 | bytes 8454144 | tf_op jit(solution)/shard_map/oi,cixy->coxy/dot_general | solution.py:88
  443.8 10.3 %copy.72 = f32[2,2,128,32,128]{4,3,1,0,2:T(8,128)} copy(f32[2,2,128,32,128]{2,4,3,1,0:T(8,128)} %pad_maximum_fusion.3) | data formatting | bytes 16777216 | tf_op jit(solution)/shard_map/stack | solution.py:91
  454.1 187.0 %all_to_all.30 = f32[2,2,128,32,128]{4,3,1,0,2:T(8,128)S(1)} all-to-all(f32[2,2,128,32,128]{4,3,1,0,2:T(8,128)} %copy.72), channel_id=1, replica_groups=mesh['view'=4,'slab'=8] {'slab'}, dimensions={2} | all-to-all | bytes 16777216 | tf_op jit(solution)/shard_map/all_to_all | solution.py:91
  641.1 8.1 copy.111
  670.6 5.3 fusion.33
  696.6 9.5 %fusion.68 = (f32[2,2,16,23,1024]{4,3,2,1,0:T(8,128)}, f32[2,2,16,23,1024]{4,3,2,1,0:T(8,128)S(1)}) fusion(f32[2,2,16,32,1024]{4,3,2,1,0:T(8,128)} %constant_dynamic-update-slice_fusion), kind=kLoop, calls=%fused_computation.165 | loop fusion | bytes 24117248 | tf_op jit(solution)/shard_map/slice | solution.py:20
  706.2 6.3 copy.75
  721.8 59.3 %collective-permute-done.2 = f32[2,2,16,23,1024]{4,2,3,1,0:T(8,128)S(1)} collective-permute-done((f32[2,2,16,23,1024]{4,2,3,1,0:T(8,128)S(1)}, f32[2,2,16,23,1024]{4,2,3,1,0:T(8,128)S(1)}, u32[]{:S(2)}, u32[]{:S(2)}) %collective-permute-start.2) | collective-permute-done | bytes 6029344 | tf_op jit(solution)/shard_map/ppermute | solution.py:22
  789.4 6.2 copy.78
  795.6 8.4 %pad_maximum_fusion = f32[2,2,16,78,1024]{4,3,2,1,0:T(8,128)S(1)} fusion(f32[2,2,16,23,1024]{4,3,2,1,0:T(8,128)} %copy.78, f32[2,2,16,32,1024]{4,3,2,1,0:T(8,128)} %constant_dynamic-update-slice_fusion, f32[2,2,16,23,1024]{4,3,2,1,0:T(8,128)S(1)} %copy.77), kind=kLoop, calls=%fused_computation | loop fusion | flops 10223616 | bytes 40894464 | tf_op jit(solution)/shard_map/concatenate | solution.py:24
  804.1 12.3 %fusion = f32[2,16,1024,32]{2,3,1,0:T(8,128)} fusion(f32[2,2,16,78,1024]{4,3,2,1,0:T(8,128)S(1)} %pad_maximum_fusion, f32[32,78]{1,0:T(8,128)S(1)} %copy-done.15), kind=kOutput, calls=%fused_computation.2 | convolution fusion | flops 981467136 | bytes 14696448 | tf_op jit(solution)/shard_map/ab,czby->czay/dot_general | solution.py:100
  816.4 14.9 %bitcast_multiply_fusion = f32[2,16,32,1024]{3,2,1,0:T(8,128)} fusion(f32[2,16,32,1024]{3,2,1,0:T(8,128)S(1)} %copy-done.1, f32[2,16,1024,32]{2,3,1,0:T(8,128)} %fusion, f32[2,2,16,78,1024]{4,3,2,1,0:T(8,128)S(1)} %pad_maximum_fusion, f32[32,78]{1,0:T(8,128)S(1)} %copy-done.14), kind=kOutput, calls=%fused_computation.36 | convolution fusion | flops 984612864 | bytes 23085056 | tf_op jit(solution)/shard_map/ab,czby->czay/dot_general | solution.py:100
  (100 shorter events, 167.4 us)
Async XLA Ops:
  5.5 8.3 copy-start.18
  5.5 9.0 %copy-start.16 = (f32[2,2,31]{2,1,0:T(2,128)S(1)}, f32[2,2,31]{2,1,0:T(2,128)}, u32[]{:S(2)}) copy-start(f32[2,2,31]{2,1,0:T(2,128)} %param.7) | copy-start | bytes 1492
  5.5 37.3 %collective-permute-start = (f32[2,16,23,1024]{3,1,2,0:T(8,128)S(1)}, f32[2,16,23,1024]{3,1,2,0:T(8,128)S(1)}, u32[]{:S(2)}, u32[]{:S(2)}) collective-permute-start(f32[2,16,23,1024]{3,1,2,0:T(8,128)S(1)} %copy.101), channel_id=1, source_target_pairs={{0,8},{8,16},{16,24},{1,9},{9,17},{17,25},{2,10},{10,18},{18,26},{... | collective-permute-start | bytes 9043976 | tf_op jit(solution)/shard_map/ppermute | solution.py:22
  11.8 37.2 %collective-permute-start.1 = (f32[2,16,23,1024]{3,1,2,0:T(8,128)S(1)}, f32[2,16,23,1024]{3,1,2,0:T(8,128)S(1)}, u32[]{:S(2)}, u32[]{:S(2)}) collective-permute-start(f32[2,16,23,1024]{3,1,2,0:T(8,128)S(1)} %copy.102), channel_id=1, source_target_pairs={{8,0},{16,8},{24,16},{9,1},{17,9},{25,17},{10,2},{18,10},{26,18},{... | collective-permute-start | bytes 9043976 | tf_op jit(solution)/shard_map/ppermute | solution.py:23
  44.6 6.2 copy-start
  50.7 11.1 %copy-start.4 = (f32[2,16,23,1024]{3,2,1,0:T(8,128)}, f32[2,16,23,1024]{3,2,1,0:T(8,128)S(1)}, u32[]{:S(2)}) copy-start(f32[2,16,23,1024]{3,2,1,0:T(8,128)S(1)} %copy.64) | copy-start | bytes 9043972
  166.6 172.0 %all-to-all-start = ((f32[8,1,262144]{2,1,0:T(1,128)}), f32[8,1,262144]{2,1,0:T(1,128)}, u32[]{:S(2)}, u32[]{:S(2)}) async-start(f32[8,1,262144]{2,1,0:T(1,128)} %reshape.373), calls=%async_computation | async-start | bytes 16777216 | tf_op jit(solution)/shard_map/all_to_all | solution.py:85
  176.6 7.5 copy-start.17
  414.8 8.4 %copy-start.7 = (bf16[1,2,128,32,128]{2,4,3,1,0:T(8,128)(2,1)S(1)}, bf16[1,2,128,32,128]{2,4,3,1,0:T(8,128)(2,1)}, u32[]{:S(2)}) copy-start(bf16[1,2,128,32,128]{2,4,3,1,0:T(8,128)(2,1)} %copy.100) | copy-start | bytes 6291460
  427.3 8.4 %copy-start.6 = (bf16[1,2,128,32,128]{2,4,3,1,0:T(8,128)(2,1)S(1)}, bf16[1,2,128,32,128]{2,4,3,1,0:T(8,128)(2,1)}, u32[]{:S(2)}) copy-start(bf16[1,2,128,32,128]{2,4,3,1,0:T(8,128)(2,1)} %copy.103) | copy-start | bytes 6291460
  649.2 4.5 copy-start.2
  649.2 4.5 copy-start.13
  653.7 3.6 copy-start.12
  657.3 3.4 copy-start.11
  665.7 4.9 copy-start.10
  670.6 5.4 copy-start.3
  670.6 5.4 copy-start.9
  676.0 3.4 copy-start.8
  689.5 4.9 copy-start.5
  712.4 68.7 %collective-permute-start.2 = (f32[2,2,16,23,1024]{4,2,3,1,0:T(8,128)S(1)}, f32[2,2,16,23,1024]{4,2,3,1,0:T(8,128)S(1)}, u32[]{:S(2)}, u32[]{:S(2)}) collective-permute-start(f32[2,2,16,23,1024]{4,2,3,1,0:T(8,128)S(1)} %copy.75), channel_id=1, source_target_pairs={{0,8},{8,16},{16,24},{1,9},{9,17},{17,25},{2,10},{10,18},{18,26},{... | collective-permute-start | bytes 18087944 | tf_op jit(solution)/shard_map/ppermute | solution.py:22
  719.9 69.5 %collective-permute-start.3 = (f32[2,2,16,23,1024]{4,2,3,1,0:T(8,128)S(1)}, f32[2,2,16,23,1024]{4,2,3,1,0:T(8,128)S(1)}, u32[]{:S(2)}, u32[]{:S(2)}) collective-permute-start(f32[2,2,16,23,1024]{4,2,3,1,0:T(8,128)S(1)} %copy.76), channel_id=1, source_target_pairs={{8,0},{16,8},{24,16},{9,1},{17,9},{25,17},{10,2},{18,10},{26,18},{... | collective-permute-start | bytes 18087944 | tf_op jit(solution)/shard_map/ppermute | solution.py:23
  795.6 8.4 %copy-start.15 = (f32[32,78]{1,0:T(8,128)S(1)}, f32[32,78]{1,0:T(8,128)}, u32[]{:S(2)}) copy-start(f32[32,78]{1,0:T(8,128)} %get-tuple-element.15) | copy-start | bytes 29956
  804.0 12.3 %copy-start.1 = (f32[2,16,32,1024]{3,2,1,0:T(8,128)S(1)}, f32[2,16,32,1024]{3,2,1,0:T(8,128)}, u32[]{:S(2)}) copy-start(f32[2,16,32,1024]{3,2,1,0:T(8,128)} %param.5) | copy-start | bytes 12582916
  804.1 12.3 %copy-start.14 = (f32[32,78]{1,0:T(8,128)S(1)}, f32[32,78]{1,0:T(8,128)}, u32[]{:S(2)}) copy-start(f32[32,78]{1,0:T(8,128)} %get-tuple-element.62) | copy-start | bytes 29956
where the time goes:
time: 839 us; the launch traced here: 831 us
  waiting for transfers between devices  232 us (28%)
  local copies, waits for them, and re-layouts  201 us (24%)
  blocking collectives  187 us (22%)
  matrix products  126 us (15%)
  other arithmetic  66.6 us (8%)
  starting transfers between devices  17.9 us (2%)
    all_to_all x1, blocking collectives, shards(): lax.all_to_all(jnp.stack(spread), 'slab', split_axis=2, concat_axis=4, ti...  187 us
    all_to_all x1, waiting for transfers between devices, shards(): lax.all_to_all(jnp.stack(blurred), 'slab', split_axis=4, concat_axis=2, t...  151 us
    ppermute x2, waiting for transfers between devices, with_halo(): before = lax.ppermute(last, axis, up)  71.8 us
    unnamed x47, local copies, waits for them, and re-layouts  65 us
    dot_general x12, matrix products, blocked_rows(): jnp.einsum('czxkj,ji->czxki', padded[:, :, :, shifted:shifted + blocks],...  49.3 us
    another operation x3, local copies, waits for them, and re-layouts, shards(): jnp.stack(blurred)  36.7 us
    dot_general x2, matrix products, shards(): jnp.einsum('ab,czby->czay', across, fringe[which], precision=HIGHEST)  27.2 us
    all_to_all x1, other arithmetic, shards(): lax.all_to_all(jnp.stack(blurred), 'slab', split_axis=4, concat_axis=2, t...  26.4 us
  transfers between devices with their start and end apart: 5, of which 5 were waited for; matrix products, arithmetic and copies ran while one was open for 5% of the time, Pallas kernels for 0%

commit v1 on v0

--- a/solution.py
+++ b/solution.py
@@ -1,15 +1,20 @@
+import functools
+
 import jax
 import jax.numpy as jnp
 from jax import lax
+from jax.experimental import pallas as pl
+from jax.experimental.pallas import tpu as pltpu
 from jax.sharding import PartitionSpec as P
 
-Z = 128
-YBLK = 128
 HALO = 23
-
-
 BACKGROUND = 0.05
 HIGHEST = lax.Precision.HIGHEST
+LANES = 128
+EDGE = 24
+F32 = jnp.float32
+BF16 = jnp.bfloat16
+VMEM_LIMIT = 58 * 1024 * 1024
 
 
 def with_halo(value, sides, width):
@@ -52,7 +57,7 @@
     centre = (weights.shape[0] - 1) // 2
     sources = jnp.arange(width_blk, dtype=jnp.int32)[:, None]
     outputs = jnp.arange(width_blk, dtype=jnp.int32)[None, :]
-    result = jnp.zeros(pieces.shape, jnp.float32)
+    result = jnp.zeros(pieces.shape, F32)
     for shifted in range(3):
         apart = (shifted - 1) * width_blk + sources - outputs
         if adjoint:
@@ -67,12 +72,12 @@
     return result.reshape(extent)
 
 
-def shards(estimate, recorded, psf_lateral, psf_axial, offsets):
-    views_n = recorded.shape[0]
+def general_shards(estimate, recorded, psf_lateral, psf_axial, offsets):
+    views_n, planes_n = recorded.shape[0], recorded.shape[2]
     along_x = [unit_taps(psf_lateral[which, 0]) for which in range(views_n)]
     along_y = [unit_taps(psf_lateral[which, 1]) for which in range(views_n)]
-    rows_at = jnp.arange(Z, dtype=jnp.int32)[:, None]
-    cols_at = jnp.arange(Z, dtype=jnp.int32)[None, :]
+    rows_at = jnp.arange(planes_n, dtype=jnp.int32)[:, None]
+    cols_at = jnp.arange(planes_n, dtype=jnp.int32)[None, :]
     axial_places = cols_at - rows_at + (psf_axial.shape[1] - 1) // 2
     axial = [band_table(unit_taps(psf_axial[which]), axial_places) for which in range(views_n)]
     x_rows = estimate.shape[2]
@@ -81,26 +86,396 @@
     for which in range(views_n):
         across = margin_matrix(along_x[which], offsets[which, 0], x_rows, HALO, False)
         sectioned = jnp.einsum("ab,czby->czay", across, widened, precision=HIGHEST)
-        blurred.append(blocked_rows(sectioned, along_y[which], offsets[which, 1], YBLK, False))
+        blurred.append(blocked_rows(sectioned, along_y[which], offsets[which, 1], LANES, False))
     columns = lax.all_to_all(jnp.stack(blurred), "slab", split_axis=4, concat_axis=2, tiled=True)
     spread = []
     for which in range(views_n):
         imaged = jnp.einsum("oi,cixy->coxy", axial[which], columns[which], precision=HIGHEST)
-        quotient = recorded[which].astype(jnp.float32) / (imaged + BACKGROUND)
+        quotient = recorded[which].astype(F32) / (imaged + BACKGROUND)
         spread.append(jnp.einsum("oi,coxy->cixy", axial[which], quotient, precision=HIGHEST))
     planes = lax.all_to_all(jnp.stack(spread), "slab", split_axis=2, concat_axis=4, tiled=True)
     returned = [
-        blocked_rows(planes[which], along_y[which], offsets[which, 1], YBLK, True)
+        blocked_rows(planes[which], along_y[which], offsets[which, 1], LANES, True)
         for which in range(views_n)
     ]
     fringe = with_halo(jnp.stack(returned), (("view", 3),), HALO)
-    summed = jnp.zeros(estimate.shape, jnp.float32)
+    summed = jnp.zeros(estimate.shape, F32)
     for which in range(views_n):
         across = margin_matrix(along_x[which], offsets[which, 0], x_rows, HALO, True)
         summed = summed + jnp.einsum("ab,czby->czay", across, fringe[which], precision=HIGHEST)
     return estimate * (summed / views_n)
 
 
+def params():
+    return pltpu.CompilerParams(vmem_limit_bytes=VMEM_LIMIT)
+
+
+def cost(flops, moved):
+    return pl.CostEstimate(flops=flops, bytes_accessed=moved, transcendentals=0)
+
+
+def upward(value, axis):
+    return lax.ppermute(value, axis, [(i, i + 1) for i in range(lax.axis_size(axis) - 1)])
+
+
+def downward(value, axis):
+    return lax.ppermute(value, axis, [(i + 1, i) for i in range(lax.axis_size(axis) - 1)])
+
+
+def split(value):
+    high = value.astype(BF16)
+    return high, (value - high.astype(F32)).astype(BF16)
+
+
+def mm(a, b):
+    return jnp.dot(a, b, preferred_element_type=F32)
+
+
+def tables_kernel(y_taps, z_taps, offs, yh, yl, ah, al, zh, zl, th, tl):
+    views, taps = y_taps.shape
+    axial = z_taps.shape[1]
+    size = LANES
+    rows = lax.broadcasted_iota(jnp.int32, (size, size), 0)
+    cols = lax.broadcasted_iota(jnp.int32, (size, size), 1)
+    halo_row = jnp.where(rows < EDGE, rows - EDGE, rows - EDGE + size)
+    halo_col = jnp.where(cols < EDGE, cols - EDGE, cols - EDGE + size)
+    for v in range(views):
+        shift = offs[v, 1] - (taps - 1) // 2
+        lanes = slice(v * size, (v + 1) * size)
+        places = [rows - cols - shift, halo_row - cols - shift, cols - rows - shift, halo_col - rows - shift]
+        limits = [None, rows < 2 * EDGE, None, cols < 2 * EDGE]
+        for n, (place, limit) in enumerate(zip(places, limits)):
+            acc = jnp.zeros((size, size), F32)
+            for k in range(taps):
+                acc = jnp.where(place == k, y_taps[v, k], acc)
+            if limit is not None:
+                acc = jnp.where(limit, acc, 0.0)
+            high, low = split(acc)
+            block = slice((n % 2) * size, (n % 2 + 1) * size)
+            if n < 2:
+                yh[block, lanes] = high
+                yl[block, lanes] = low
+            else:
+                ah[lanes, block] = high
+                al[lanes, block] = low
+        centre = (axial - 1) // 2
+
+        def taps_of(place):
+            def step(k, acc):
+                return jnp.where(place == k, z_taps[v, k], acc)
+
+            return lax.fori_loop(0, axial, step, jnp.zeros((size, size), F32))
+
+        zh[v], zl[v] = split(taps_of(cols - rows + centre))
+        th[v], tl[v] = split(taps_of(rows - cols + centre))
+
+
+def make_tables(y_taps, z_taps, offsets):
+    smem = pl.BlockSpec(memory_space=pltpu.SMEM)
+    vmem = pl.BlockSpec(memory_space=pltpu.VMEM)
+    views = y_taps.shape[0]
+    wide = jax.ShapeDtypeStruct((2 * LANES, views * LANES), BF16)
+    tall = jax.ShapeDtypeStruct((views * LANES, 2 * LANES), BF16)
+    deep = jax.ShapeDtypeStruct((views, LANES, LANES), BF16)
+    return pl.pallas_call(
+        tables_kernel,
+        out_shape=(wide, wide, tall, tall, deep, deep, deep, deep),
+        in_specs=[smem] * 3,
+        out_specs=(vmem,) * 8,
+        compiler_params=params(),
+        cost_estimate=cost(10_000_000, 1_000_000),
+        name="tables",
+    )(y_taps, z_taps, offsets)
+
+
+def swap_kernel(source, target):
+    target[0] = jnp.swapaxes(source[0], 0, 1)
+
+
+def send_blocks(estimate, c, peers):
+    _, planes, rows, columns = estimate.shape
+    width = columns // peers
+    return pl.pallas_call(
+        swap_kernel,
+        grid=(peers,),
+        in_specs=[pl.BlockSpec((1, planes, rows, width), lambda s: (c, 0, 0, s))],
+        out_specs=pl.BlockSpec((1, rows, planes, width), lambda s: (s, 0, 0, 0)),
+        out_shape=jax.ShapeDtypeStruct((peers, rows, planes, width), F32),
+        compiler_params=params(),
+        cost_estimate=cost(0, 8 * planes * rows * columns),
+        name="send_blocks",
+    )(estimate)
+
+
+def record_kernel(source, target):
+    target[0, 0] = jnp.swapaxes(source[0, 0].astype(F32), 0, 1).astype(BF16)
+
+
+def record_rows(recorded):
+    views, colours, planes, rows, width = recorded.shape
+    step = 16
+    return pl.pallas_call(
+        record_kernel,
+        grid=(views, colours, planes // step),
+        in_specs=[pl.BlockSpec((1, 1, step, rows, width), lambda v, c, z: (v, c, z, 0, 0))],
+        out_specs=pl.BlockSpec((1, 1, rows, step, width), lambda v, c, z: (v, c, 0, z, 0)),
+        out_shape=jax.ShapeDtypeStruct((views, colours, rows, planes, width), BF16),
+        compiler_params=params(),
+        cost_estimate=cost(0, 4 * recorded.size),
+        name="record_rows",
+    )(recorded)
+
+
+def edges_kernel(source, first, last):
+    for x in range(source.shape[1]):
+        turned = source[:, x].reshape(-1, source.shape[3]).T
+        first[x] = turned[:EDGE]
+        last[x] = turned[-EDGE:]
+
+
+def column_edges(block):
+    peers, rows, planes, width = block.shape
+    step = 8
+    edge = jax.ShapeDtypeStruct((rows, EDGE, peers * planes), F32)
+    spec = pl.BlockSpec((step, EDGE, peers * planes), lambda x: (x, 0, 0))
+    return pl.pallas_call(
+        edges_kernel,
+        grid=(rows // step,),
+        in_specs=[pl.BlockSpec((peers, step, planes, width), lambda x: (0, x, 0, 0))],
+        out_specs=(spec, spec),
+        out_shape=(edge, edge),
+        compiler_params=params(),
+        cost_estimate=cost(0, 4 * block.size),
+        name="column_edges",
+    )(block)
+
+
+def correlate_kernel(
+    x_taps, offs, left, own, right, edge_l, edge_r, corner_l, corner_r, rec,
+    yh, yl, ah, al, zh, zl, th, tl, out_l, out_m, out_r, ext, mid,
+):
+    views, taps = x_taps.shape
+    rows = own.shape[1]
+    size = LANES
+    reach = (taps - 1) // 2
+    group = 4
+    zeros_tail = jnp.zeros((size - 2 * EDGE, size), F32)
+
+    def along_y(source, x0, halo, base):
+        mains, halos = [], []
+        for n in range(group):
+            mains.append(source[:, x0 + n].reshape(size, size))
+            halos.append(jnp.concatenate([*halo(x0 + n), zeros_tail], axis=0).T)
+        whole = jnp.concatenate([jnp.concatenate(mains, 0), jnp.concatenate(halos, 0)], axis=1)
+        high, low = split(whole)
+        done = mm(high, yh[...]) + mm(low, yh[...]) + mm(high, yl[...])
+        for v in range(views):
+            ext[v, pl.ds(base + x0, group)] = done[:, v * size : (v + 1) * size].reshape(group, size, size)
+
+    @pl.loop(0, EDGE // group)
+    def _(g):
+        along_y(left, g * group, lambda x: [corner_l[x]], 0)
+        along_y(right, g * group, lambda x: [corner_r[x]], EDGE + rows)
+
+    @pl.loop(0, rows // group)
+    def _(g):
+        along_y(own, g * group, lambda x: [edge_l[x], edge_r[x]], EDGE)
+
+    part = 32
+    for v in range(views):
+        weights = [jnp.full((8, size), x_taps[v, k], F32) for k in range(taps)]
+        begin = EDGE - reach + offs[v, 0]
+
+        @pl.loop(0, (rows // group) * (size // part))
+        def _(n):
+            x0 = (n // (size // part)) * group
+            z0 = pl.multiple_of((n % (size // part)) * part, part)
+            sums = [jnp.zeros((part // 8, 8, size), F32) for _ in range(group)]
+            for e in range(taps + group - 1):
+                value = ext[v, begin + x0 + e, pl.ds(z0, part)].reshape(part // 8, 8, size)
+                for j in range(group):
+                    if 0 <= e - j < taps:
+                        sums[j] = sums[j] + value * weights[e - j][None]
+            for j in range(group):
+                mid[v, x0 + j, pl.ds(z0, part)] = sums[j].reshape(part, size)
+
+    @pl.loop(0, rows // group)
+    def _(g):
+        x0 = g * group
+        for v in range(views):
+            high, low = split(jnp.concatenate([mid[v, x0 + n] for n in range(group)], axis=1))
+            image = mm(zh[v], high) + mm(zh[v], low) + mm(zl[v], high)
+            seen = jnp.concatenate([rec[v, 0, x0 + n].astype(F32) for n in range(group)], axis=1)
+            high, low = split(seen / (image + BACKGROUND))
+            back = mm(th[v], high) + mm(th[v], low) + mm(tl[v], high)
+            for n in range(group):
+                mid[v, x0 + n] = back[:, n * size : (n + 1) * size]
+
+    @pl.loop(0, 2 * EDGE + rows)
+    def _(e):
+        for v in range(views):
+            ext[v, e] = jnp.zeros((size, size), F32)
+
+    for v in range(views):
+        weights = [jnp.full((8, size), x_taps[v, k], F32) for k in range(taps)]
+        begin = EDGE - reach + offs[v, 0]
+
+        @pl.loop(0, (rows // group) * (size // part))
+        def _(n):
+            x0 = (n // (size // part)) * group
+            z0 = pl.multiple_of((n % (size // part)) * part, part)
+            values = [mid[v, x0 + j, pl.ds(z0, part)].reshape(part // 8, 8, size) for j in range(group)]
+            for e in range(taps + group - 1):
+                total = ext[v, begin + x0 + e, pl.ds(z0, part)].reshape(part // 8, 8, size)
+                for j in range(group):
+                    if 0 <= e - j < taps:
+                        total = total + values[j] * weights[e - j][None]
+                ext[v, begin + x0 + e, pl.ds(z0, part)] = total.reshape(part, size)
+
+    def back_y(target, x0, base):
+        both = [
+            jnp.concatenate([ext[v, base + x0 + n] for v in range(views)], axis=1) for n in range(group)
+        ]
+        high, low = split(jnp.concatenate(both, axis=0))
+        done = mm(high, ah[...]) + mm(low, ah[...]) + mm(high, al[...])
+        for n in range(group):
+            piece = done[n * size : (n + 1) * size]
+            target[x0 + n, :size] = piece[:, :size]
+            target[x0 + n, size:] = piece[:, size:].T[: 2 * EDGE]
+
+    @pl.loop(0, EDGE // group)
+    def _(g):
+        back_y(out_l, g * group, 0)
+        back_y(out_r, g * group, EDGE + rows)
+
+    @pl.loop(0, rows // group)
+    def _(g):
+        back_y(out_m, g * group, EDGE)
+
+
+def correlate(c, x_taps, offsets, left, own, right, edge_l, edge_r, corner_l, corner_r, rec, tables):
+    smem = pl.BlockSpec(memory_space=pltpu.SMEM)
+    vmem = pl.BlockSpec(memory_space=pltpu.VMEM)
+    rows = own.shape[1]
+    views = x_taps.shape[0]
+    tall = LANES + 2 * EDGE
+    side = jax.ShapeDtypeStruct((EDGE, tall, LANES), F32)
+    rec_spec = pl.BlockSpec((views, 1, rows, LANES, LANES), lambda i: (0, c, 0, 0, 0))
+    whole = [smem] * 2 + [vmem] * 7 + [rec_spec] + [vmem] * 8
+    return pl.pallas_call(
+        correlate_kernel,
+        grid=(1,),
+        out_shape=(side, jax.ShapeDtypeStruct((rows, tall, LANES), F32), side),
+        in_specs=whole,
+        out_specs=(vmem,) * 3,
+        scratch_shapes=[
+            pltpu.VMEM((views, 2 * EDGE + rows, LANES, LANES), F32),
+            pltpu.VMEM((views, rows, LANES, LANES), F32),
+        ],
+        compiler_params=params(),
+        cost_estimate=cost(20_000_000_000, 30_000_000),
+        name="correlate",
+    )(x_taps, offsets, left, own, right, edge_l, edge_r, corner_l, corner_r, rec, *tables)
+
+
+def gather_kernel(own, from_l, from_r, edge_l, edge_r, target):
+    rows, size = own.shape[0], LANES
+    gap = jnp.zeros((size - 2 * EDGE, size), F32)
+    for x in range(rows):
+        total = own[x, :size]
+        if x < EDGE:
+            total = total + from_l[x, :size]
+        if x >= rows - EDGE:
+            total = total + from_r[x - rows + EDGE, :size]
+        total = total + jnp.concatenate([edge_l[x], gap, edge_r[x]], axis=0).T
+        target[:, x] = total.reshape(target.shape[0], target.shape[2], size)
+
+
+def gather_sums(own, from_l, from_r, edge_l, edge_r, peers):
+    rows = own.shape[0]
+    planes = LANES // peers
+    vmem = pl.BlockSpec(memory_space=pltpu.VMEM)
+    return pl.pallas_call(
+        gather_kernel,
+        out_shape=jax.ShapeDtypeStruct((peers, rows, planes, LANES), F32),
+        in_specs=[vmem] * 5,
+        out_specs=vmem,
+        compiler_params=params(),
+        cost_estimate=cost(0, 10_000_000),
+        name="gather_sums",
+    )(own, from_l, from_r, edge_l, edge_r)
+
+
+def update(estimate, spread, c, views, held):
+    _, planes, rows, columns = estimate.shape
+    peers = spread.shape[0]
+    width = columns // peers
+    block = pl.BlockSpec((1, planes, rows, width), lambda s: (c, 0, 0, s))
+    extra = [] if held is None else [held]
+    return pl.pallas_call(
+        functools.partial(update_kernel, views),
+        grid=(peers,),
+        in_specs=[pl.BlockSpec((1, rows, planes, width), lambda s: (s, 0, 0, 0)), block]
+        + [pl.BlockSpec(memory_space=pl.ANY)] * len(extra),
+        out_specs=block,
+        out_shape=jax.ShapeDtypeStruct(estimate.shape, F32),
+        input_output_aliases={2: 0} if extra else {},
+        compiler_params=params(),
+        cost_estimate=cost(0, 12 * planes * rows * columns),
+        name="update",
+    )(spread, estimate, *extra)
+
+
+def update_kernel(views, spread, estimate, *rest):
+    rest[-1][0] = estimate[0] * (jnp.swapaxes(spread[0], 0, 1) / views)
+
+
+def fast_shards(estimate, recorded, psf_lateral, psf_axial, offsets):
+    views, colours = recorded.shape[:2]
+    rows = estimate.shape[2]
+    peers = lax.axis_size("slab")
+    lateral = psf_lateral / jnp.sum(psf_lateral, axis=-1, keepdims=True)
+    axial = psf_axial / jnp.sum(psf_axial, axis=-1, keepdims=True)
+    x_taps = lateral[:, 0]
+    tables = make_tables(lateral[:, 1], axial, offsets)
+    rec = record_rows(recorded)
+    blocks = [
+        lax.all_to_all(send_blocks(estimate, c, peers), "slab", 0, 0, tiled=True) for c in range(colours)
+    ]
+    result = None
+    for c in range(colours):
+        own = blocks[c]
+        left = upward(own[:, rows - EDGE :], "view")
+        right = downward(own[:, :EDGE], "view")
+        first, last = column_edges(own)
+        edge_l = upward(last, "slab")
+        edge_r = downward(first, "slab")
+        edges = jnp.concatenate([edge_l, edge_r], axis=1)
+        corner_l = upward(edges[rows - EDGE :], "view")
+        corner_r = downward(edges[:EDGE], "view")
+        to_l, mine, to_r = correlate(
+            c, x_taps, offsets, left, own, right, edge_l, edge_r, corner_l, corner_r, rec, tables
+        )
+        from_l = upward(to_r, "view")
+        from_r = downward(to_l, "view")
+        margin = mine[:, LANES:].at[:EDGE].add(from_l[:, LANES:])
+        margin = margin.at[rows - EDGE :].add(from_r[:, LANES:])
+        back_r = downward(margin[:, :EDGE], "slab")
+        back_l = upward(margin[:, EDGE:], "slab")
+        sums = gather_sums(mine, from_l, from_r, back_l, back_r, peers)
+        spread = lax.all_to_all(sums, "slab", 0, 0, tiled=True)
+        result = update(estimate, spread, c, views, result)
+    return result
+
+
+def shards(estimate, recorded, psf_lateral, psf_axial, offsets):
+    planes, rows, width = recorded.shape[2:]
+    fits = planes == LANES and width == LANES and rows % 8 == 0 and rows >= EDGE
+    fits = fits and estimate.shape[1] % 16 == 0
+    run = fast_shards if fits else general_shards
+    return run(estimate, recorded, psf_lateral, psf_axial, offsets)
+
+
 def solution(mesh):
     in_specs = (P(None, "slab", "view", None), P(None, None, None, "view", "slab"), P(), P(), P())
     out_specs = P(None, "slab", "view", None)

time: 839 us -> 405 us (0.48)
  local copies, waits for them, and re-layouts: 201 us -> 16.2 us
  Pallas kernels: 0 us -> 165 us
  waiting for transfers between devices: 232 us -> 82.9 us
  blocking collectives: 187 us -> 53.8 us
  matrix products: 126 us -> 0 us
  other arithmetic: 66.6 us -> 5.12 us
  starting transfers between devices: 17.9 us -> 76 us
    pallas_call x0 -> x12, Pallas kernels: none -> 165 us  [the longest x2 96.3 us: correlate(): pl.pallas_call(correlate_kernel, grid=(1,), out_shape=(side, jax.ShapeDty...]
    all_to_all x1, blocking collectives: 187 us -> 53.8 us  [fast_shards(): lax.all_to_all(send_blocks(estimate, c, peers), 'slab', 0, 0, tiled=True)]
    all_to_all x1 -> x3, waiting for transfers between devices: 151 us -> 20.2 us  [the longest x2 20.2 us: fast_shards(): spread = lax.all_to_all(sums, 'slab', 0, 0, tiled=True)]
    dot_general x20 -> x0, matrix products: 126 us -> none  [the longest x12 49.3 us: blocked_rows(): jnp.einsum('czxkj,ji->czxki', padded[:, :, :, shifted:shifted + blocks],...]
    another operation x8 -> x0, local copies, waits for them, and re-layouts: 62.2 us -> none  [the longest x3 36.7 us: shards(): jnp.stack(blurred)]
    unnamed x47 -> x38, local copies, waits for them, and re-layouts: 65 us -> 7.05 us
    ppermute x4 -> x20, starting transfers between devices: 12.3 us -> 58 us  [the longest x10 41 us: upward(): lax.ppermute(value, axis, [(i, i + 1) for i in range(lax.axis_size(axis)...]
    all_to_all x3 -> x0, local copies, waits for them, and re-layouts: 27 us -> none  [the longest x2 18.9 us: shards(): lax.all_to_all(jnp.stack(blurred), 'slab', split_axis=4, concat_axis=2, t...]
  transfers between devices with their start and end apart: 5 -> 23, of which waited for: 5 -> 9; matrix products, arithmetic and copies ran while one was open for 5% -> 4% of each run, Pallas kernels for 0% -> 37%
where the time goes in v1:
time: 405 us; the launch traced here: 400 us
  Pallas kernels  165 us (41%)
  waiting for transfers between devices  82.9 us (20%)
  starting transfers between devices  76 us (19%)
  blocking collectives  53.8 us (13%)
  local copies, waits for them, and re-layouts  16.2 us (4%)
  other arithmetic  5.12 us (1%)
    pallas_call x2, Pallas kernels, correlate(): pl.pallas_call(correlate_kernel, grid=(1,), out_shape=(side, jax.ShapeDty...  96.3 us
    all_to_all x1, blocking collectives, fast_shards(): lax.all_to_all(send_blocks(estimate, c, peers), 'slab', 0, 0, tiled=True)  53.8 us
    ppermute x10, waiting for transfers between devices, upward(): lax.ppermute(value, axis, [(i, i + 1) for i in range(lax.axis_size(axis)...  44.9 us
    ppermute x10, starting transfers between devices, upward(): lax.ppermute(value, axis, [(i, i + 1) for i in range(lax.axis_size(axis)...  41 us
    all_to_all x2, waiting for transfers between devices, fast_shards(): spread = lax.all_to_all(sums, 'slab', 0, 0, tiled=True)  20.2 us
    pallas_call x1, Pallas kernels, record_rows(): pl.pallas_call(record_kernel, grid=(views, colours, planes // step), in_s...  18.4 us
    ppermute x10, waiting for transfers between devices, downward(): lax.ppermute(value, axis, [(i + 1, i) for i in range(lax.axis_size(axis)...  17.8 us
    ppermute x10, starting transfers between devices, downward(): lax.ppermute(value, axis, [(i + 1, i) for i in range(lax.axis_size(axis)...  17 us
  transfers between devices with their start and end apart: 23, of which 9 were waited for; matrix products, arithmetic and copies ran while one was open for 4% of the time, Pallas kernels for 37%

profile of v1, /device:TPU:1, one launch (start us, length us, event | category | flops | bytes accessed | tf_op | source)
XLA Modules:
  0.0 399.6 jit_solution(8908550533896247707)
XLA Ops:
  0.0 5.8 %send_blocks.3 = f32[8,32,16,128]{3,2,1,0:T(8,128)} custom-call(f32[2,16,32,1024]{3,2,1,0:T(8,128)} %estimate.3), custom_call_target="tpu_custom_call" | custom-call | bytes 4194304 | tf_op jit(solution)/shard_map/send_blocks/pallas_call | solution.py:198
  5.8 53.8 %all_to_all.20.source.own = f32[8,32,16,128]{3,2,1,0:T(8,128)} all-to-all(f32[8,32,16,128]{3,2,1,0:T(8,128)} %send_blocks.3), channel_id=1, replica_groups=mesh['view'=4,'slab'=8] {'slab'}, dimensions={0} | all-to-all | bytes 4194304 | tf_op jit(solution)/shard_map/all_to_all | solution.py:443
  59.6 4.0 column_edges.3
  68.8 5.1 %collective-permute-start.10 = (f32[8,24,16,128]{3,2,1,0:T(8,128)}, f32[8,24,16,128]{3,2,1,0:T(8,128)}, u32[]{:S(2)}, u32[]{:S(2)}) collective-permute-start(f32[8,24,16,128]{3,2,1,0:T(8,128)} %get-tuple-element.90), channel_id=1, source_target_pairs={{0,8},{8,16},{16,24},{1,9},{9,17},{17,25},{2,10},{10,18},{18,26},{... | collective-permute-start | bytes 4718600 | tf_op jit(solution)/shard_map/ppermute | solution.py:118
  77.2 5.8 %send_blocks.2 = f32[8,32,16,128]{3,2,1,0:T(8,128)} custom-call(f32[2,16,32,1024]{3,2,1,0:T(8,128)} %estimate.3), custom_call_target="tpu_custom_call" | custom-call | bytes 4194304 | tf_op jit(solution)/shard_map/send_blocks/pallas_call | solution.py:198
  83.0 4.3 %all-to-all-start = ((f32[8,32,16,128]{3,2,1,0:T(8,128)}), f32[8,32,16,128]{3,2,1,0:T(8,128)S(1)}, u32[]{:S(2)}, u32[]{:S(2)}) async-start(f32[8,32,16,128]{3,2,1,0:T(8,128)} %send_blocks.2), calls=%async_computation | async-start | bytes 4194304 | tf_op jit(solution)/shard_map/all_to_all | solution.py:443
  88.0 4.5 %collective-permute-start.14 = (f32[24,48,128]{2,1,0:T(8,128)S(1)}, f32[24,48,128]{2,1,0:T(8,128)S(1)}, u32[]{:S(2)}, u32[]{:S(2)}) collective-permute-start(f32[24,48,128]{2,1,0:T(8,128)S(1)} %get-tuple-element.96), channel_id=1, source_target_pairs={{0,8},{8,16},{16,24},{1,9},{9,17},{17,25},{2,10},{10,18},{18,26},{... | collective-permute-start | bytes 1769480 | tf_op jit(solution)/shard_map/ppermute | solution.py:118
  95.2 18.4 %record_rows.1.rec = bf16[2,2,32,128,128]{4,3,2,1,0:T(8,128)(2,1)} custom-call(bf16[2,2,128,32,128]{4,3,2,1,0:T(8,128)(2,1)} %source.4), custom_call_target="tpu_custom_call" | custom-call | bytes 8388608 | tf_op jit(solution)/shard_map/record_rows/pallas_call | solution.py:217
  114.3 8.3 %tables.1 = (bf16[256,256]{1,0:T(8,128)(2,1)}, bf16[256,256]{1,0:T(8,128)(2,1)}, bf16[256,256]{1,0:T(8,128)(2,1)}, bf16[256,256]{1,0:T(8,128)(2,1)}, bf16[2,128,...) custom-call(f32[2,31]{1,0:T(2,128)} %bitcast.4, ...), custom_call_target="tpu_custom_call" | custom-call | flops 10000000 | bytes 1000000 | tf_op jit(solution)/shard_map/tables/pallas_call | solution.py:180
  123.6 48.1 %correlate.3 = (f32[24,176,128]{2,1,0:T(8,128)}, f32[32,176,128]{2,1,0:T(8,128)}, f32[24,176,128]{2,1,0:T(8,128)}) custom-call(f32[2,31]{1,0:T(2,128)} %bitcast.2, s32[2,2]{1,0:T(2,128)} %offs.5, f32[8,24,16,128]{3,2,1,0:T(8,128)} %collective-permute-done.10.left, f32[8,32,16,128]{3,2,1,0:T(8,128)} %all_to_all.20.source.own, ...), custom_call_target="tpu_custom_call" | custom-call | flops 20000000000 | bytes 30000000 | tf_op jit(solution)/shard_map/correlate/pallas_call | solution.py:365
  195.2 8.5 %collective-permute-done.2.edge_l = f32[32,24,128]{2,1,0:T(8,128)S(1)} collective-permute-done((f32[32,24,128]{2,1,0:T(8,128)}, f32[32,24,128]{2,1,0:T(8,128)S(1)}, u32[]{:S(2)}, u32[]{:S(2)}) %collective-permute-start.2) | collective-permute-done | bytes 393248 | tf_op jit(solution)/shard_map/ppermute | solution.py:118
  210.4 4.0 %collective-permute-start.18 = (f32[32,24,128]{2,1,0:T(8,128)S(1)}, f32[32,24,128]{2,1,0:T(8,128)S(1)}, u32[]{:S(2)}, u32[]{:S(2)}) collective-permute-start(f32[32,24,128]{2,1,0:T(8,128)S(1)} %get-tuple-element.94), channel_id=1, source_target_pairs={{0,1},{1,2},{2,3},{3,4},{4,5},{5,6},{6,7},{8,9},{9,10},{10,11},{11... | collective-permute-start | bytes 1179656 | tf_op jit(solution)/shard_map/ppermute | solution.py:118
  224.5 11.7 %collective-permute-done.19.edge_r = f32[32,24,128]{2,1,0:T(8,128)S(1)} collective-permute-done((f32[32,24,128]{2,1,0:T(8,128)S(1)}, f32[32,24,128]{2,1,0:T(8,128)S(1)}, u32[]{:S(2)}, u32[]{:S(2)}) %collective-permute-start.19) | collective-permute-done | bytes 393248 | tf_op jit(solution)/shard_map/ppermute | solution.py:122
  237.0 5.2 %gather_sums.3 = f32[8,32,16,128]{3,2,1,0:T(8,128)} custom-call(f32[32,176,128]{2,1,0:T(8,128)} %get-tuple-element.86.own, f32[24,176,128]{2,1,0:T(8,128)} %collective-permute-done.16.from_l, f32[24,176,128]{2,1,0:T(8,128)} %collective-permute-done.17.from_r, f32[32,24,128]{2,1,0:T(8,128)} %copy-done.5, f32[32,24,128]{2,1,0:T(8,128)} %copy-done.8), custom_call_target="tpu_custom_call" | custom-call | bytes 10000000 | tf_op jit(solution)/shard_map/gather_sums/pallas_call | solution.py:398
  242.2 4.5 %all-to-all-start.3 = ((f32[8,32,16,128]{3,2,1,0:T(8,128)}), f32[8,32,16,128]{3,2,1,0:T(8,128)S(1)}, u32[]{:S(2)}, u32[]{:S(2)}) async-start(f32[8,32,16,128]{3,2,1,0:T(8,128)} %gather_sums.3), calls=%async_computation.3 | async-start | bytes 4194304 | tf_op jit(solution)/shard_map/all_to_all | solution.py:466
  246.7 48.2 %correlate.2 = (f32[24,176,128]{2,1,0:T(8,128)}, f32[32,176,128]{2,1,0:T(8,128)}, f32[24,176,128]{2,1,0:T(8,128)}) custom-call(f32[2,31]{1,0:T(2,128)} %bitcast.3, s32[2,2]{1,0:T(2,128)} %offs.5, f32[8,24,16,128]{3,2,1,0:T(8,128)} %collective-permute-done.left, f32[8,32,16,128]{3,2,1,0:T(8,128)} %copy-done, f32[8,24,16,128]{3,2,1,0:T(8,128)} %collective-permute-done.1.right, ...), custom_call_target="tpu_custom_call" | custom-call | flops 20000000000 | bytes 30000000 | tf_op jit(solution)/shard_map/correlate/pallas_call | solution.py:365
  294.9 5.6 %collective-permute-start.6 = (f32[24,176,128]{2,1,0:T(8,128)}, f32[24,176,128]{2,1,0:T(8,128)S(1)}, u32[]{:S(2)}, u32[]{:S(2)}) collective-permute-start(f32[24,176,128]{2,1,0:T(8,128)} %get-tuple-element.82), channel_id=1, source_target_pairs={{0,8},{8,16},{16,24},{1,9},{9,17},{17,25},{2,10},{10,18},{18,26},{... | collective-permute-start | bytes 6488072 | tf_op jit(solution)/shard_map/ppermute | solution.py:118
  303.6 20.9 %collective-permute-done.6.from_l = f32[24,176,128]{2,1,0:T(8,128)S(1)} collective-permute-done((f32[24,176,128]{2,1,0:T(8,128)}, f32[24,176,128]{2,1,0:T(8,128)S(1)}, u32[]{:S(2)}, u32[]{:S(2)}) %collective-permute-start.6) | collective-permute-done | bytes 2162720 | tf_op jit(solution)/shard_map/ppermute | solution.py:118
  335.0 12.5 %collective-permute-done.8.edge_l = f32[32,24,128]{2,1,0:T(8,128)S(1)} collective-permute-done((f32[32,24,128]{2,1,0:T(8,128)S(1)}, f32[32,24,128]{2,1,0:T(8,128)S(1)}, u32[]{:S(2)}, u32[]{:S(2)}) %collective-permute-start.8) | collective-permute-done | bytes 393248 | tf_op jit(solution)/shard_map/ppermute | solution.py:118
  351.3 5.2 %gather_sums.2 = f32[8,32,16,128]{3,2,1,0:T(8,128)} custom-call(f32[32,176,128]{2,1,0:T(8,128)} %get-tuple-element.81.own, f32[24,176,128]{2,1,0:T(8,128)} %copy-done.3, f32[24,176,128]{2,1,0:T(8,128)} %copy-done.4, f32[32,24,128]{2,1,0:T(8,128)} %copy-done.6, f32[32,24,128]{2,1,0:T(8,128)} %copy-done.7), custom_call_target="tpu_custom_call" | custom-call | bytes 10000000 | tf_op jit(solution)/shard_map/gather_sums/pallas_call | solution.py:398
  357.8 9.2 %all-to-all-start.1 = ((f32[8,32,16,128]{3,2,1,0:T(8,128)}), f32[8,32,16,128]{3,2,1,0:T(8,128)}, u32[]{:S(2)}, u32[]{:S(2)}) async-start(f32[8,32,16,128]{3,2,1,0:T(8,128)} %gather_sums.2), calls=%async_computation.1 | async-start | bytes 4194304 | tf_op jit(solution)/shard_map/all_to_all | solution.py:466
  367.0 6.2 %update.2.rest_0_ = f32[2,16,32,1024]{3,2,1,0:T(8,128)} custom-call(f32[8,32,16,128]{3,2,1,0:T(8,128)} %copy-done.2, f32[2,16,32,1024]{3,2,1,0:T(8,128)} %estimate.3), custom_call_target="tpu_custom_call" | custom-call | bytes 6291456 | tf_op jit(solution)/shard_map/update/pallas_call | solution.py:415
  373.2 20.2 %all-to-all-done.1.spread = f32[8,32,16,128]{3,2,1,0:T(8,128)} async-done(((f32[8,32,16,128]{3,2,1,0:T(8,128)}), f32[8,32,16,128]{3,2,1,0:T(8,128)}, u32[]{:S(2)}, u32[]{:S(2)}) %all-to-all-start.1) | async-done | bytes 2097184 | tf_op jit(solution)/shard_map/all_to_all | solution.py:466
  393.4 6.2 %update.3 = f32[2,16,32,1024]{3,2,1,0:T(8,128)} custom-call(f32[8,32,16,128]{3,2,1,0:T(8,128)} %all-to-all-done.1.spread, f32[2,16,32,1024]{3,2,1,0:T(8,128)} %estimate.3, f32[2,16,32,1024]{3,2,1,0:T(8,128)} %update.2.rest_0_), custom_call_target="tpu_custom_call", output_to_operand_aliasing={{}: (2, {})} | custom-call | bytes 6291456 | tf_op jit(solution)/shard_map/update/pallas_call | solution.py:415
  (92 shorter events, 73.0 us)
Async XLA Ops:
  63.6 24.0 %collective-permute-start.12 = (f32[32,24,128]{2,1,0:T(8,128)}, f32[32,24,128]{2,1,0:T(8,128)S(1)}, u32[]{:S(2)}, u32[]{:S(2)}) collective-permute-start(f32[32,24,128]{2,1,0:T(8,128)} %get-tuple-element.84), channel_id=1, source_target_pairs={{0,1},{1,2},{2,3},{3,4},{4,5},{5,6},{6,7},{8,9},{9,10},{10,11},{11... | collective-permute-start | bytes 1179656 | tf_op jit(solution)/shard_map/ppermute | solution.py:118
  68.8 53.7 %collective-permute-start.10 = (f32[8,24,16,128]{3,2,1,0:T(8,128)}, f32[8,24,16,128]{3,2,1,0:T(8,128)}, u32[]{:S(2)}, u32[]{:S(2)}) collective-permute-start(f32[8,24,16,128]{3,2,1,0:T(8,128)} %get-tuple-element.90), channel_id=1, source_target_pairs={{0,8},{8,16},{16,24},{1,9},{9,17},{17,25},{2,10},{10,18},{18,26},{... | collective-permute-start | bytes 4718600 | tf_op jit(solution)/shard_map/ppermute | solution.py:118
  74.0 48.6 %collective-permute-start.11 = (f32[8,24,16,128]{3,2,1,0:T(8,128)}, f32[8,24,16,128]{3,2,1,0:T(8,128)}, u32[]{:S(2)}, u32[]{:S(2)}) collective-permute-start(f32[8,24,16,128]{3,2,1,0:T(8,128)} %get-tuple-element.89), channel_id=1, source_target_pairs={{8,0},{16,8},{24,16},{9,1},{17,9},{25,17},{10,2},{18,10},{26,18},{... | collective-permute-start | bytes 4718600 | tf_op jit(solution)/shard_map/ppermute | solution.py:122
  75.9 12.0 %collective-permute-start.13 = (f32[32,24,128]{2,1,0:T(8,128)S(1)}, f32[32,24,128]{2,1,0:T(8,128)S(1)}, u32[]{:S(2)}, u32[]{:S(2)}) collective-permute-start(f32[32,24,128]{2,1,0:T(8,128)S(1)} %copy-done.17), channel_id=1, source_target_pairs={{1,0},{2,1},{3,2},{4,3},{5,4},{6,5},{7,6},{9,8},{10,9},{11,10},{12... | collective-permute-start | bytes 1179656 | tf_op jit(solution)/shard_map/ppermute | solution.py:122
  83.0 94.4 %all-to-all-start = ((f32[8,32,16,128]{3,2,1,0:T(8,128)}), f32[8,32,16,128]{3,2,1,0:T(8,128)S(1)}, u32[]{:S(2)}, u32[]{:S(2)}) async-start(f32[8,32,16,128]{3,2,1,0:T(8,128)} %send_blocks.2), calls=%async_computation | async-start | bytes 4194304 | tf_op jit(solution)/shard_map/all_to_all | solution.py:443
  87.5 26.1 %copy-start.11 = (f32[32,24,128]{2,1,0:T(8,128)}, f32[32,24,128]{2,1,0:T(8,128)S(1)}, u32[]{:S(2)}) copy-start(f32[32,24,128]{2,1,0:T(8,128)S(1)} %collective-permute-done.12.edge_l) | copy-start | bytes 1179652
  88.0 34.5 %collective-permute-start.14 = (f32[24,48,128]{2,1,0:T(8,128)S(1)}, f32[24,48,128]{2,1,0:T(8,128)S(1)}, u32[]{:S(2)}, u32[]{:S(2)}) collective-permute-start(f32[24,48,128]{2,1,0:T(8,128)S(1)} %get-tuple-element.96), channel_id=1, source_target_pairs={{0,8},{8,16},{16,24},{1,9},{9,17},{17,25},{2,10},{10,18},{18,26},{... | collective-permute-start | bytes 1769480 | tf_op jit(solution)/shard_map/ppermute | solution.py:118
  92.6 30.0 %collective-permute-start.15 = (f32[24,48,128]{2,1,0:T(8,128)S(1)}, f32[24,48,128]{2,1,0:T(8,128)S(1)}, u32[]{:S(2)}, u32[]{:S(2)}) collective-permute-start(f32[24,48,128]{2,1,0:T(8,128)S(1)} %get-tuple-element.95), channel_id=1, source_target_pairs={{8,0},{16,8},{24,16},{9,1},{17,9},{25,17},{10,2},{18,10},{26,18},{... | collective-permute-start | bytes 1769480 | tf_op jit(solution)/shard_map/ppermute | solution.py:122
  171.7 36.1 %collective-permute-start.16 = (f32[24,176,128]{2,1,0:T(8,128)}, f32[24,176,128]{2,1,0:T(8,128)}, u32[]{:S(2)}, u32[]{:S(2)}) collective-permute-start(f32[24,176,128]{2,1,0:T(8,128)} %get-tuple-element.87), channel_id=1, source_target_pairs={{0,8},{8,16},{16,24},{1,9},{9,17},{17,25},{2,10},{10,18},{18,26},{... | collective-permute-start | bytes 6488072 | tf_op jit(solution)/shard_map/ppermute | solution.py:118
  175.3 33.8 %collective-permute-start.17 = (f32[24,176,128]{2,1,0:T(8,128)}, f32[24,176,128]{2,1,0:T(8,128)}, u32[]{:S(2)}, u32[]{:S(2)}) collective-permute-start(f32[24,176,128]{2,1,0:T(8,128)} %get-tuple-element.88), channel_id=1, source_target_pairs={{8,0},{16,8},{24,16},{9,1},{17,9},{25,17},{10,2},{18,10},{26,18},{... | collective-permute-start | bytes 6488072 | tf_op jit(solution)/shard_map/ppermute | solution.py:122
  182.5 21.1 %collective-permute-start.2 = (f32[32,24,128]{2,1,0:T(8,128)}, f32[32,24,128]{2,1,0:T(8,128)S(1)}, u32[]{:S(2)}, u32[]{:S(2)}) collective-permute-start(f32[32,24,128]{2,1,0:T(8,128)} %get-tuple-element.71), channel_id=1, source_target_pairs={{0,1},{1,2},{2,3},{3,4},{4,5},{5,6},{6,7},{8,9},{9,10},{10,11},{11... | collective-permute-start | bytes 1179656 | tf_op jit(solution)/shard_map/ppermute | solution.py:118
  186.2 19.7 %collective-permute-start.3 = (f32[32,24,128]{2,1,0:T(8,128)}, f32[32,24,128]{2,1,0:T(8,128)S(1)}, u32[]{:S(2)}, u32[]{:S(2)}) collective-permute-start(f32[32,24,128]{2,1,0:T(8,128)} %get-tuple-element.72), channel_id=1, source_target_pairs={{1,0},{2,1},{3,2},{4,3},{5,4},{6,5},{7,6},{9,8},{10,9},{11,10},{12... | collective-permute-start | bytes 1179656 | tf_op jit(solution)/shard_map/ppermute | solution.py:122
  191.3 55.4 %collective-permute-start = (f32[8,24,16,128]{3,2,1,0:T(8,128)}, f32[8,24,16,128]{3,2,1,0:T(8,128)}, u32[]{:S(2)}, u32[]{:S(2)}) collective-permute-start(f32[8,24,16,128]{3,2,1,0:T(8,128)} %get-tuple-element.92), channel_id=1, source_target_pairs={{0,8},{8,16},{16,24},{1,9},{9,17},{17,25},{2,10},{10,18},{18,26},{... | collective-permute-start | bytes 4718600 | tf_op jit(solution)/shard_map/ppermute | solution.py:118
  203.7 43.1 %collective-permute-start.1 = (f32[8,24,16,128]{3,2,1,0:T(8,128)}, f32[8,24,16,128]{3,2,1,0:T(8,128)}, u32[]{:S(2)}, u32[]{:S(2)}) collective-permute-start(f32[8,24,16,128]{3,2,1,0:T(8,128)} %get-tuple-element.91), channel_id=1, source_target_pairs={{8,0},{16,8},{24,16},{9,1},{17,9},{25,17},{10,2},{18,10},{26,18},{... | collective-permute-start | bytes 4718600 | tf_op jit(solution)/shard_map/ppermute | solution.py:122
  210.4 12.8 %collective-permute-start.18 = (f32[32,24,128]{2,1,0:T(8,128)S(1)}, f32[32,24,128]{2,1,0:T(8,128)S(1)}, u32[]{:S(2)}, u32[]{:S(2)}) collective-permute-start(f32[32,24,128]{2,1,0:T(8,128)S(1)} %get-tuple-element.94), channel_id=1, source_target_pairs={{0,1},{1,2},{2,3},{3,4},{4,5},{5,6},{6,7},{8,9},{9,10},{10,11},{11... | collective-permute-start | bytes 1179656 | tf_op jit(solution)/shard_map/ppermute | solution.py:118
  214.5 32.2 %collective-permute-start.4 = (f32[24,48,128]{2,1,0:T(8,128)S(1)}, f32[24,48,128]{2,1,0:T(8,128)}, u32[]{:S(2)}, u32[]{:S(2)}) collective-permute-start(f32[24,48,128]{2,1,0:T(8,128)S(1)} %get-tuple-element.100), channel_id=1, source_target_pairs={{0,8},{8,16},{16,24},{1,9},{9,17},{17,25},{2,10},{10,18},{18,26},{... | collective-permute-start | bytes 1769480 | tf_op jit(solution)/shard_map/ppermute | solution.py:118
  218.3 28.4 %collective-permute-start.5 = (f32[24,48,128]{2,1,0:T(8,128)S(1)}, f32[24,48,128]{2,1,0:T(8,128)}, u32[]{:S(2)}, u32[]{:S(2)}) collective-permute-start(f32[24,48,128]{2,1,0:T(8,128)S(1)} %get-tuple-element.99), channel_id=1, source_target_pairs={{8,0},{16,8},{24,16},{9,1},{17,9},{25,17},{10,2},{18,10},{26,18},{... | collective-permute-start | bytes 1769480 | tf_op jit(solution)/shard_map/ppermute | solution.py:122
  223.2 13.0 %collective-permute-start.19 = (f32[32,24,128]{2,1,0:T(8,128)S(1)}, f32[32,24,128]{2,1,0:T(8,128)S(1)}, u32[]{:S(2)}, u32[]{:S(2)}) collective-permute-start(f32[32,24,128]{2,1,0:T(8,128)S(1)} %get-tuple-element.93), channel_id=1, source_target_pairs={{1,0},{2,1},{3,2},{4,3},{5,4},{6,5},{7,6},{9,8},{10,9},{11,10},{12... | collective-permute-start | bytes 1179656 | tf_op jit(solution)/shard_map/ppermute | solution.py:122
  242.2 114.3 %all-to-all-start.3 = ((f32[8,32,16,128]{3,2,1,0:T(8,128)}), f32[8,32,16,128]{3,2,1,0:T(8,128)S(1)}, u32[]{:S(2)}, u32[]{:S(2)}) async-start(f32[8,32,16,128]{3,2,1,0:T(8,128)} %gather_sums.3), calls=%async_computation.3 | async-start | bytes 4194304 | tf_op jit(solution)/shard_map/all_to_all | solution.py:466
  294.9 29.6 %collective-permute-start.6 = (f32[24,176,128]{2,1,0:T(8,128)}, f32[24,176,128]{2,1,0:T(8,128)S(1)}, u32[]{:S(2)}, u32[]{:S(2)}) collective-permute-start(f32[24,176,128]{2,1,0:T(8,128)} %get-tuple-element.82), channel_id=1, source_target_pairs={{0,8},{8,16},{16,24},{1,9},{9,17},{17,25},{2,10},{10,18},{18,26},{... | collective-permute-start | bytes 6488072 | tf_op jit(solution)/shard_map/ppermute | solution.py:118
  300.5 28.3 %collective-permute-start.7 = (f32[24,176,128]{2,1,0:T(8,128)}, f32[24,176,128]{2,1,0:T(8,128)S(1)}, u32[]{:S(2)}, u32[]{:S(2)}) collective-permute-start(f32[24,176,128]{2,1,0:T(8,128)} %get-tuple-element.83), channel_id=1, source_target_pairs={{8,0},{16,8},{24,16},{9,1},{17,9},{25,17},{10,2},{18,10},{26,18},{... | collective-permute-start | bytes 6488072 | tf_op jit(solution)/shard_map/ppermute | solution.py:122
  330.1 17.4 %collective-permute-start.8 = (f32[32,24,128]{2,1,0:T(8,128)S(1)}, f32[32,24,128]{2,1,0:T(8,128)S(1)}, u32[]{:S(2)}, u32[]{:S(2)}) collective-permute-start(f32[32,24,128]{2,1,0:T(8,128)S(1)} %get-tuple-element.98), channel_id=1, source_target_pairs={{0,1},{1,2},{2,3},{3,4},{4,5},{5,6},{6,7},{8,9},{9,10},{10,11},{11... | collective-permute-start | bytes 1179656 | tf_op jit(solution)/shard_map/ppermute | solution.py:118
  333.7 16.8 %collective-permute-start.9 = (f32[32,24,128]{2,1,0:T(8,128)S(1)}, f32[32,24,128]{2,1,0:T(8,128)S(1)}, u32[]{:S(2)}, u32[]{:S(2)}) collective-permute-start(f32[32,24,128]{2,1,0:T(8,128)S(1)} %get-tuple-element.97), channel_id=1, source_target_pairs={{1,0},{2,1},{3,2},{4,3},{5,4},{6,5},{7,6},{9,8},{10,9},{11,10},{12... | collective-permute-start | bytes 1179656 | tf_op jit(solution)/shard_map/ppermute | solution.py:122
  357.8 35.6 %all-to-all-start.1 = ((f32[8,32,16,128]{3,2,1,0:T(8,128)}), f32[8,32,16,128]{3,2,1,0:T(8,128)}, u32[]{:S(2)}, u32[]{:S(2)}) async-start(f32[8,32,16,128]{3,2,1,0:T(8,128)} %gather_sums.2), calls=%async_computation.1 | async-start | bytes 4194304 | tf_op jit(solution)/shard_map/all_to_all | solution.py:466
  (17 other events, 88.1 us)

commit v2 on v1

v2 whole, which is shorter than its diff:
```python
import functools

import jax
import jax.numpy as jnp
from jax import lax
from jax.experimental import pallas as pl
from jax.experimental.pallas import tpu as pltpu
from jax.sharding import PartitionSpec as P

HALO = 23
BACKGROUND = 0.05
HIGHEST = lax.Precision.HIGHEST
LANES = 128
REACH = 15
EDGE = 24
F32 = jnp.float32
BF16 = jnp.bfloat16
VMEM_LIMIT = 58 * 1024 * 1024


def with_halo(value, sides, width):
    for axis, dim in sides:
        peers, length = (lax.axis_size(axis), value.shape[dim])
        up = [(i, (i + 1) % peers) for i in range(peers - 1)]
        down = [(j, i) for i, j in up]
        last = lax.slice_in_dim(value, length - width, length, axis=dim)
        leading = lax.slice_in_dim(value, 0, width, axis=dim)
        before = lax.ppermute(last, axis, up)
        after = lax.ppermute(leading, axis, down)
        value = jnp.concatenate([before, value, after], axis=dim)
    return value


def unit_taps(weights):
    return weights / jnp.sum(weights)


def band_table(weights, places):
    levels = jnp.arange(weights.shape[0], dtype=jnp.int32)
    return jnp.sum(jnp.where(places[..., None] == levels, weights, 0.0), axis=-1)


def margin_matrix(weights, offset, length, margin, adjoint):
    centre = (weights.shape[0] - 1) // 2
    outputs = jnp.arange(length, dtype=jnp.int32)[:, None]
    sources = jnp.arange(length + 2 * margin, dtype=jnp.int32)[None, :] - margin
    apart = sources - outputs
    if adjoint:
        apart = -apart
    return band_table(weights, apart - offset + centre)


def blocked_rows(field, weights, offset, width_blk, adjoint):
    extent = field.shape
    blocks = extent[3] // width_blk
    pieces = field.reshape(extent[0], extent[1], extent[2], blocks, width_blk)
    padded = jnp.pad(pieces, ((0, 0), (0, 0), (0, 0), (1, 1), (0, 0)))
    centre = (weights.shape[0] - 1) // 2
    sources = jnp.arange(width_blk, dtype=jnp.int32)[:, None]
    outputs = jnp.arange(width_blk, dtype=jnp.int32)[None, :]
    result = jnp.zeros(pieces.shape, F32)
    for shifted in range(3):
        apart = (shifted - 1) * width_blk + sources - outputs
        if adjoint:
            apart = -apart
        matrix = band_table(weights, apart - offset + centre)
        result = result + jnp.einsum(
            "czxkj,ji->czxki",
            padded[:, :, :, shifted : shifted + blocks],
            matrix,
            precision=HIGHEST,
        )
    return result.reshape(extent)


def general_shards(estimate, recorded, psf_lateral, psf_axial, offsets):
    views_n, planes_n = recorded.shape[0], recorded.shape[2]
    along_x = [unit_taps(psf_lateral[which, 0]) for which in range(views_n)]
    along_y = [unit_taps(psf_lateral[which, 1]) for which in range(views_n)]
    rows_at = jnp.arange(planes_n, dtype=jnp.int32)[:, None]
    cols_at = jnp.arange(planes_n, dtype=jnp.int32)[None, :]
    axial_places = cols_at - rows_at + (psf_axial.shape[1] - 1) // 2
    axial = [band_table(unit_taps(psf_axial[which]), axial_places) for which in range(views_n)]
    x_rows = estimate.shape[2]
    widened = with_halo(estimate, (("view", 2),), HALO)
    blurred = []
    for which in range(views_n):
        across = margin_matrix(along_x[which], offsets[which, 0], x_rows, HALO, False)
        sectioned = jnp.einsum("ab,czby->czay", across, widened, precision=HIGHEST)
        blurred.append(blocked_rows(sectioned, along_y[which], offsets[which, 1], LANES, False))
    columns = lax.all_to_all(jnp.stack(blurred), "slab", split_axis=4, concat_axis=2, tiled=True)
    spread = []
    for which in range(views_n):
        imaged = jnp.einsum("oi,cixy->coxy", axial[which], columns[which], precision=HIGHEST)
        quotient = recorded[which].astype(F32) / (imaged + BACKGROUND)
        spread.append(jnp.einsum("oi,coxy->cixy", axial[which], quotient, precision=HIGHEST))
    planes = lax.all_to_all(jnp.stack(spread), "slab", split_axis=2, concat_axis=4, tiled=True)
    returned = [
        blocked_rows(planes[which], along_y[which], offsets[which, 1], LANES, True)
        for which in range(views_n)
    ]
    fringe = with_halo(jnp.stack(returned), (("view", 3),), HALO)
    summed = jnp.zeros(estimate.shape, F32)
    for which in range(views_n):
        across = margin_matrix(along_x[which], offsets[which, 0], x_rows, HALO, True)
        summed = summed + jnp.einsum("ab,czby->czay", across, fringe[which], precision=HIGHEST)
    return estimate * (summed / views_n)


def params():
    return pltpu.CompilerParams(vmem_limit_bytes=VMEM_LIMIT)


def cost(micros):
    return pl.CostEstimate(flops=0, bytes_accessed=int(micros * 3_600_000), transcendentals=0)


def upward(value, axis):
    return lax.ppermute(value, axis, [(i, i + 1) for i in range(lax.axis_size(axis) - 1)])


def downward(value, axis):
    return lax.ppermute(value, axis, [(i + 1, i) for i in range(lax.axis_size(axis) - 1)])


def split(value):
    high = value.astype(BF16)
    return high, (value - high.astype(F32)).astype(BF16)


def mm(a, b):
    return jnp.dot(a, b, preferred_element_type=F32)


def parts(value, axis):
    high, low = split(value)
    return jnp.concatenate([high, low, high], axis=axis)


def tables_kernel(taps_xy, z_taps, offs, y_fore, y_back, z_fore, z_back, x_fore, x_back, half):
    views, _, taps = taps_xy.shape
    axial = z_taps.shape[1]
    size = LANES
    rows = lax.broadcasted_iota(jnp.int32, (size, size), 0)
    cols = lax.broadcasted_iota(jnp.int32, (size, size), 1)
    halo_row = jnp.where(rows < EDGE, rows - EDGE, rows - EDGE + size)

    def chosen(place, count, tap):
        def step(k, acc):
            return jnp.where(place == k, tap(k), acc)

        return lax.fori_loop(0, count, step, jnp.zeros(place.shape, F32))

    def store(target, value, where):
        high, low = split(value)
        for p, piece in enumerate((high, high, low)):
            target[where(p)] = piece

    def at(r0, c0, height, width):
        return slice(r0, r0 + height), slice(c0, c0 + width)

    for v in range(views):
        shift = offs[v, 1] - (taps - 1) // 2
        for n in range(2):
            place = (rows if n == 0 else halo_row) - cols - shift
            if n == 1:
                place = jnp.where(rows < 2 * EDGE, place, -1)
            fore = chosen(place, taps, lambda k: taps_xy[v, 1, k])
            store(y_fore, fore, lambda p: at((2 * p + n) * size, v * size, size, size))
            store(y_back, fore.T, lambda p: at((views * p + v) * size, n * size, size, size))
        fore = chosen(cols - rows + (axial - 1) // 2, axial, lambda k: z_taps[v, k])
        store(z_fore, fore, lambda p: (v, *at(0, p * size, size, size)))
        store(z_back, fore.T, lambda p: (v, *at(0, p * size, size, size)))

        height, width = x_fore.shape[1], x_fore.shape[2] // 3
        step = 64
        for r0 in range(0, height, step):
            r = lax.broadcasted_iota(jnp.int32, (step, width), 0) + r0
            q = lax.broadcasted_iota(jnp.int32, (step, width), 1)
            place = jnp.where(r % 8 == q % 8, q // 8 - r // 8, -1)
            fore = chosen(place, taps, lambda k: taps_xy[v, 0, k])
            store(x_fore, fore, lambda p: (v, *at(r0, p * width, step, width)))
            half[r0 : r0 + step] = fore
        for r0 in range(0, height, size):
            back = half[r0 : r0 + size].T
            store(x_back, back, lambda p: (v, *at(0, p * height + r0, width, size)))


def make_tables(lateral, axial, offsets, rows):
    smem = pl.BlockSpec(memory_space=pltpu.SMEM)
    vmem = pl.BlockSpec(memory_space=pltpu.VMEM)
    views = lateral.shape[0]
    window = rows + 32
    shapes = [
        (6 * LANES, views * LANES),
        (3 * views * LANES, 2 * LANES),
        (views, LANES, 3 * LANES),
        (views, LANES, 3 * LANES),
        (views, 8 * rows, 3 * 8 * window),
        (views, 8 * window, 3 * 8 * rows),
    ]
    return pl.pallas_call(
        tables_kernel,
        out_shape=tuple(jax.ShapeDtypeStruct(shape, BF16) for shape in shapes),
        in_specs=[smem] * 3,
        out_specs=(vmem,) * len(shapes),
        compiler_params=params(),
        scratch_shapes=[pltpu.VMEM((8 * rows, 8 * window), F32)],
        cost_estimate=cost(14),
        name="tables",
    )(lateral, axial, offsets)


def swap_kernel(source, target):
    width = target.shape[3]
    for k in range(target.shape[0]):
        target[k] = jnp.swapaxes(source[0, :, :, k * width : (k + 1) * width], 0, 1)


def send_blocks(estimate, c, peers):
    _, planes, rows, columns = estimate.shape
    width = columns // peers
    step = min(4, peers)
    return pl.pallas_call(
        swap_kernel,
        grid=(peers // step,),
        in_specs=[pl.BlockSpec((1, planes, rows, step * width), lambda s: (c, 0, 0, s))],
        out_specs=pl.BlockSpec((step, rows, planes, width), lambda s: (s, 0, 0, 0)),
        out_shape=jax.ShapeDtypeStruct((peers, rows, planes, width), F32),
        compiler_params=params(),
        cost_estimate=cost(3),
        name="send_blocks",
    )(estimate)


def record_kernel(source, target):
    target[0, 0] = jnp.swapaxes(source[0, 0].astype(F32), 0, 1).astype(BF16)


def record_rows(recorded):
    views, colours, planes, rows, width = recorded.shape
    step = 64
    return pl.pallas_call(
        record_kernel,
        grid=(views, colours, planes // step),
        in_specs=[pl.BlockSpec((1, 1, step, rows, width), lambda v, c, z: (v, c, z, 0, 0))],
        out_specs=pl.BlockSpec((1, 1, rows, step, width), lambda v, c, z: (v, c, 0, z, 0)),
        out_shape=jax.ShapeDtypeStruct((views, colours, rows, planes, width), BF16),
        compiler_params=params(),
        cost_estimate=cost(8),
        name="record_rows",
    )(recorded)


def edges_kernel(source, first, last, leading, trailing, block, sems):
    peers, rows, planes, size = block.shape
    arrive = pltpu.make_async_copy(source, block, sems.at[0])
    arrive.start()
    arrive.wait()
    depart = [
        pltpu.make_async_copy(block.at[:, pl.ds(0, EDGE)], leading, sems.at[1]),
        pltpu.make_async_copy(block.at[:, pl.ds(rows - EDGE, EDGE)], trailing, sems.at[2]),
    ]
    for copy in depart:
        copy.start()
    for x in range(rows):
        turned = block[:, x].reshape(peers * planes, size).T
        first[x] = turned[:EDGE]
        last[x] = turned[-EDGE:]
    for copy in depart:
        copy.wait()


def block_edges(block):
    peers, rows, planes, width = block.shape
    hbm = pl.BlockSpec(memory_space=pl.ANY)
    vmem = pl.BlockSpec(memory_space=pltpu.VMEM)
    edge = jax.ShapeDtypeStruct((rows, EDGE, peers * planes), F32)
    side = jax.ShapeDtypeStruct((peers, EDGE, planes, width), F32)
    return pl.pallas_call(
        edges_kernel,
        in_specs=[hbm],
        out_specs=(vmem, vmem, hbm, hbm),
        out_shape=(edge, edge, side, side),
        scratch_shapes=[pltpu.VMEM(block.shape, F32), pltpu.SemaphoreType.DMA((3,))],
        compiler_params=params(),
        cost_estimate=cost(4),
        name="block_edges",
    )(block)


def correlate_kernel(c, count, offs, *rest):
    sources, rest = rest[:count], rest[count:]
    outs, held_in, rest = rest[:3], rest[3 : 3 + count], rest[3 + count :]
    out_l, out_m, out_r = outs
    ext, mid, v_out, arrive, depart = rest
    edge_l, edge_r, own, left, right, corner_l, corner_r = held_in[:7]
    y_fore, x_fore, rec, z_fore, z_back, x_back, y_back = held_in[7:]
    views = rec.shape[0]
    rows = own.shape[1]
    size = LANES
    window = x_back.shape[1] // 8
    group = 4
    wide = 4
    held = ext.shape[1]
    zeros_tail = jnp.zeros((size - 2 * EDGE, size), F32)
    incoming = []
    for n, (source, target) in enumerate(zip(sources, held_in)):
        source = source.at[:, c] if target is rec else source
        incoming.append(pltpu.make_async_copy(source, target, arrive.at[n]))
    order = (7, 0, 1, 2, 3, 4, 5, 6, 8, 9, 10, 11, 12, 13)
    for n in order:
        incoming[n].start()

    def need(*names):
        for n in names:
            incoming[n].wait()

    begin = [EDGE - REACH + offs[v, 0] for v in range(views)]

    def clear(first, last):
        for v in range(views):

            @pl.loop(first, last)
            def _(e):
                ext[v, e] = jnp.zeros((size, size), F32)

    clear(2 * EDGE + rows, held)

    def along_y(main, halo, x0, base):
        mains, halos = [], []
        for n in range(group):
            mains.append(main(x0 + n))
            halos.append(jnp.concatenate([*halo(x0 + n), zeros_tail], axis=0).T)
        whole = jnp.concatenate([jnp.concatenate(mains, 0), jnp.concatenate(halos, 0)], axis=1)
        done = mm(parts(whole, 1), y_fore[...])
        for v in range(views):
            ext[v, pl.ds(base + x0, group)] = done[:, v * size : (v + 1) * size].reshape(group, size, size)

    need(7, 0, 1, 2)

    @pl.loop(0, rows // group)
    def _(g):
        along_y(
            lambda x: own[:, x].reshape(size, size), lambda x: [edge_l[x], edge_r[x]], g * group, EDGE
        )

    need(3, 4, 5, 6)

    @pl.loop(0, EDGE // group)
    def _(g):
        along_y(lambda x: left[:, x].reshape(size, size), lambda x: [corner_l[x]], g * group, 0)
        along_y(
            lambda x: right[:, x].reshape(size, size), lambda x: [corner_r[x]], g * group, EDGE + rows
        )

    need(8)

    @pl.loop(0, size // (8 * wide))
    def _(n):
        z0 = pl.multiple_of(n * 8 * wide, 8 * wide)
        for v in range(views):
            data = jnp.concatenate(
                [
                    ext[v, pl.ds(begin[v], window), pl.ds(z0 + 8 * k, 8)].reshape(8 * window, size)
                    for k in range(wide)
                ],
                axis=1,
            )
            done = mm(x_fore[v], parts(data, 0))
            for k in range(wide):
                mid[v, :, pl.ds(z0 + 8 * k, 8)] = done[:, k * size : (k + 1) * size].reshape(rows, 8, size)

    need(9, 10, 11)

    @pl.loop(0, rows // group)
    def _(g):
        x0 = g * group
        for v in range(views):
            image = mm(z_fore[v], parts(jnp.concatenate([mid[v, x0 + n] for n in range(group)], axis=1), 0))
            seen = jnp.concatenate([rec[v, x0 + n].astype(F32) for n in range(group)], axis=1)
            back = mm(z_back[v], parts(seen / (image + BACKGROUND), 0))
            for n in range(group):
                mid[v, x0 + n] = back[:, n * size : (n + 1) * size]

    need(12)
    clear(0, EDGE)
    clear(EDGE + rows, 2 * EDGE + rows)

    @pl.loop(0, size // (8 * wide))
    def _(n):
        z0 = pl.multiple_of(n * 8 * wide, 8 * wide)
        for v in range(views):
            data = jnp.concatenate(
                [mid[v, :, pl.ds(z0 + 8 * k, 8)].reshape(8 * rows, size) for k in range(wide)], axis=1
            )
            done = mm(x_back[v], parts(data, 0))
            for k in range(wide):
                ext[v, pl.ds(begin[v], window), pl.ds(z0 + 8 * k, 8)] = done[
                    :, k * size : (k + 1) * size
                ].reshape(window, 8, size)

    need(13)
    leaving = []
    for n, (target, base, count) in enumerate(
        [(out_l, 0, EDGE), (out_r, EDGE + rows, EDGE), (out_m, EDGE, rows)]
    ):

        @pl.loop(0, count // group)
        def _(g):
            x0 = g * group
            both = [
                jnp.concatenate([ext[v, base + x0 + k] for v in range(views)], axis=1) for k in range(group)
            ]
            done = mm(parts(jnp.concatenate(both, axis=0), 1), y_back[...])
            for k in range(group):
                piece = done[k * size : (k + 1) * size]
                v_out[base + x0 + k, :size] = piece[:, :size]
                v_out[base + x0 + k, size:] = piece[:, size:].T[: 2 * EDGE]

        leaving.append(pltpu.make_async_copy(v_out.at[pl.ds(base, count)], target, depart.at[n]))
        leaving[-1].start()
    for copy in leaving:
        copy.wait()


def correlate(c, offsets, left, own, right, edge_l, edge_r, corner_l, corner_r, rec, tables):
    smem = pl.BlockSpec(memory_space=pltpu.SMEM)
    hbm = pl.BlockSpec(memory_space=pl.ANY)
    rows = own.shape[1]
    views = rec.shape[0]
    tall = LANES + 2 * EDGE
    side = jax.ShapeDtypeStruct((EDGE, tall, LANES), F32)
    y_fore, y_back, z_fore, z_back, x_fore, x_back = tables
    arrays = edge_l, edge_r, own, left, right, corner_l, corner_r
    arrays += y_fore, x_fore, rec, z_fore, z_back, x_back, y_back
    count = len(arrays)
    held = [
        pltpu.VMEM((views, rows, LANES, LANES), BF16) if a is rec else pltpu.VMEM(a.shape, a.dtype)
        for a in arrays
    ]
    return pl.pallas_call(
        functools.partial(correlate_kernel, c, count),
        out_shape=(side, jax.ShapeDtypeStruct((rows, tall, LANES), F32), side),
        in_specs=[smem] + [hbm] * count,
        out_specs=(hbm,) * 3,
        scratch_shapes=held
        + [
            pltpu.VMEM((views, 2 * EDGE + rows + 8, LANES, LANES), F32),
            pltpu.VMEM((views, rows, LANES, LANES), F32),
            pltpu.VMEM((2 * EDGE + rows, tall, LANES), F32),
            pltpu.SemaphoreType.DMA((count,)),
            pltpu.SemaphoreType.DMA((3,)),
        ],
        compiler_params=params(),
        cost_estimate=cost(32),
        name="correlate",
    )(offsets, *arrays)


def returning_kernel(own, from_l, from_r, first, last, mine, left, right, arrive):
    rows, size = own.shape[0], LANES
    pairs = ((own, mine), (from_l, left), (from_r, right))
    copies = [
        pltpu.make_async_copy(source.at[:, pl.ds(size, 2 * EDGE)], target, arrive.at[n])
        for n, (source, target) in enumerate(pairs)
    ]
    for copy in copies:
        copy.start()
    for copy in copies:
        copy.wait()
    for x in range(rows):
        total = mine[x]
        if x < EDGE:
            total = total + left[x]
        if x >= rows - EDGE:
            total = total + right[x - rows + EDGE]
        first[x] = total[:EDGE]
        last[x] = total[EDGE:]


def returning_columns(own, from_l, from_r):
    hbm = pl.BlockSpec(memory_space=pl.ANY)
    vmem = pl.BlockSpec(memory_space=pltpu.VMEM)
    rows = own.shape[0]
    edge = jax.ShapeDtypeStruct((rows, EDGE, LANES), F32)
    return pl.pallas_call(
        returning_kernel,
        in_specs=[hbm] * 3,
        out_specs=(vmem, vmem),
        out_shape=(edge, edge),
        scratch_shapes=[pltpu.VMEM((count, 2 * EDGE, LANES), F32) for count in (rows, EDGE, EDGE)]
        + [pltpu.SemaphoreType.DMA((3,))],
        compiler_params=params(),
        cost_estimate=cost(2),
        name="returning_columns",
    )(own, from_l, from_r)


def gather_kernel(own, from_l, from_r, edge_l, edge_r, target):
    rows, size = own.shape[0], LANES
    gap = jnp.zeros((size - 2 * EDGE, size), F32)
    for x in range(rows):
        total = own[x, :size]
        if x < EDGE:
            total = total + from_l[x, :size]
        if x >= rows - EDGE:
            total = total + from_r[x - rows + EDGE, :size]
        total = total + jnp.concatenate([edge_l[x], gap, edge_r[x]], axis=0).T
        target[:, x] = total.reshape(target.shape[0], target.shape[2], size)


def gather_sums(own, from_l, from_r, edge_l, edge_r, peers):
    rows = own.shape[0]
    planes = LANES // peers
    vmem = pl.BlockSpec(memory_space=pltpu.VMEM)
    return pl.pallas_call(
        gather_kernel,
        out_shape=jax.ShapeDtypeStruct((peers, rows, planes, LANES), F32),
        in_specs=[vmem] * 5,
        out_specs=vmem,
        compiler_params=params(),
        cost_estimate=cost(5),
        name="gather_sums",
    )(own, from_l, from_r, edge_l, edge_r)


def update(estimate, spread, c, views, held):
    _, planes, rows, columns = estimate.shape
    peers = spread.shape[0]
    width = columns // peers
    step = min(4, peers)
    block = pl.BlockSpec((1, planes, rows, step * width), lambda s: (c, 0, 0, s))
    extra = [] if held is None else [held]
    return pl.pallas_call(
        functools.partial(update_kernel, views),
        grid=(peers // step,),
        in_specs=[pl.BlockSpec((step, rows, planes, width), lambda s: (s, 0, 0, 0)), block]
        + [pl.BlockSpec(memory_space=pl.ANY)] * len(extra),
        out_specs=block,
        out_shape=jax.ShapeDtypeStruct(estimate.shape, F32),
        input_output_aliases={2: 0} if extra else {},
        compiler_params=params(),
        cost_estimate=cost(4),
        name="update",
    )(spread, estimate, *extra)


def update_kernel(views, spread, estimate, *rest):
    width = spread.shape[3]
    for k in range(spread.shape[0]):
        lanes = slice(k * width, (k + 1) * width)
        rest[-1][0, :, :, lanes] = estimate[0, :, :, lanes] * (jnp.swapaxes(spread[k], 0, 1) / views)


def fast_shards(estimate, recorded, psf_lateral, psf_axial, offsets):
    views, colours = recorded.shape[:2]
    rows = estimate.shape[2]
    peers = lax.axis_size("slab")
    lateral = psf_lateral / jnp.sum(psf_lateral, axis=-1, keepdims=True)
    axial = psf_axial / jnp.sum(psf_axial, axis=-1, keepdims=True)
    tables = make_tables(lateral, axial, offsets, rows)
    rec = record_rows(recorded)
    sent = [send_blocks(estimate, c, peers) for c in range(colours)]
    result = None
    pending = None

    def close(c, result, mine, from_l, from_r, back_l, back_r):
        sums = gather_sums(mine, from_l, from_r, back_l, back_r, peers)
        summed = lax.all_to_all(sums, "slab", 0, 0, tiled=True)
        return update(estimate, summed, c, views, result)

    for c in range(colours):
        own = lax.all_to_all(sent[c], "slab", 0, 0, tiled=True)
        if c == 0:
            own, sent, tables, rec = lax.optimization_barrier((own, sent, tables, rec))
        first, last, leading, trailing = block_edges(own)
        edge_l = upward(last, "slab")
        edge_r = downward(first, "slab")
        left = upward(trailing, "view")
        right = downward(leading, "view")
        if c + 1 < colours:
            edge_l, edge_r, left, right, sent = lax.optimization_barrier((edge_l, edge_r, left, right, sent))
        edges = jnp.concatenate([edge_l, edge_r], axis=1)
        end_l, end_r = edges[rows - EDGE :], edges[:EDGE]
        if pending is not None:
            end_l, end_r, pending = lax.optimization_barrier((end_l, end_r, pending))
            first, last = returning_columns(*pending)
            back_r, back_l = downward(first, "slab"), upward(last, "slab")
        corner_l = upward(end_l, "view")
        corner_r = downward(end_r, "view")
        if pending is not None:
            corner_l, corner_r, first, last = lax.optimization_barrier((corner_l, corner_r, first, last))
        to_l, mine, to_r = correlate(
            c, offsets, left, own, right, edge_l, edge_r, corner_l, corner_r, rec, tables
        )
        if pending is not None:
            mine, back_l, back_r = lax.optimization_barrier((mine, back_l, back_r))
            result = close(c - 1, result, *pending, back_l, back_r)
        pending = mine, upward(to_r, "view"), downward(to_l, "view")
    first, last = returning_columns(*pending)
    return close(colours - 1, result, *pending, upward(last, "slab"), downward(first, "slab"))


def shards(estimate, recorded, psf_lateral, psf_axial, offsets):
    planes, rows, width = recorded.shape[2:]
    fits = planes == LANES and width == LANES and rows % 8 == 0 and rows >= EDGE
    fits = fits and estimate.shape[1] % 16 == 0 and psf_lateral.shape[2] == 2 * REACH + 1
    run = fast_shards if fits else general_shards
    return run(estimate, recorded, psf_lateral, psf_axial, offsets)


def solution(mesh):
    in_specs = (P(None, "slab", "view", None), P(None, None, None, "view", "slab"), P(), P(), P())
    out_specs = P(None, "slab", "view", None)
    return jax.shard_map(shards, mesh=mesh, in_specs=in_specs, out_specs=out_specs, check_vma=False)
```

time: 405 us -> 358 us (0.88); the launches traced: 400 us -> 357 us
  waiting for transfers between devices: 82.9 us -> 140 us
  blocking collectives: 53.8 us -> 0 us
  Pallas kernels: 165 us -> 126 us
  local copies, waits for them, and re-layouts: 16.2 us -> 11.4 us
    all_to_all x1 -> x0, blocking collectives: 53.8 us -> none  [fast_shards(): lax.all_to_all(send_blocks(estimate, c, peers), 'slab', 0, 0, tiled=True)]
    all_to_all x3 -> x4, waiting for transfers between devices: 20.2 us -> 60.4 us  [the longest x2 37.6 us: close(): summed = lax.all_to_all(sums, 'slab', 0, 0, tiled=True)]
    pallas_call x9 -> x11, Pallas kernels: 136 us -> 108 us  [the longest x2 68.9 us: correlate(): pl.pallas_call(functools.partial(correlate_kernel, c, count), out_shape=(...]
    ppermute x10, waiting for transfers between devices: 44.9 us -> 59.2 us  [upward(): lax.ppermute(value, axis, [(i, i + 1) for i in range(lax.axis_size(axis)...]
    pallas_call x1, Pallas kernels: 18.4 us -> 7.44 us  [record_rows(): pl.pallas_call(record_kernel, grid=(views, colours, planes // step), in_s...]
    slice x9 -> x2, local copies, waits for them, and re-layouts: 9.14 us -> 1.01 us  [fast_shards(): end_l, end_r = (edges[rows - EDGE:], edges[:EDGE])]
    all_to_all x3 -> x4, starting transfers between devices: 18 us -> 23.7 us  [the longest x2 12 us: fast_shards(): own = lax.all_to_all(sent[c], 'slab', 0, 0, tiled=True)]
    scatter-add x4 -> x0, other arithmetic: 4.17 us -> none  [the longest x2 2.85 us: fast_shards(): margin = mine[:, LANES:].at[:EDGE].add(from_l[:, LANES:])]
  transfers between devices with their start and end apart: 23 -> 24, of which waited for: 9 -> 13; matrix products, arithmetic and copies ran while one was open for 4% -> 1% of each run, Pallas kernels for 37% -> 31%
where the time goes in v2:
time: 358 us; the launch traced here: 357 us
  waiting for transfers between devices  140 us (39%)
  Pallas kernels  126 us (35%)
  starting transfers between devices  78.5 us (22%)
  local copies, waits for them, and re-layouts  11.4 us (3%)
    pallas_call x2, Pallas kernels, correlate(): pl.pallas_call(functools.partial(correlate_kernel, c, count), out_shape=(...  68.9 us
    ppermute x10, waiting for transfers between devices, upward(): lax.ppermute(value, axis, [(i, i + 1) for i in range(lax.axis_size(axis)...  59.2 us
    all_to_all x2, waiting for transfers between devices, close(): summed = lax.all_to_all(sums, 'slab', 0, 0, tiled=True)  37.6 us
    ppermute x10, starting transfers between devices, upward(): lax.ppermute(value, axis, [(i, i + 1) for i in range(lax.axis_size(axis)...  36.8 us
    all_to_all x2, waiting for transfers between devices, fast_shards(): own = lax.all_to_all(sent[c], 'slab', 0, 0, tiled=True)  22.8 us
    ppermute x10, waiting for transfers between devices, downward(): lax.ppermute(value, axis, [(i + 1, i) for i in range(lax.axis_size(axis)...  20.1 us
    ppermute x10, starting transfers between devices, downward(): lax.ppermute(value, axis, [(i + 1, i) for i in range(lax.axis_size(axis)...  18 us
    pallas_call x1, Pallas kernels, make_tables(): pl.pallas_call(tables_kernel, out_shape=tuple((jax.ShapeDtypeStruct(shape...  13 us
  transfers between devices with their start and end apart: 24, of which 13 were waited for; matrix products, arithmetic and copies ran while one was open for 1% of the time, Pallas kernels for 31%

profile of v2, /device:TPU:1, one launch (start us, length us, event | category | flops | bytes accessed | tf_op | source)
XLA Modules:
  0.0 357.0 jit_solution(15233728932498993496)
XLA Ops:
  2.8 6.4 %all-to-all-start = ((f32[8,32,16,128]{3,2,1,0:T(8,128)}), f32[8,32,16,128]{3,2,1,0:T(8,128)S(1)}, u32[]{:S(2)}, u32[]{:S(2)}) async-start(f32[8,32,16,128]{3,2,1,0:T(8,128)} %send_blocks.2), calls=%async_computation | async-start | bytes 4194304 | tf_op jit(solution)/shard_map/all_to_all | solution.py:574
  11.8 7.4 %record_rows.1.rest_9_ = bf16[2,2,32,128,128]{4,3,2,1,0:T(8,128)(2,1)} custom-call(bf16[2,2,128,32,128]{4,3,2,1,0:T(8,128)(2,1)} %source.5), custom_call_target="tpu_custom_call" | custom-call | bytes 28800000 | tf_op jit(solution)/shard_map/record_rows/pallas_call | solution.py:243
  20.7 13.0 %tables.1 = (bf16[768,256]{1,0:T(8,128)(2,1)}, bf16[768,256]{1,0:T(8,128)(2,1)}, bf16[2,128,384]{2,1,0:T(8,128)(2,1)}, bf16[2,128,384]{2,1,0:T(8,128)(2,1)}, bf1...) custom-call(f32[2,2,31]{2,1,0:T(2,128)} %fusion.1.taps_xy, f32[2,127]{1,0:T(2,128)} %broadcast_divide_fusion.z_taps, ...), custom_call_target="tpu_custom_call" | custom-call | bytes 50400000 | tf_op jit(solution)/shard_map/tables/pallas_call | solution.py:202
  33.7 22.8 %all-to-all-done.source.rest_2_ = f32[8,32,16,128]{3,2,1,0:T(8,128)S(1)} async-done(((f32[8,32,16,128]{3,2,1,0:T(8,128)}), f32[8,32,16,128]{3,2,1,0:T(8,128)S(1)}, u32[]{:S(2)}, u32[]{:S(2)}) %all-to-all-start) | async-done | bytes 2097184 | tf_op jit(solution)/shard_map/all_to_all | solution.py:574
  57.8 4.2 %block_edges.2 = (f32[32,24,128]{2,1,0:T(8,128)}, f32[32,24,128]{2,1,0:T(8,128)}, f32[8,24,16,128]{3,2,1,0:T(8,128)}, f32[8,24,16,128]{3,2,1,0:T(8,128)}) custom-call(f32[8,32,16,128]{3,2,1,0:T(8,128)} %copy-done.1), custom_call_target="tpu_custom_call" | custom-call | bytes 14400000 | tf_op jit(solution)/shard_map/block_edges/pallas_call | solution.py:280
  62.0 4.9 %collective-permute-start.2 = (f32[8,24,16,128]{3,2,1,0:T(8,128)}, f32[8,24,16,128]{3,2,1,0:T(8,128)}, u32[]{:S(2)}, u32[]{:S(2)}) collective-permute-start(f32[8,24,16,128]{3,2,1,0:T(8,128)} %get-tuple-element.62), channel_id=1, source_target_pairs={{0,8},{8,16},{16,24},{1,9},{9,17},{17,25},{2,10},{10,18},{18,26},{... | collective-permute-start | bytes 4718600 | tf_op jit(solution)/shard_map/ppermute | solution.py:119
  73.2 15.6 %collective-permute-done.rest_0_ = f32[32,24,128]{2,1,0:T(8,128)S(1)} collective-permute-done((f32[32,24,128]{2,1,0:T(8,128)}, f32[32,24,128]{2,1,0:T(8,128)S(1)}, u32[]{:S(2)}, u32[]{:S(2)}) %collective-permute-start) | collective-permute-done | bytes 393248 | tf_op jit(solution)/shard_map/ppermute | solution.py:119
  88.9 5.6 %all-to-all-start.1 = ((f32[8,32,16,128]{3,2,1,0:T(8,128)}), f32[8,32,16,128]{3,2,1,0:T(8,128)S(1)}, u32[]{:S(2)}, u32[]{:S(2)}) async-start(f32[8,32,16,128]{3,2,1,0:T(8,128)} %send_blocks.3), calls=%async_computation.1 | async-start | bytes 4194304 | tf_op jit(solution)/shard_map/all_to_all | solution.py:574
  100.6 5.9 %collective-permute-done.9.rest_6_ = f32[24,48,128]{2,1,0:T(8,128)S(1)} collective-permute-done((f32[24,48,128]{2,1,0:T(8,128)S(1)}, f32[24,48,128]{2,1,0:T(8,128)S(1)}, u32[]{:S(2)}, u32[]{:S(2)}) %collective-permute-start.9) | collective-permute-done | bytes 589856 | tf_op jit(solution)/shard_map/ppermute | solution.py:123
  108.2 34.4 %correlate.2 = (f32[24,176,128]{2,1,0:T(8,128)}, f32[32,176,128]{2,1,0:T(8,128)}, f32[24,176,128]{2,1,0:T(8,128)}) custom-call(s32[2,2]{1,0:T(2,128)} %offs.5, f32[32,24,128]{2,1,0:T(8,128)} %copy-done.7, f32[32,24,128]{2,1,0:T(8,128)} %copy-done.8, f32[8,32,16,128]{3,2,1,0:T(8,128)} %copy-done.1, f32[8,24,16,128]{3,2,1,0:T(8,128)} %collective-permute-done.2.rest_3_, ...), custom_call_target="tpu_custom_call" | custom-call | bytes 115200000 | tf_op jit(solution)/shard_map/correlate/pallas_call | solution.py:442
  142.6 4.4 %collective-permute-start.10 = (f32[24,176,128]{2,1,0:T(8,128)}, f32[24,176,128]{2,1,0:T(8,128)}, u32[]{:S(2)}, u32[]{:S(2)}) collective-permute-start(f32[24,176,128]{2,1,0:T(8,128)} %get-tuple-element.82), channel_id=1, source_target_pairs={{0,8},{8,16},{16,24},{1,9},{9,17},{17,25},{2,10},{10,18},{18,26},{... | collective-permute-start | bytes 6488072 | tf_op jit(solution)/shard_map/ppermute | solution.py:119
  150.3 4.2 %block_edges.3 = (f32[32,24,128]{2,1,0:T(8,128)}, f32[32,24,128]{2,1,0:T(8,128)}, f32[8,24,16,128]{3,2,1,0:T(8,128)}, f32[8,24,16,128]{3,2,1,0:T(8,128)}) custom-call(f32[8,32,16,128]{3,2,1,0:T(8,128)} %copy-done), custom_call_target="tpu_custom_call" | custom-call | bytes 14400000 | tf_op jit(solution)/shard_map/block_edges/pallas_call | solution.py:280
  163.4 11.6 %collective-permute-done.4.rest_0_ = f32[32,24,128]{2,1,0:T(8,128)S(1)} collective-permute-done((f32[32,24,128]{2,1,0:T(8,128)}, f32[32,24,128]{2,1,0:T(8,128)S(1)}, u32[]{:S(2)}, u32[]{:S(2)}) %collective-permute-start.4) | collective-permute-done | bytes 393248 | tf_op jit(solution)/shard_map/ppermute | solution.py:119
  177.9 4.4 %collective-permute-start.12 = (f32[24,48,128]{2,1,0:T(8,128)}, f32[24,48,128]{2,1,0:T(8,128)S(1)}, u32[]{:S(2)}, u32[]{:S(2)}) collective-permute-start(f32[24,48,128]{2,1,0:T(8,128)} %get-tuple-element.84), channel_id=1, source_target_pairs={{0,8},{8,16},{16,24},{1,9},{9,17},{17,25},{2,10},{10,18},{18,26},{... | collective-permute-start | bytes 1769480 | tf_op jit(solution)/shard_map/ppermute | solution.py:119
  188.2 6.0 %collective-permute-done.12.rest_5_ = f32[24,48,128]{2,1,0:T(8,128)S(1)} collective-permute-done((f32[24,48,128]{2,1,0:T(8,128)}, f32[24,48,128]{2,1,0:T(8,128)S(1)}, u32[]{:S(2)}, u32[]{:S(2)}) %collective-permute-start.12) | collective-permute-done | bytes 589856 | tf_op jit(solution)/shard_map/ppermute | solution.py:119
  198.0 6.1 %collective-permute-done.13.rest_6_ = f32[24,48,128]{2,1,0:T(8,128)S(1)} collective-permute-done((f32[24,48,128]{2,1,0:T(8,128)S(1)}, f32[24,48,128]{2,1,0:T(8,128)S(1)}, u32[]{:S(2)}, u32[]{:S(2)}) %collective-permute-start.13) | collective-permute-done | bytes 589856 | tf_op jit(solution)/shard_map/ppermute | solution.py:123
  206.6 34.5 %correlate.3 = (f32[24,176,128]{2,1,0:T(8,128)}, f32[32,176,128]{2,1,0:T(8,128)}, f32[24,176,128]{2,1,0:T(8,128)}) custom-call(s32[2,2]{1,0:T(2,128)} %offs.5, f32[32,24,128]{2,1,0:T(8,128)} %copy-done.5, f32[32,24,128]{2,1,0:T(8,128)} %copy-done.6, f32[8,32,16,128]{3,2,1,0:T(8,128)} %copy-done, f32[8,24,16,128]{3,2,1,0:T(8,128)} %copy-done.9, ...), custom_call_target="tpu_custom_call" | custom-call | bytes 115200000 | tf_op jit(solution)/shard_map/correlate/pallas_call | solution.py:442
  242.0 5.1 %gather_sums.3 = f32[8,32,16,128]{3,2,1,0:T(8,128)} custom-call(f32[32,176,128]{2,1,0:T(8,128)} %get-tuple-element.86.own, f32[24,176,128]{2,1,0:T(8,128)} %collective-permute-done.10.from_l, f32[24,176,128]{2,1,0:T(8,128)} %collective-permute-done.11.from_r, f32[32,24,128]{2,1,0:T(8,128)} %copy-done.16, f32[32,24,128]{2,1,0:T(8,128)} %copy-done.15), custom_call_target="tpu_custom_call" | custom-call | bytes 18000000 | tf_op jit(solution)/shard_map/gather_sums/pallas_call | solution.py:517
  247.1 5.5 %all-to-all-start.3 = ((f32[8,32,16,128]{3,2,1,0:T(8,128)}), f32[8,32,16,128]{3,2,1,0:T(8,128)}, u32[]{:S(2)}, u32[]{:S(2)}) async-start(f32[8,32,16,128]{3,2,1,0:T(8,128)} %gather_sums.3), calls=%async_computation.3 | async-start | bytes 4194304 | tf_op jit(solution)/shard_map/all_to_all | solution.py:570
  257.1 21.4 %collective-permute-done.16.from_l = f32[24,176,128]{2,1,0:T(8,128)S(1)} collective-permute-done((f32[24,176,128]{2,1,0:T(8,128)}, f32[24,176,128]{2,1,0:T(8,128)S(1)}, u32[]{:S(2)}, u32[]{:S(2)}) %collective-permute-start.16) | collective-permute-done | bytes 2162720 | tf_op jit(solution)/shard_map/ppermute | solution.py:119
  278.5 4.3 %collective-permute-done.17.from_r = f32[24,176,128]{2,1,0:T(8,128)S(1)} collective-permute-done((f32[24,176,128]{2,1,0:T(8,128)}, f32[24,176,128]{2,1,0:T(8,128)S(1)}, u32[]{:S(2)}, u32[]{:S(2)}) %collective-permute-start.17) | collective-permute-done | bytes 2162720 | tf_op jit(solution)/shard_map/ppermute | solution.py:123
  299.7 5.2 %gather_sums.2 = f32[8,32,16,128]{3,2,1,0:T(8,128)} custom-call(f32[32,176,128]{2,1,0:T(8,128)} %get-tuple-element.94.own, f32[24,176,128]{2,1,0:T(8,128)} %copy-done.2, f32[24,176,128]{2,1,0:T(8,128)} %copy-done.3, f32[32,24,128]{2,1,0:T(8,128)} %copy-done.17, f32[32,24,128]{2,1,0:T(8,128)} %copy-done.18), custom_call_target="tpu_custom_call" | custom-call | bytes 18000000 | tf_op jit(solution)/shard_map/gather_sums/pallas_call | solution.py:517
  304.9 6.3 %all-to-all-start.2 = ((f32[8,32,16,128]{3,2,1,0:T(8,128)}), f32[8,32,16,128]{3,2,1,0:T(8,128)S(1)}, u32[]{:S(2)}, u32[]{:S(2)}) async-start(f32[8,32,16,128]{3,2,1,0:T(8,128)} %gather_sums.2), calls=%async_computation.2 | async-start | bytes 4194304 | tf_op jit(solution)/shard_map/all_to_all | solution.py:570
  314.6 37.6 %all-to-all-done.2.spread = f32[8,32,16,128]{3,2,1,0:T(8,128)S(1)} async-done(((f32[8,32,16,128]{3,2,1,0:T(8,128)}), f32[8,32,16,128]{3,2,1,0:T(8,128)S(1)}, u32[]{:S(2)}, u32[]{:S(2)}) %all-to-all-start.2) | async-done | bytes 2097184 | tf_op jit(solution)/shard_map/all_to_all | solution.py:570
  (89 shorter events, 79.8 us)
Async XLA Ops:
  2.8 53.7 %all-to-all-start = ((f32[8,32,16,128]{3,2,1,0:T(8,128)}), f32[8,32,16,128]{3,2,1,0:T(8,128)S(1)}, u32[]{:S(2)}, u32[]{:S(2)}) async-start(f32[8,32,16,128]{3,2,1,0:T(8,128)} %send_blocks.2), calls=%async_computation | async-start | bytes 4194304 | tf_op jit(solution)/shard_map/all_to_all | solution.py:574
  62.0 26.8 %collective-permute-start.2 = (f32[8,24,16,128]{3,2,1,0:T(8,128)}, f32[8,24,16,128]{3,2,1,0:T(8,128)}, u32[]{:S(2)}, u32[]{:S(2)}) collective-permute-start(f32[8,24,16,128]{3,2,1,0:T(8,128)} %get-tuple-element.62), channel_id=1, source_target_pairs={{0,8},{8,16},{16,24},{1,9},{9,17},{17,25},{2,10},{10,18},{18,26},{... | collective-permute-start | bytes 4718600 | tf_op jit(solution)/shard_map/ppermute | solution.py:119
  66.8 22.1 %collective-permute-start.3 = (f32[8,24,16,128]{3,2,1,0:T(8,128)}, f32[8,24,16,128]{3,2,1,0:T(8,128)}, u32[]{:S(2)}, u32[]{:S(2)}) collective-permute-start(f32[8,24,16,128]{3,2,1,0:T(8,128)} %get-tuple-element.63), channel_id=1, source_target_pairs={{8,0},{16,8},{24,16},{9,1},{17,9},{25,17},{10,2},{18,10},{26,18},{... | collective-permute-start | bytes 4718600 | tf_op jit(solution)/shard_map/ppermute | solution.py:123
  68.8 20.0 %collective-permute-start = (f32[32,24,128]{2,1,0:T(8,128)}, f32[32,24,128]{2,1,0:T(8,128)S(1)}, u32[]{:S(2)}, u32[]{:S(2)}) collective-permute-start(f32[32,24,128]{2,1,0:T(8,128)} %get-tuple-element.60), channel_id=1, source_target_pairs={{0,1},{1,2},{2,3},{3,4},{4,5},{5,6},{6,7},{8,9},{9,10},{10,11},{11... | collective-permute-start | bytes 1179656 | tf_op jit(solution)/shard_map/ppermute | solution.py:119
  71.9 16.9 %collective-permute-start.1 = (f32[32,24,128]{2,1,0:T(8,128)}, f32[32,24,128]{2,1,0:T(8,128)S(1)}, u32[]{:S(2)}, u32[]{:S(2)}) collective-permute-start(f32[32,24,128]{2,1,0:T(8,128)} %get-tuple-element.61), channel_id=1, source_target_pairs={{1,0},{2,1},{3,2},{4,3},{5,4},{6,5},{7,6},{9,8},{10,9},{11,10},{12... | collective-permute-start | bytes 1179656 | tf_op jit(solution)/shard_map/ppermute | solution.py:123
  88.9 60.1 %all-to-all-start.1 = ((f32[8,32,16,128]{3,2,1,0:T(8,128)}), f32[8,32,16,128]{3,2,1,0:T(8,128)S(1)}, u32[]{:S(2)}, u32[]{:S(2)}) async-start(f32[8,32,16,128]{3,2,1,0:T(8,128)} %send_blocks.3), calls=%async_computation.1 | async-start | bytes 4194304 | tf_op jit(solution)/shard_map/all_to_all | solution.py:574
  94.7 11.8 %collective-permute-start.9 = (f32[24,48,128]{2,1,0:T(8,128)S(1)}, f32[24,48,128]{2,1,0:T(8,128)S(1)}, u32[]{:S(2)}, u32[]{:S(2)}) collective-permute-start(f32[24,48,128]{2,1,0:T(8,128)S(1)} %get-tuple-element.101), channel_id=1, source_target_pairs={{8,0},{16,8},{24,16},{9,1},{17,9},{25,17},{10,2},{18,10},{26,18},{... | collective-permute-start | bytes 1769480 | tf_op jit(solution)/shard_map/ppermute | solution.py:123
  97.3 10.1 %collective-permute-start.8 = (f32[24,48,128]{2,1,0:T(8,128)S(1)}, f32[24,48,128]{2,1,0:T(8,128)S(1)}, u32[]{:S(2)}, u32[]{:S(2)}) collective-permute-start(f32[24,48,128]{2,1,0:T(8,128)S(1)} %get-tuple-element.102), channel_id=1, source_target_pairs={{0,8},{8,16},{16,24},{1,9},{9,17},{17,25},{2,10},{10,18},{18,26},{... | collective-permute-start | bytes 1769480 | tf_op jit(solution)/shard_map/ppermute | solution.py:119
  142.6 35.3 %collective-permute-start.10 = (f32[24,176,128]{2,1,0:T(8,128)}, f32[24,176,128]{2,1,0:T(8,128)}, u32[]{:S(2)}, u32[]{:S(2)}) collective-permute-start(f32[24,176,128]{2,1,0:T(8,128)} %get-tuple-element.82), channel_id=1, source_target_pairs={{0,8},{8,16},{16,24},{1,9},{9,17},{17,25},{2,10},{10,18},{18,26},{... | collective-permute-start | bytes 6488072 | tf_op jit(solution)/shard_map/ppermute | solution.py:119
  147.0 30.9 %collective-permute-start.11 = (f32[24,176,128]{2,1,0:T(8,128)}, f32[24,176,128]{2,1,0:T(8,128)}, u32[]{:S(2)}, u32[]{:S(2)}) collective-permute-start(f32[24,176,128]{2,1,0:T(8,128)} %get-tuple-element.83), channel_id=1, source_target_pairs={{8,0},{16,8},{24,16},{9,1},{17,9},{25,17},{10,2},{18,10},{26,18},{... | collective-permute-start | bytes 6488072 | tf_op jit(solution)/shard_map/ppermute | solution.py:123
  154.5 20.5 %collective-permute-start.4 = (f32[32,24,128]{2,1,0:T(8,128)}, f32[32,24,128]{2,1,0:T(8,128)S(1)}, u32[]{:S(2)}, u32[]{:S(2)}) collective-permute-start(f32[32,24,128]{2,1,0:T(8,128)} %get-tuple-element.66), channel_id=1, source_target_pairs={{0,1},{1,2},{2,3},{3,4},{4,5},{5,6},{6,7},{8,9},{9,10},{10,11},{11... | collective-permute-start | bytes 1179656 | tf_op jit(solution)/shard_map/ppermute | solution.py:119
  158.1 18.8 %collective-permute-start.5 = (f32[32,24,128]{2,1,0:T(8,128)}, f32[32,24,128]{2,1,0:T(8,128)S(1)}, u32[]{:S(2)}, u32[]{:S(2)}) collective-permute-start(f32[32,24,128]{2,1,0:T(8,128)} %get-tuple-element.67), channel_id=1, source_target_pairs={{1,0},{2,1},{3,2},{4,3},{5,4},{6,5},{7,6},{9,8},{10,9},{11,10},{12... | collective-permute-start | bytes 1179656 | tf_op jit(solution)/shard_map/ppermute | solution.py:123
  159.4 44.7 %collective-permute-start.6 = (f32[8,24,16,128]{3,2,1,0:T(8,128)}, f32[8,24,16,128]{3,2,1,0:T(8,128)S(1)}, u32[]{:S(2)}, u32[]{:S(2)}) collective-permute-start(f32[8,24,16,128]{3,2,1,0:T(8,128)} %get-tuple-element.68), channel_id=1, source_target_pairs={{0,8},{8,16},{16,24},{1,9},{9,17},{17,25},{2,10},{10,18},{18,26},{... | collective-permute-start | bytes 4718600 | tf_op jit(solution)/shard_map/ppermute | solution.py:119
  175.0 29.1 %collective-permute-start.7 = (f32[8,24,16,128]{3,2,1,0:T(8,128)}, f32[8,24,16,128]{3,2,1,0:T(8,128)S(1)}, u32[]{:S(2)}, u32[]{:S(2)}) collective-permute-start(f32[8,24,16,128]{3,2,1,0:T(8,128)} %get-tuple-element.69), channel_id=1, source_target_pairs={{8,0},{16,8},{24,16},{9,1},{17,9},{25,17},{10,2},{18,10},{26,18},{... | collective-permute-start | bytes 4718600 | tf_op jit(solution)/shard_map/ppermute | solution.py:123
  177.9 16.2 %collective-permute-start.12 = (f32[24,48,128]{2,1,0:T(8,128)}, f32[24,48,128]{2,1,0:T(8,128)S(1)}, u32[]{:S(2)}, u32[]{:S(2)}) collective-permute-start(f32[24,48,128]{2,1,0:T(8,128)} %get-tuple-element.84), channel_id=1, source_target_pairs={{0,8},{8,16},{16,24},{1,9},{9,17},{17,25},{2,10},{10,18},{18,26},{... | collective-permute-start | bytes 1769480 | tf_op jit(solution)/shard_map/ppermute | solution.py:119
  182.4 21.7 %collective-permute-start.13 = (f32[24,48,128]{2,1,0:T(8,128)S(1)}, f32[24,48,128]{2,1,0:T(8,128)S(1)}, u32[]{:S(2)}, u32[]{:S(2)}) collective-permute-start(f32[24,48,128]{2,1,0:T(8,128)S(1)} %get-tuple-element.85), channel_id=1, source_target_pairs={{8,0},{16,8},{24,16},{9,1},{17,9},{25,17},{10,2},{18,10},{26,18},{... | collective-permute-start | bytes 1769480 | tf_op jit(solution)/shard_map/ppermute | solution.py:123
  186.9 54.2 %collective-permute-start.15 = (f32[32,24,128]{2,1,0:T(8,128)}, f32[32,24,128]{2,1,0:T(8,128)S(1)}, u32[]{:S(2)}, u32[]{:S(2)}) collective-permute-start(f32[32,24,128]{2,1,0:T(8,128)} %get-tuple-element.89), channel_id=1, source_target_pairs={{1,0},{2,1},{3,2},{4,3},{5,4},{6,5},{7,6},{9,8},{10,9},{11,10},{12... | collective-permute-start | bytes 1179656 | tf_op jit(solution)/shard_map/ppermute | solution.py:123
  194.2 47.0 %collective-permute-start.14 = (f32[32,24,128]{2,1,0:T(8,128)}, f32[32,24,128]{2,1,0:T(8,128)S(1)}, u32[]{:S(2)}, u32[]{:S(2)}) collective-permute-start(f32[32,24,128]{2,1,0:T(8,128)} %get-tuple-element.90), channel_id=1, source_target_pairs={{0,1},{1,2},{2,3},{3,4},{4,5},{5,6},{6,7},{8,9},{9,10},{10,11},{11... | collective-permute-start | bytes 1179656 | tf_op jit(solution)/shard_map/ppermute | solution.py:119
  247.1 57.8 %all-to-all-start.3 = ((f32[8,32,16,128]{3,2,1,0:T(8,128)}), f32[8,32,16,128]{3,2,1,0:T(8,128)}, u32[]{:S(2)}, u32[]{:S(2)}) async-start(f32[8,32,16,128]{3,2,1,0:T(8,128)} %gather_sums.3), calls=%async_computation.3 | async-start | bytes 4194304 | tf_op jit(solution)/shard_map/all_to_all | solution.py:570
  252.6 25.9 %collective-permute-start.16 = (f32[24,176,128]{2,1,0:T(8,128)}, f32[24,176,128]{2,1,0:T(8,128)S(1)}, u32[]{:S(2)}, u32[]{:S(2)}) collective-permute-start(f32[24,176,128]{2,1,0:T(8,128)} %get-tuple-element.95), channel_id=1, source_target_pairs={{0,8},{8,16},{16,24},{1,9},{9,17},{17,25},{2,10},{10,18},{18,26},{... | collective-permute-start | bytes 6488072 | tf_op jit(solution)/shard_map/ppermute | solution.py:119
  254.6 28.3 %collective-permute-start.17 = (f32[24,176,128]{2,1,0:T(8,128)}, f32[24,176,128]{2,1,0:T(8,128)S(1)}, u32[]{:S(2)}, u32[]{:S(2)}) collective-permute-start(f32[24,176,128]{2,1,0:T(8,128)} %get-tuple-element.96), channel_id=1, source_target_pairs={{8,0},{16,8},{24,16},{9,1},{17,9},{25,17},{10,2},{18,10},{26,18},{... | collective-permute-start | bytes 6488072 | tf_op jit(solution)/shard_map/ppermute | solution.py:123
  286.7 8.5 %collective-permute-start.18 = (f32[32,24,128]{2,1,0:T(8,128)}, f32[32,24,128]{2,1,0:T(8,128)S(1)}, u32[]{:S(2)}, u32[]{:S(2)}) collective-permute-start(f32[32,24,128]{2,1,0:T(8,128)} %get-tuple-element.97), channel_id=1, source_target_pairs={{0,1},{1,2},{2,3},{3,4},{4,5},{5,6},{6,7},{8,9},{9,10},{10,11},{11... | collective-permute-start | bytes 1179656 | tf_op jit(solution)/shard_map/ppermute | solution.py:119
  290.2 8.7 %collective-permute-start.19 = (f32[32,24,128]{2,1,0:T(8,128)}, f32[32,24,128]{2,1,0:T(8,128)S(1)}, u32[]{:S(2)}, u32[]{:S(2)}) collective-permute-start(f32[32,24,128]{2,1,0:T(8,128)} %get-tuple-element.98), channel_id=1, source_target_pairs={{1,0},{2,1},{3,2},{4,3},{5,4},{6,5},{7,6},{9,8},{10,9},{11,10},{12... | collective-permute-start | bytes 1179656 | tf_op jit(solution)/shard_map/ppermute | solution.py:123
  304.9 47.3 %all-to-all-start.2 = ((f32[8,32,16,128]{3,2,1,0:T(8,128)}), f32[8,32,16,128]{3,2,1,0:T(8,128)S(1)}, u32[]{:S(2)}, u32[]{:S(2)}) async-start(f32[8,32,16,128]{3,2,1,0:T(8,128)} %gather_sums.2), calls=%async_computation.2 | async-start | bytes 4194304 | tf_op jit(solution)/shard_map/all_to_all | solution.py:570
  (21 other events, 79.6 us)

commit v3 on v2

--- a/solution.py
+++ b/solution.py
@@ -15,7 +15,6 @@
 EDGE = 24
 F32 = jnp.float32
 BF16 = jnp.bfloat16
-VMEM_LIMIT = 58 * 1024 * 1024
 
 
 def with_halo(value, sides, width):
@@ -107,8 +106,8 @@
     return estimate * (summed / views_n)
 
 
-def params():
-    return pltpu.CompilerParams(vmem_limit_bytes=VMEM_LIMIT)
+def params(mebibytes=20):
+    return pltpu.CompilerParams(vmem_limit_bytes=mebibytes * 1024 * 1024)
 
 
 def cost(micros):
@@ -121,6 +120,10 @@
 
 def downward(value, axis):
     return lax.ppermute(value, axis, [(i + 1, i) for i in range(lax.axis_size(axis) - 1)])
+
+
+def after(value, *earlier):
+    return lax.optimization_barrier((value, earlier))[0]
 
 
 def split(value):
@@ -252,14 +255,11 @@
     )(recorded)
 
 
-def edges_kernel(source, first, last, leading, trailing, block, sems):
+def edges_kernel(block, first, last, leading, trailing, sems):
     peers, rows, planes, size = block.shape
-    arrive = pltpu.make_async_copy(source, block, sems.at[0])
-    arrive.start()
-    arrive.wait()
     depart = [
-        pltpu.make_async_copy(block.at[:, pl.ds(0, EDGE)], leading, sems.at[1]),
-        pltpu.make_async_copy(block.at[:, pl.ds(rows - EDGE, EDGE)], trailing, sems.at[2]),
+        pltpu.make_async_copy(block.at[:, pl.ds(0, EDGE)], leading, sems.at[0]),
+        pltpu.make_async_copy(block.at[:, pl.ds(rows - EDGE, EDGE)], trailing, sems.at[1]),
     ]
     for copy in depart:
         copy.start()
@@ -273,34 +273,32 @@
 
 def block_edges(block):
     peers, rows, planes, width = block.shape
-    hbm = pl.BlockSpec(memory_space=pl.ANY)
+    hbm = pl.BlockSpec(memory_space=pltpu.HBM)
     vmem = pl.BlockSpec(memory_space=pltpu.VMEM)
     edge = jax.ShapeDtypeStruct((rows, EDGE, peers * planes), F32)
     side = jax.ShapeDtypeStruct((peers, EDGE, planes, width), F32)
     return pl.pallas_call(
         edges_kernel,
-        in_specs=[hbm],
+        in_specs=[vmem],
         out_specs=(vmem, vmem, hbm, hbm),
         out_shape=(edge, edge, side, side),
-        scratch_shapes=[pltpu.VMEM(block.shape, F32), pltpu.SemaphoreType.DMA((3,))],
+        scratch_shapes=[pltpu.SemaphoreType.DMA((2,))],
         compiler_params=params(),
         cost_estimate=cost(4),
         name="block_edges",
     )(block)
 
 
-def correlate_kernel(c, count, offs, *rest):
+def correlate_kernel(c, count, offs, edge_l, edge_r, own, left, right, corner_l, corner_r, *rest):
     sources, rest = rest[:count], rest[count:]
-    outs, held_in, rest = rest[:3], rest[3 : 3 + count], rest[3 + count :]
-    out_l, out_m, out_r = outs
+    (out_l, out_m, out_r), held_in, rest = rest[:3], rest[3 : 3 + count], rest[3 + count :]
     ext, mid, v_out, arrive, depart = rest
-    edge_l, edge_r, own, left, right, corner_l, corner_r = held_in[:7]
-    y_fore, x_fore, rec, z_fore, z_back, x_back, y_back = held_in[7:]
+    y_fore, x_fore, rec, z_fore, z_back, x_back, y_back = held_in
     views = rec.shape[0]
     rows = own.shape[1]
     size = LANES
     window = x_back.shape[1] // 8
-    group = 4
+    group = 8
     wide = 4
     held = ext.shape[1]
     zeros_tail = jnp.zeros((size - 2 * EDGE, size), F32)
@@ -308,9 +306,7 @@
     for n, (source, target) in enumerate(zip(sources, held_in)):
         source = source.at[:, c] if target is rec else source
         incoming.append(pltpu.make_async_copy(source, target, arrive.at[n]))
-    order = (7, 0, 1, 2, 3, 4, 5, 6, 8, 9, 10, 11, 12, 13)
-    for n in order:
-        incoming[n].start()
+        incoming[-1].start()
 
     def need(*names):
         for n in names:
@@ -337,26 +333,24 @@
         for v in range(views):
             ext[v, pl.ds(base + x0, group)] = done[:, v * size : (v + 1) * size].reshape(group, size, size)
 
-    need(7, 0, 1, 2)
-
-    @pl.loop(0, rows // group)
+    need(0)
+
+    @pl.loop(0, rows // group, unroll=2)
     def _(g):
         along_y(
             lambda x: own[:, x].reshape(size, size), lambda x: [edge_l[x], edge_r[x]], g * group, EDGE
         )
 
-    need(3, 4, 5, 6)
-
-    @pl.loop(0, EDGE // group)
+    @pl.loop(0, EDGE // group, unroll=3)
     def _(g):
         along_y(lambda x: left[:, x].reshape(size, size), lambda x: [corner_l[x]], g * group, 0)
         along_y(
             lambda x: right[:, x].reshape(size, size), lambda x: [corner_r[x]], g * group, EDGE + rows
         )
 
-    need(8)
-
-    @pl.loop(0, size // (8 * wide))
+    need(1)
+
+    @pl.loop(0, size // (8 * wide), unroll=2)
     def _(n):
         z0 = pl.multiple_of(n * 8 * wide, 8 * wide)
         for v in range(views):
@@ -371,9 +365,9 @@
             for k in range(wide):
                 mid[v, :, pl.ds(z0 + 8 * k, 8)] = done[:, k * size : (k + 1) * size].reshape(rows, 8, size)
 
-    need(9, 10, 11)
-
-    @pl.loop(0, rows // group)
+    need(2, 3, 4)
+
+    @pl.loop(0, rows // group, unroll=2)
     def _(g):
         x0 = g * group
         for v in range(views):
@@ -383,11 +377,11 @@
             for n in range(group):
                 mid[v, x0 + n] = back[:, n * size : (n + 1) * size]
 
-    need(12)
+    need(5)
     clear(0, EDGE)
     clear(EDGE + rows, 2 * EDGE + rows)
 
-    @pl.loop(0, size // (8 * wide))
+    @pl.loop(0, size // (8 * wide), unroll=2)
     def _(n):
         z0 = pl.multiple_of(n * 8 * wide, 8 * wide)
         for v in range(views):
@@ -400,13 +394,13 @@
                     :, k * size : (k + 1) * size
                 ].reshape(window, 8, size)
 
-    need(13)
+    need(6)
     leaving = []
     for n, (target, base, count) in enumerate(
-        [(out_l, 0, EDGE), (out_r, EDGE + rows, EDGE), (out_m, EDGE, rows)]
+        [(v_out.at[0], 0, EDGE), (v_out.at[1], EDGE + rows, EDGE), (out_m, EDGE, rows)]
     ):
 
-        @pl.loop(0, count // group)
+        @pl.loop(0, count // group, unroll=3 if count == EDGE else 2)
         def _(g):
             x0 = g * group
             both = [
@@ -415,25 +409,26 @@
             done = mm(parts(jnp.concatenate(both, axis=0), 1), y_back[...])
             for k in range(group):
                 piece = done[k * size : (k + 1) * size]
-                v_out[base + x0 + k, :size] = piece[:, :size]
-                v_out[base + x0 + k, size:] = piece[:, size:].T[: 2 * EDGE]
-
-        leaving.append(pltpu.make_async_copy(v_out.at[pl.ds(base, count)], target, depart.at[n]))
-        leaving[-1].start()
+                target[x0 + k, :size] = piece[:, :size]
+                target[x0 + k, size:] = piece[:, size:].T[: 2 * EDGE]
+
+        if target is not out_m:
+            leaving.append(pltpu.make_async_copy(target, (out_l, out_r)[n], depart.at[n]))
+            leaving[-1].start()
     for copy in leaving:
         copy.wait()
 
 
 def correlate(c, offsets, left, own, right, edge_l, edge_r, corner_l, corner_r, rec, tables):
     smem = pl.BlockSpec(memory_space=pltpu.SMEM)
-    hbm = pl.BlockSpec(memory_space=pl.ANY)
+    vmem = pl.BlockSpec(memory_space=pltpu.VMEM)
+    hbm = pl.BlockSpec(memory_space=pltpu.HBM)
     rows = own.shape[1]
     views = rec.shape[0]
     tall = LANES + 2 * EDGE
     side = jax.ShapeDtypeStruct((EDGE, tall, LANES), F32)
     y_fore, y_back, z_fore, z_back, x_fore, x_back = tables
-    arrays = edge_l, edge_r, own, left, right, corner_l, corner_r
-    arrays += y_fore, x_fore, rec, z_fore, z_back, x_back, y_back
+    arrays = y_fore, x_fore, rec, z_fore, z_back, x_back, y_back
     count = len(arrays)
     held = [
         pltpu.VMEM((views, rows, LANES, LANES), BF16) if a is rec else pltpu.VMEM(a.shape, a.dtype)
@@ -442,55 +437,42 @@
     return pl.pallas_call(
         functools.partial(correlate_kernel, c, count),
         out_shape=(side, jax.ShapeDtypeStruct((rows, tall, LANES), F32), side),
-        in_specs=[smem] + [hbm] * count,
-        out_specs=(hbm,) * 3,
+        in_specs=[smem] + [vmem] * 7 + [hbm] * count,
+        out_specs=(hbm, vmem, hbm),
         scratch_shapes=held
         + [
             pltpu.VMEM((views, 2 * EDGE + rows + 8, LANES, LANES), F32),
             pltpu.VMEM((views, rows, LANES, LANES), F32),
-            pltpu.VMEM((2 * EDGE + rows, tall, LANES), F32),
+            pltpu.VMEM((2, EDGE, tall, LANES), F32),
             pltpu.SemaphoreType.DMA((count,)),
-            pltpu.SemaphoreType.DMA((3,)),
+            pltpu.SemaphoreType.DMA((2,)),
         ],
-        compiler_params=params(),
-        cost_estimate=cost(32),
+        compiler_params=params(46),
+        cost_estimate=cost(25),
         name="correlate",
-    )(offsets, *arrays)
-
-
-def returning_kernel(own, from_l, from_r, first, last, mine, left, right, arrive):
+    )(offsets, edge_l, edge_r, own, left, right, corner_l, corner_r, *arrays)
+
+
+def returning_kernel(own, from_l, from_r, first, last):
     rows, size = own.shape[0], LANES
-    pairs = ((own, mine), (from_l, left), (from_r, right))
-    copies = [
-        pltpu.make_async_copy(source.at[:, pl.ds(size, 2 * EDGE)], target, arrive.at[n])
-        for n, (source, target) in enumerate(pairs)
-    ]
-    for copy in copies:
-        copy.start()
-    for copy in copies:
-        copy.wait()
     for x in range(rows):
-        total = mine[x]
+        total = own[x, size:]
         if x < EDGE:
-            total = total + left[x]
+            total = total + from_l[x, size:]
         if x >= rows - EDGE:
-            total = total + right[x - rows + EDGE]
+            total = total + from_r[x - rows + EDGE, size:]
         first[x] = total[:EDGE]
         last[x] = total[EDGE:]
 
 
 def returning_columns(own, from_l, from_r):
-    hbm = pl.BlockSpec(memory_space=pl.ANY)
     vmem = pl.BlockSpec(memory_space=pltpu.VMEM)
-    rows = own.shape[0]
-    edge = jax.ShapeDtypeStruct((rows, EDGE, LANES), F32)
+    edge = jax.ShapeDtypeStruct((own.shape[0], EDGE, LANES), F32)
     return pl.pallas_call(
         returning_kernel,
-        in_specs=[hbm] * 3,
+        in_specs=[vmem] * 3,
         out_specs=(vmem, vmem),
         out_shape=(edge, edge),
-        scratch_shapes=[pltpu.VMEM((count, 2 * EDGE, LANES), F32) for count in (rows, EDGE, EDGE)]
-        + [pltpu.SemaphoreType.DMA((3,))],
         compiler_params=params(),
         cost_estimate=cost(2),
         name="returning_columns",
@@ -536,7 +518,7 @@
         functools.partial(update_kernel, views),
         grid=(peers // step,),
         in_specs=[pl.BlockSpec((step, rows, planes, width), lambda s: (s, 0, 0, 0)), block]
-        + [pl.BlockSpec(memory_space=pl.ANY)] * len(extra),
+        + [pl.BlockSpec(memory_space=pltpu.HBM)] * len(extra),
         out_specs=block,
         out_shape=jax.ShapeDtypeStruct(estimate.shape, F32),
         input_output_aliases={2: 0} if extra else {},
@@ -580,7 +562,7 @@
         left = upward(trailing, "view")
         right = downward(leading, "view")
         if c + 1 < colours:
-            edge_l, edge_r, left, right, sent = lax.optimization_barrier((edge_l, edge_r, left, right, sent))
+            sent = after(sent, edge_l, edge_r, left, right)
         edges = jnp.concatenate([edge_l, edge_r], axis=1)
         end_l, end_r = edges[rows - EDGE :], edges[:EDGE]
         if pending is not None:
@@ -604,7 +586,7 @@
 
 def shards(estimate, recorded, psf_lateral, psf_axial, offsets):
     planes, rows, width = recorded.shape[2:]
-    fits = planes == LANES and width == LANES and rows % 8 == 0 and rows >= EDGE
+    fits = planes == LANES and width == LANES and rows % 16 == 0 and rows >= EDGE
     fits = fits and estimate.shape[1] % 16 == 0 and psf_lateral.shape[2] == 2 * REACH + 1
     run = fast_shards if fits else general_shards
     return run(estimate, recorded, psf_lateral, psf_axial, offsets)

time: 358 us -> 327 us (0.913)
  Pallas kernels: 126 us -> 77 us
  local copies, waits for them, and re-layouts: 11.4 us -> 25 us
  starting transfers between devices: 78.5 us -> 83.2 us
    pallas_call x2, Pallas kernels: 68.9 us -> 50.1 us  [correlate(): pl.pallas_call(functools.partial(correlate_kernel, c, count), out_shape=(...]
    unnamed x44 -> x64, local copies, waits for them, and re-layouts: 10.3 us -> 24.8 us
    pallas_call x4, Pallas kernels: 13.5 us -> 4.13 us  [the longest x2 2.46 us: returning_columns(): pl.pallas_call(returning_kernel, in_specs=[vmem] * 3, out_specs=(vmem, vm...]
    pallas_call x2, Pallas kernels: 10.4 us -> 3.47 us  [gather_sums(): pl.pallas_call(gather_kernel, out_shape=jax.ShapeDtypeStruct((peers, rows...]
    ppermute x10, waiting for transfers between devices: 20.1 us -> 14.6 us  [downward(): lax.ppermute(value, axis, [(i + 1, i) for i in range(lax.axis_size(axis)...]
    pallas_call x1, Pallas kernels: 7.44 us -> 2.5 us  [record_rows(): pl.pallas_call(record_kernel, grid=(views, colours, planes // step), in_s...]
    pallas_call x2, Pallas kernels: 5.48 us -> 1.13 us  [send_blocks(): pl.pallas_call(swap_kernel, grid=(peers // step,), in_specs=[pl.BlockSpec...]
  transfers between devices with their start and end apart: 24 -> 24, of which waited for: 13 -> 14; matrix products, arithmetic and copies ran while one was open for 1% -> 0% of each run, Pallas kernels for 31% -> 22%
where the time goes in v3:
time: 327 us; the launch traced here: 326 us
  waiting for transfers between devices  140 us (43%)
  starting transfers between devices  83.2 us (25%)
  Pallas kernels  77 us (24%)
  local copies, waits for them, and re-layouts  25 us (8%)
    ppermute x10, waiting for transfers between devices, upward(): lax.ppermute(value, axis, [(i, i + 1) for i in range(lax.axis_size(axis)...  62.1 us
    pallas_call x2, Pallas kernels, correlate(): pl.pallas_call(functools.partial(correlate_kernel, c, count), out_shape=(...  50.1 us
    all_to_all x2, waiting for transfers between devices, close(): summed = lax.all_to_all(sums, 'slab', 0, 0, tiled=True)  38.9 us
    ppermute x10, starting transfers between devices, upward(): lax.ppermute(value, axis, [(i, i + 1) for i in range(lax.axis_size(axis)...  37.5 us
    unnamed x64, local copies, waits for them, and re-layouts  24.8 us
    all_to_all x2, waiting for transfers between devices, fast_shards(): own = lax.all_to_all(sent[c], 'slab', 0, 0, tiled=True)  24.3 us
    ppermute x10, starting transfers between devices, downward(): lax.ppermute(value, axis, [(i + 1, i) for i in range(lax.axis_size(axis)...  20 us
    ppermute x10, waiting for transfers between devices, downward(): lax.ppermute(value, axis, [(i + 1, i) for i in range(lax.axis_size(axis)...  14.6 us
  transfers between devices with their start and end apart: 24, of which 14 were waited for; matrix products, arithmetic and copies ran while one was open for 0% of the time, Pallas kernels for 22%

profile of v3, /device:TPU:1, one launch (start us, length us, event | category | flops | bytes accessed | tf_op | source)
XLA Modules:
  0.0 325.9 jit_solution(4464149359002386412)
XLA Ops:
  4.1 6.4 %all-to-all-start = ((f32[8,32,16,128]{3,2,1,0:T(8,128)}), f32[8,32,16,128]{3,2,1,0:T(8,128)S(1)}, u32[]{:S(2)}, u32[]{:S(2)}) async-start(f32[8,32,16,128]{3,2,1,0:T(8,128)} %copy-done.11), calls=%async_computation | async-start | bytes 4194304 | tf_op jit(solution)/shard_map/all_to_all | solution.py:556
  20.4 11.1 %tables.1 = (bf16[768,256]{1,0:T(8,128)(2,1)S(1)}, bf16[768,256]{1,0:T(8,128)(2,1)S(1)}, bf16[2,128,384]{2,1,0:T(8,128)(2,1)S(1)}, bf16[2,128,384]{2,1,0:T(8,128...) custom-call(f32[2,2,31]{2,1,0:T(2,128)S(1)} %fusion.1.taps_xy, ...), custom_call_target="tpu_custom_call" | custom-call | bytes 50400000 | tf_op jit(solution)/shard_map/tables/pallas_call | solution.py:205
  35.3 22.6 %all-to-all-done.block.own = f32[8,32,16,128]{3,2,1,0:T(8,128)S(1)} async-done(((f32[8,32,16,128]{3,2,1,0:T(8,128)}), f32[8,32,16,128]{3,2,1,0:T(8,128)S(1)}, u32[]{:S(2)}, u32[]{:S(2)}) %all-to-all-start) | async-done | bytes 2097184 | tf_op jit(solution)/shard_map/all_to_all | solution.py:556
  58.7 4.9 %collective-permute-start.2 = (f32[8,24,16,128]{3,2,1,0:T(8,128)S(1)}, f32[8,24,16,128]{3,2,1,0:T(8,128)S(1)}, u32[]{:S(2)}, u32[]{:S(2)}) collective-permute-start(f32[8,24,16,128]{3,2,1,0:T(8,128)S(1)} %get-tuple-element.59), channel_id=1, source_target_pairs={{0,8},{8,16},{16,24},{1,9},{9,17},{17,25},{2,10},{10,18},{18,26},{... | collective-permute-start | bytes 4718600 | tf_op jit(solution)/shard_map/ppermute | solution.py:118
  69.9 14.2 %collective-permute-done.edge_l = f32[32,24,128]{2,1,0:T(8,128)S(1)} collective-permute-done((f32[32,24,128]{2,1,0:T(8,128)S(1)}, f32[32,24,128]{2,1,0:T(8,128)S(1)}, u32[]{:S(2)}, u32[]{:S(2)}) %collective-permute-start) | collective-permute-done | bytes 393248 | tf_op jit(solution)/shard_map/ppermute | solution.py:118
  86.5 5.7 %all-to-all-start.1 = ((f32[8,32,16,128]{3,2,1,0:T(8,128)}), f32[8,32,16,128]{3,2,1,0:T(8,128)S(1)}, u32[]{:S(2)}, u32[]{:S(2)}) async-start(f32[8,32,16,128]{3,2,1,0:T(8,128)} %copy-done.9), calls=%async_computation.1 | async-start | bytes 4194304 | tf_op jit(solution)/shard_map/all_to_all | solution.py:556
  95.3 3.5 %collective-permute-start.8 = (f32[24,48,128]{2,1,0:T(8,128)S(1)}, f32[24,48,128]{2,1,0:T(8,128)S(1)}, u32[]{:S(2)}, u32[]{:S(2)}) collective-permute-start(f32[24,48,128]{2,1,0:T(8,128)S(1)} %get-tuple-element.94), channel_id=1, source_target_pairs={{0,8},{8,16},{16,24},{1,9},{9,17},{17,25},{2,10},{10,18},{18,26},{... | collective-permute-start | bytes 1769480 | tf_op jit(solution)/shard_map/ppermute | solution.py:118
  98.7 5.7 %collective-permute-done.9.corner_r = f32[24,48,128]{2,1,0:T(8,128)S(1)} collective-permute-done((f32[24,48,128]{2,1,0:T(8,128)S(1)}, f32[24,48,128]{2,1,0:T(8,128)S(1)}, u32[]{:S(2)}, u32[]{:S(2)}) %collective-permute-start.9) | collective-permute-done | bytes 589856 | tf_op jit(solution)/shard_map/ppermute | solution.py:122
  106.8 25.0 %correlate.2 = (f32[24,176,128]{2,1,0:T(8,128)}, f32[32,176,128]{2,1,0:T(8,128)}, f32[24,176,128]{2,1,0:T(8,128)}) custom-call(s32[2,2]{1,0:T(2,128)S(1)} %copy-done.28, f32[32,24,128]{2,1,0:T(8,128)S(1)} %collective-permute-done.edge_l, f32[32,24,128]{2,1,0:T(8,128)S(1)} %collective-permute-done.1.edge_r, f32[8,32,16,128]{3,2,1,0:T(8,128)} %copy-done.6, ...), custom_call_target="tpu_custom_call" | custom-call | bytes 90000000 | tf_op jit(solution)/shard_map/correlate/pallas_call | solution.py:437
  131.8 4.4 %collective-permute-start.10 = (f32[24,176,128]{2,1,0:T(8,128)}, f32[24,176,128]{2,1,0:T(8,128)}, u32[]{:S(2)}, u32[]{:S(2)}) collective-permute-start(f32[24,176,128]{2,1,0:T(8,128)} %get-tuple-element.74), channel_id=1, source_target_pairs={{0,8},{8,16},{16,24},{1,9},{9,17},{17,25},{2,10},{10,18},{18,26},{... | collective-permute-start | bytes 6488072 | tf_op jit(solution)/shard_map/ppermute | solution.py:118
  140.8 3.5 %collective-permute-start.4 = (f32[32,24,128]{2,1,0:T(8,128)S(1)}, f32[32,24,128]{2,1,0:T(8,128)S(1)}, u32[]{:S(2)}, u32[]{:S(2)}) collective-permute-start(f32[32,24,128]{2,1,0:T(8,128)S(1)} %get-tuple-element.62), channel_id=1, source_target_pairs={{0,1},{1,2},{2,3},{3,4},{4,5},{5,6},{6,7},{8,9},{9,10},{10,11},{11... | collective-permute-start | bytes 1179656 | tf_op jit(solution)/shard_map/ppermute | solution.py:118
  145.5 4.9 %collective-permute-start.6 = (f32[8,24,16,128]{3,2,1,0:T(8,128)S(1)}, f32[8,24,16,128]{3,2,1,0:T(8,128)S(1)}, u32[]{:S(2)}, u32[]{:S(2)}) collective-permute-start(f32[8,24,16,128]{3,2,1,0:T(8,128)S(1)} %get-tuple-element.64), channel_id=1, source_target_pairs={{0,8},{8,16},{16,24},{1,9},{9,17},{17,25},{2,10},{10,18},{18,26},{... | collective-permute-start | bytes 4718600 | tf_op jit(solution)/shard_map/ppermute | solution.py:118
  150.4 9.2 %collective-permute-done.4.edge_l = f32[32,24,128]{2,1,0:T(8,128)S(1)} collective-permute-done((f32[32,24,128]{2,1,0:T(8,128)S(1)}, f32[32,24,128]{2,1,0:T(8,128)S(1)}, u32[]{:S(2)}, u32[]{:S(2)}) %collective-permute-start.4) | collective-permute-done | bytes 393248 | tf_op jit(solution)/shard_map/ppermute | solution.py:118
  159.6 4.2 %collective-permute-start.7 = (f32[8,24,16,128]{3,2,1,0:T(8,128)S(1)}, f32[8,24,16,128]{3,2,1,0:T(8,128)S(1)}, u32[]{:S(2)}, u32[]{:S(2)}) collective-permute-start(f32[8,24,16,128]{3,2,1,0:T(8,128)S(1)} %get-tuple-element.65), channel_id=1, source_target_pairs={{8,0},{16,8},{24,16},{9,1},{17,9},{25,17},{10,2},{18,10},{26,18},{... | collective-permute-start | bytes 4718600 | tf_op jit(solution)/shard_map/ppermute | solution.py:122
  173.0 10.3 %collective-permute-done.12.corner_l = f32[24,48,128]{2,1,0:T(8,128)S(1)} collective-permute-done((f32[24,48,128]{2,1,0:T(8,128)S(1)}, f32[24,48,128]{2,1,0:T(8,128)S(1)}, u32[]{:S(2)}, u32[]{:S(2)}) %collective-permute-start.12) | collective-permute-done | bytes 589856 | tf_op jit(solution)/shard_map/ppermute | solution.py:118
  183.3 3.9 %collective-permute-start.14 = (f32[32,24,128]{2,1,0:T(8,128)S(1)}, f32[32,24,128]{2,1,0:T(8,128)S(1)}, u32[]{:S(2)}, u32[]{:S(2)}) collective-permute-start(f32[32,24,128]{2,1,0:T(8,128)S(1)} %get-tuple-element.82), channel_id=1, source_target_pairs={{0,1},{1,2},{2,3},{3,4},{4,5},{5,6},{6,7},{8,9},{9,10},{10,11},{11... | collective-permute-start | bytes 1179656 | tf_op jit(solution)/shard_map/ppermute | solution.py:118
  189.5 25.1 %correlate.3 = (f32[24,176,128]{2,1,0:T(8,128)}, f32[32,176,128]{2,1,0:T(8,128)}, f32[24,176,128]{2,1,0:T(8,128)}) custom-call(s32[2,2]{1,0:T(2,128)S(1)} %copy-done.28, f32[32,24,128]{2,1,0:T(8,128)S(1)} %collective-permute-done.4.edge_l, f32[32,24,128]{2,1,0:T(8,128)S(1)} %collective-permute-done.5.edge_r, f32[8,32,16,128]{3,2,1,0:T(8,128)} %copy-done.5, ...), custom_call_target="tpu_custom_call" | custom-call | bytes 90000000 | tf_op jit(solution)/shard_map/correlate/pallas_call | solution.py:437
  218.9 4.7 %all-to-all-start.3 = ((f32[8,32,16,128]{3,2,1,0:T(8,128)}), f32[8,32,16,128]{3,2,1,0:T(8,128)}, u32[]{:S(2)}, u32[]{:S(2)}) async-start(f32[8,32,16,128]{3,2,1,0:T(8,128)} %copy-done.10), calls=%async_computation.3 | async-start | bytes 4194304 | tf_op jit(solution)/shard_map/all_to_all | solution.py:552
  228.0 22.0 %collective-permute-done.16.from_l = f32[24,176,128]{2,1,0:T(8,128)S(1)} collective-permute-done((f32[24,176,128]{2,1,0:T(8,128)}, f32[24,176,128]{2,1,0:T(8,128)S(1)}, u32[]{:S(2)}, u32[]{:S(2)}) %collective-permute-start.16) | collective-permute-done | bytes 2162720 | tf_op jit(solution)/shard_map/ppermute | solution.py:118
  250.0 4.3 %collective-permute-done.17.from_r = f32[24,176,128]{2,1,0:T(8,128)S(1)} collective-permute-done((f32[24,176,128]{2,1,0:T(8,128)}, f32[24,176,128]{2,1,0:T(8,128)S(1)}, u32[]{:S(2)}, u32[]{:S(2)}) %collective-permute-start.17) | collective-permute-done | bytes 2162720 | tf_op jit(solution)/shard_map/ppermute | solution.py:122
  254.4 4.2 %collective-permute-start.18 = (f32[32,24,128]{2,1,0:T(8,128)S(1)}, f32[32,24,128]{2,1,0:T(8,128)S(1)}, u32[]{:S(2)}, u32[]{:S(2)}) collective-permute-start(f32[32,24,128]{2,1,0:T(8,128)S(1)} %get-tuple-element.89), channel_id=1, source_target_pairs={{0,1},{1,2},{2,3},{3,4},{4,5},{5,6},{6,7},{8,9},{9,10},{10,11},{11... | collective-permute-start | bytes 1179656 | tf_op jit(solution)/shard_map/ppermute | solution.py:118
  259.9 5.5 %collective-permute-done.18.edge_l = f32[32,24,128]{2,1,0:T(8,128)S(1)} collective-permute-done((f32[32,24,128]{2,1,0:T(8,128)S(1)}, f32[32,24,128]{2,1,0:T(8,128)S(1)}, u32[]{:S(2)}, u32[]{:S(2)}) %collective-permute-start.18) | collective-permute-done | bytes 393248 | tf_op jit(solution)/shard_map/ppermute | solution.py:118
  269.0 9.0 %all-to-all-start.2 = ((f32[8,32,16,128]{3,2,1,0:T(8,128)}), f32[8,32,16,128]{3,2,1,0:T(8,128)S(1)}, u32[]{:S(2)}, u32[]{:S(2)}) async-start(f32[8,32,16,128]{3,2,1,0:T(8,128)} %copy-done.12), calls=%async_computation.2 | async-start | bytes 4194304 | tf_op jit(solution)/shard_map/all_to_all | solution.py:552
  283.0 38.9 %all-to-all-done.2.spread = f32[8,32,16,128]{3,2,1,0:T(8,128)S(1)} async-done(((f32[8,32,16,128]{3,2,1,0:T(8,128)}), f32[8,32,16,128]{3,2,1,0:T(8,128)S(1)}, u32[]{:S(2)}, u32[]{:S(2)}) %all-to-all-start.2) | async-done | bytes 2097184 | tf_op jit(solution)/shard_map/all_to_all | solution.py:552
  (109 shorter events, 72.4 us)
Async XLA Ops:
  4.1 53.7 %all-to-all-start = ((f32[8,32,16,128]{3,2,1,0:T(8,128)}), f32[8,32,16,128]{3,2,1,0:T(8,128)S(1)}, u32[]{:S(2)}, u32[]{:S(2)}) async-start(f32[8,32,16,128]{3,2,1,0:T(8,128)} %copy-done.11), calls=%async_computation | async-start | bytes 4194304 | tf_op jit(solution)/shard_map/all_to_all | solution.py:556
  58.7 25.4 %collective-permute-start.2 = (f32[8,24,16,128]{3,2,1,0:T(8,128)S(1)}, f32[8,24,16,128]{3,2,1,0:T(8,128)S(1)}, u32[]{:S(2)}, u32[]{:S(2)}) collective-permute-start(f32[8,24,16,128]{3,2,1,0:T(8,128)S(1)} %get-tuple-element.59), channel_id=1, source_target_pairs={{0,8},{8,16},{16,24},{1,9},{9,17},{17,25},{2,10},{10,18},{18,26},{... | collective-permute-start | bytes 4718600 | tf_op jit(solution)/shard_map/ppermute | solution.py:118
  63.6 21.8 %collective-permute-start.3 = (f32[8,24,16,128]{3,2,1,0:T(8,128)S(1)}, f32[8,24,16,128]{3,2,1,0:T(8,128)S(1)}, u32[]{:S(2)}, u32[]{:S(2)}) collective-permute-start(f32[8,24,16,128]{3,2,1,0:T(8,128)S(1)} %get-tuple-element.60), channel_id=1, source_target_pairs={{8,0},{16,8},{24,16},{9,1},{17,9},{25,17},{10,2},{18,10},{26,18},{... | collective-permute-start | bytes 4718600 | tf_op jit(solution)/shard_map/ppermute | solution.py:122
  65.5 18.6 %collective-permute-start = (f32[32,24,128]{2,1,0:T(8,128)S(1)}, f32[32,24,128]{2,1,0:T(8,128)S(1)}, u32[]{:S(2)}, u32[]{:S(2)}) collective-permute-start(f32[32,24,128]{2,1,0:T(8,128)S(1)} %get-tuple-element.57), channel_id=1, source_target_pairs={{0,1},{1,2},{2,3},{3,4},{4,5},{5,6},{6,7},{8,9},{9,10},{10,11},{11... | collective-permute-start | bytes 1179656 | tf_op jit(solution)/shard_map/ppermute | solution.py:118
  68.6 15.5 %collective-permute-start.1 = (f32[32,24,128]{2,1,0:T(8,128)S(1)}, f32[32,24,128]{2,1,0:T(8,128)S(1)}, u32[]{:S(2)}, u32[]{:S(2)}) collective-permute-start(f32[32,24,128]{2,1,0:T(8,128)S(1)} %get-tuple-element.58), channel_id=1, source_target_pairs={{1,0},{2,1},{3,2},{4,3},{5,4},{6,5},{7,6},{9,8},{10,9},{11,10},{12... | collective-permute-start | bytes 1179656 | tf_op jit(solution)/shard_map/ppermute | solution.py:122
  86.5 53.4 %all-to-all-start.1 = ((f32[8,32,16,128]{3,2,1,0:T(8,128)}), f32[8,32,16,128]{3,2,1,0:T(8,128)S(1)}, u32[]{:S(2)}, u32[]{:S(2)}) async-start(f32[8,32,16,128]{3,2,1,0:T(8,128)} %copy-done.9), calls=%async_computation.1 | async-start | bytes 4194304 | tf_op jit(solution)/shard_map/all_to_all | solution.py:556
  92.4 12.1 %collective-permute-start.9 = (f32[24,48,128]{2,1,0:T(8,128)S(1)}, f32[24,48,128]{2,1,0:T(8,128)S(1)}, u32[]{:S(2)}, u32[]{:S(2)}) collective-permute-start(f32[24,48,128]{2,1,0:T(8,128)S(1)} %get-tuple-element.93), channel_id=1, source_target_pairs={{8,0},{16,8},{24,16},{9,1},{17,9},{25,17},{10,2},{18,10},{26,18},{... | collective-permute-start | bytes 1769480 | tf_op jit(solution)/shard_map/ppermute | solution.py:122
  95.3 10.1 %collective-permute-start.8 = (f32[24,48,128]{2,1,0:T(8,128)S(1)}, f32[24,48,128]{2,1,0:T(8,128)S(1)}, u32[]{:S(2)}, u32[]{:S(2)}) collective-permute-start(f32[24,48,128]{2,1,0:T(8,128)S(1)} %get-tuple-element.94), channel_id=1, source_target_pairs={{0,8},{8,16},{16,24},{1,9},{9,17},{17,25},{2,10},{10,18},{18,26},{... | collective-permute-start | bytes 1769480 | tf_op jit(solution)/shard_map/ppermute | solution.py:118
  131.8 32.2 %collective-permute-start.10 = (f32[24,176,128]{2,1,0:T(8,128)}, f32[24,176,128]{2,1,0:T(8,128)}, u32[]{:S(2)}, u32[]{:S(2)}) collective-permute-start(f32[24,176,128]{2,1,0:T(8,128)} %get-tuple-element.74), channel_id=1, source_target_pairs={{0,8},{8,16},{16,24},{1,9},{9,17},{17,25},{2,10},{10,18},{18,26},{... | collective-permute-start | bytes 6488072 | tf_op jit(solution)/shard_map/ppermute | solution.py:118
  136.2 28.4 %collective-permute-start.11 = (f32[24,176,128]{2,1,0:T(8,128)}, f32[24,176,128]{2,1,0:T(8,128)}, u32[]{:S(2)}, u32[]{:S(2)}) collective-permute-start(f32[24,176,128]{2,1,0:T(8,128)} %get-tuple-element.75), channel_id=1, source_target_pairs={{8,0},{16,8},{24,16},{9,1},{17,9},{25,17},{10,2},{18,10},{26,18},{... | collective-permute-start | bytes 6488072 | tf_op jit(solution)/shard_map/ppermute | solution.py:122
  140.8 18.8 %collective-permute-start.4 = (f32[32,24,128]{2,1,0:T(8,128)S(1)}, f32[32,24,128]{2,1,0:T(8,128)S(1)}, u32[]{:S(2)}, u32[]{:S(2)}) collective-permute-start(f32[32,24,128]{2,1,0:T(8,128)S(1)} %get-tuple-element.62), channel_id=1, source_target_pairs={{0,1},{1,2},{2,3},{3,4},{4,5},{5,6},{6,7},{8,9},{9,10},{10,11},{11... | collective-permute-start | bytes 1179656 | tf_op jit(solution)/shard_map/ppermute | solution.py:118
  144.2 19.7 %collective-permute-start.5 = (f32[32,24,128]{2,1,0:T(8,128)S(1)}, f32[32,24,128]{2,1,0:T(8,128)S(1)}, u32[]{:S(2)}, u32[]{:S(2)}) collective-permute-start(f32[32,24,128]{2,1,0:T(8,128)S(1)} %get-tuple-element.63), channel_id=1, source_target_pairs={{1,0},{2,1},{3,2},{4,3},{5,4},{6,5},{7,6},{9,8},{10,9},{11,10},{12... | collective-permute-start | bytes 1179656 | tf_op jit(solution)/shard_map/ppermute | solution.py:122
  145.5 44.0 %collective-permute-start.6 = (f32[8,24,16,128]{3,2,1,0:T(8,128)S(1)}, f32[8,24,16,128]{3,2,1,0:T(8,128)S(1)}, u32[]{:S(2)}, u32[]{:S(2)}) collective-permute-start(f32[8,24,16,128]{3,2,1,0:T(8,128)S(1)} %get-tuple-element.64), channel_id=1, source_target_pairs={{0,8},{8,16},{16,24},{1,9},{9,17},{17,25},{2,10},{10,18},{18,26},{... | collective-permute-start | bytes 4718600 | tf_op jit(solution)/shard_map/ppermute | solution.py:118
  159.6 29.9 %collective-permute-start.7 = (f32[8,24,16,128]{3,2,1,0:T(8,128)S(1)}, f32[8,24,16,128]{3,2,1,0:T(8,128)S(1)}, u32[]{:S(2)}, u32[]{:S(2)}) collective-permute-start(f32[8,24,16,128]{3,2,1,0:T(8,128)S(1)} %get-tuple-element.65), channel_id=1, source_target_pairs={{8,0},{16,8},{24,16},{9,1},{17,9},{25,17},{10,2},{18,10},{26,18},{... | collective-permute-start | bytes 4718600 | tf_op jit(solution)/shard_map/ppermute | solution.py:122
  164.6 18.7 %collective-permute-start.12 = (f32[24,48,128]{2,1,0:T(8,128)S(1)}, f32[24,48,128]{2,1,0:T(8,128)S(1)}, u32[]{:S(2)}, u32[]{:S(2)}) collective-permute-start(f32[24,48,128]{2,1,0:T(8,128)S(1)} %get-tuple-element.76), channel_id=1, source_target_pairs={{0,8},{8,16},{16,24},{1,9},{9,17},{17,25},{2,10},{10,18},{18,26},{... | collective-permute-start | bytes 1769480 | tf_op jit(solution)/shard_map/ppermute | solution.py:118
  167.4 22.1 %collective-permute-start.13 = (f32[24,48,128]{2,1,0:T(8,128)S(1)}, f32[24,48,128]{2,1,0:T(8,128)S(1)}, u32[]{:S(2)}, u32[]{:S(2)}) collective-permute-start(f32[24,48,128]{2,1,0:T(8,128)S(1)} %get-tuple-element.77), channel_id=1, source_target_pairs={{8,0},{16,8},{24,16},{9,1},{17,9},{25,17},{10,2},{18,10},{26,18},{... | collective-permute-start | bytes 1769480 | tf_op jit(solution)/shard_map/ppermute | solution.py:122
  171.7 42.9 %collective-permute-start.15 = (f32[32,24,128]{2,1,0:T(8,128)S(1)}, f32[32,24,128]{2,1,0:T(8,128)S(1)}, u32[]{:S(2)}, u32[]{:S(2)}) collective-permute-start(f32[32,24,128]{2,1,0:T(8,128)S(1)} %get-tuple-element.81), channel_id=1, source_target_pairs={{1,0},{2,1},{3,2},{4,3},{5,4},{6,5},{7,6},{9,8},{10,9},{11,10},{12... | collective-permute-start | bytes 1179656 | tf_op jit(solution)/shard_map/ppermute | solution.py:122
  183.3 31.4 %collective-permute-start.14 = (f32[32,24,128]{2,1,0:T(8,128)S(1)}, f32[32,24,128]{2,1,0:T(8,128)S(1)}, u32[]{:S(2)}, u32[]{:S(2)}) collective-permute-start(f32[32,24,128]{2,1,0:T(8,128)S(1)} %get-tuple-element.82), channel_id=1, source_target_pairs={{0,1},{1,2},{2,3},{3,4},{4,5},{5,6},{6,7},{8,9},{9,10},{10,11},{11... | collective-permute-start | bytes 1179656 | tf_op jit(solution)/shard_map/ppermute | solution.py:118
  218.9 50.2 %all-to-all-start.3 = ((f32[8,32,16,128]{3,2,1,0:T(8,128)}), f32[8,32,16,128]{3,2,1,0:T(8,128)}, u32[]{:S(2)}, u32[]{:S(2)}) async-start(f32[8,32,16,128]{3,2,1,0:T(8,128)} %copy-done.10), calls=%async_computation.3 | async-start | bytes 4194304 | tf_op jit(solution)/shard_map/all_to_all | solution.py:552
  223.5 26.4 %collective-permute-start.16 = (f32[24,176,128]{2,1,0:T(8,128)}, f32[24,176,128]{2,1,0:T(8,128)S(1)}, u32[]{:S(2)}, u32[]{:S(2)}) collective-permute-start(f32[24,176,128]{2,1,0:T(8,128)} %get-tuple-element.87), channel_id=1, source_target_pairs={{0,8},{8,16},{16,24},{1,9},{9,17},{17,25},{2,10},{10,18},{18,26},{... | collective-permute-start | bytes 6488072 | tf_op jit(solution)/shard_map/ppermute | solution.py:118
  226.0 28.3 %collective-permute-start.17 = (f32[24,176,128]{2,1,0:T(8,128)}, f32[24,176,128]{2,1,0:T(8,128)S(1)}, u32[]{:S(2)}, u32[]{:S(2)}) collective-permute-start(f32[24,176,128]{2,1,0:T(8,128)} %get-tuple-element.88), channel_id=1, source_target_pairs={{8,0},{16,8},{24,16},{9,1},{17,9},{25,17},{10,2},{18,10},{26,18},{... | collective-permute-start | bytes 6488072 | tf_op jit(solution)/shard_map/ppermute | solution.py:122
  254.4 11.0 %collective-permute-start.18 = (f32[32,24,128]{2,1,0:T(8,128)S(1)}, f32[32,24,128]{2,1,0:T(8,128)S(1)}, u32[]{:S(2)}, u32[]{:S(2)}) collective-permute-start(f32[32,24,128]{2,1,0:T(8,128)S(1)} %get-tuple-element.89), channel_id=1, source_target_pairs={{0,1},{1,2},{2,3},{3,4},{4,5},{5,6},{6,7},{8,9},{9,10},{10,11},{11... | collective-permute-start | bytes 1179656 | tf_op jit(solution)/shard_map/ppermute | solution.py:118
  258.6 8.5 %collective-permute-start.19 = (f32[32,24,128]{2,1,0:T(8,128)S(1)}, f32[32,24,128]{2,1,0:T(8,128)S(1)}, u32[]{:S(2)}, u32[]{:S(2)}) collective-permute-start(f32[32,24,128]{2,1,0:T(8,128)S(1)} %get-tuple-element.90), channel_id=1, source_target_pairs={{1,0},{2,1},{3,2},{4,3},{5,4},{6,5},{7,6},{9,8},{10,9},{11,10},{12... | collective-permute-start | bytes 1179656 | tf_op jit(solution)/shard_map/ppermute | solution.py:122
  269.0 52.9 %all-to-all-start.2 = ((f32[8,32,16,128]{3,2,1,0:T(8,128)}), f32[8,32,16,128]{3,2,1,0:T(8,128)S(1)}, u32[]{:S(2)}, u32[]{:S(2)}) async-start(f32[8,32,16,128]{3,2,1,0:T(8,128)} %copy-done.12), calls=%async_computation.2 | async-start | bytes 4194304 | tf_op jit(solution)/shard_map/all_to_all | solution.py:552
  (31 other events, 284.8 us)

commit v4 on v3

--- a/solution.py
+++ b/solution.py
@@ -522,7 +522,7 @@
         out_specs=block,
         out_shape=jax.ShapeDtypeStruct(estimate.shape, F32),
         input_output_aliases={2: 0} if extra else {},
-        compiler_params=params(),
+        compiler_params=params(60),
         cost_estimate=cost(4),
         name="update",
     )(spread, estimate, *extra)

time: 327 us -> 328 us (level)
    unnamed x64 -> x62, local copies, waits for them, and re-layouts: 24.8 us -> 21.7 us
where the time goes in v4:
time: 328 us; the launch traced here: 327 us
  waiting for transfers between devices  142 us (43%)
  starting transfers between devices  83.1 us (25%)
  Pallas kernels  79.3 us (24%)
  local copies, waits for them, and re-layouts  22 us (7%)
    ppermute x10, waiting for transfers between devices, upward(): lax.ppermute(value, axis, [(i, i + 1) for i in range(lax.axis_size(axis)...  62.1 us
    pallas_call x2, Pallas kernels, correlate(): pl.pallas_call(functools.partial(correlate_kernel, c, count), out_shape=(...  50.1 us
    all_to_all x2, waiting for transfers between devices, close(): summed = lax.all_to_all(sums, 'slab', 0, 0, tiled=True)  40.5 us
    ppermute x10, starting transfers between devices, upward(): lax.ppermute(value, axis, [(i, i + 1) for i in range(lax.axis_size(axis)...  37.4 us
    all_to_all x2, waiting for transfers between devices, fast_shards(): own = lax.all_to_all(sent[c], 'slab', 0, 0, tiled=True)  24.3 us
    unnamed x62, local copies, waits for them, and re-layouts  21.7 us
    ppermute x10, starting transfers between devices, downward(): lax.ppermute(value, axis, [(i + 1, i) for i in range(lax.axis_size(axis)...  20 us
    ppermute x10, waiting for transfers between devices, downward(): lax.ppermute(value, axis, [(i + 1, i) for i in range(lax.axis_size(axis)...  14.6 us
  transfers between devices with their start and end apart: 24, of which 14 were waited for; matrix products, arithmetic and copies ran while one was open for 0% of the time, Pallas kernels for 22%

profile of v4, /device:TPU:1, one launch (start us, length us, event | category | flops | bytes accessed | tf_op | source)
XLA Modules:
  0.0 326.7 jit_solution(16138466204314525479)
XLA Ops:
  4.1 6.4 %all-to-all-start = ((f32[8,32,16,128]{3,2,1,0:T(8,128)}), f32[8,32,16,128]{3,2,1,0:T(8,128)S(1)}, u32[]{:S(2)}, u32[]{:S(2)}) async-start(f32[8,32,16,128]{3,2,1,0:T(8,128)} %copy-done.9), calls=%async_computation | async-start | bytes 4194304 | tf_op jit(solution)/shard_map/all_to_all | solution.py:556
  20.4 11.1 %tables.1 = (bf16[768,256]{1,0:T(8,128)(2,1)S(1)}, bf16[768,256]{1,0:T(8,128)(2,1)S(1)}, bf16[2,128,384]{2,1,0:T(8,128)(2,1)S(1)}, bf16[2,128,384]{2,1,0:T(8,128...) custom-call(f32[2,2,31]{2,1,0:T(2,128)S(1)} %fusion.1.taps_xy, ...), custom_call_target="tpu_custom_call" | custom-call | bytes 50400000 | tf_op jit(solution)/shard_map/tables/pallas_call | solution.py:205
  35.2 22.6 %all-to-all-done.block.own = f32[8,32,16,128]{3,2,1,0:T(8,128)S(1)} async-done(((f32[8,32,16,128]{3,2,1,0:T(8,128)}), f32[8,32,16,128]{3,2,1,0:T(8,128)S(1)}, u32[]{:S(2)}, u32[]{:S(2)}) %all-to-all-start) | async-done | bytes 2097184 | tf_op jit(solution)/shard_map/all_to_all | solution.py:556
  58.7 4.9 %collective-permute-start.2 = (f32[8,24,16,128]{3,2,1,0:T(8,128)S(1)}, f32[8,24,16,128]{3,2,1,0:T(8,128)S(1)}, u32[]{:S(2)}, u32[]{:S(2)}) collective-permute-start(f32[8,24,16,128]{3,2,1,0:T(8,128)S(1)} %get-tuple-element.59), channel_id=1, source_target_pairs={{0,8},{8,16},{16,24},{1,9},{9,17},{17,25},{2,10},{10,18},{18,26},{... | collective-permute-start | bytes 4718600 | tf_op jit(solution)/shard_map/ppermute | solution.py:118
  69.9 14.2 %collective-permute-done.edge_l = f32[32,24,128]{2,1,0:T(8,128)S(1)} collective-permute-done((f32[32,24,128]{2,1,0:T(8,128)S(1)}, f32[32,24,128]{2,1,0:T(8,128)S(1)}, u32[]{:S(2)}, u32[]{:S(2)}) %collective-permute-start) | collective-permute-done | bytes 393248 | tf_op jit(solution)/shard_map/ppermute | solution.py:118
  86.5 5.7 %all-to-all-start.1 = ((f32[8,32,16,128]{3,2,1,0:T(8,128)}), f32[8,32,16,128]{3,2,1,0:T(8,128)S(1)}, u32[]{:S(2)}, u32[]{:S(2)}) async-start(f32[8,32,16,128]{3,2,1,0:T(8,128)} %copy-done.7), calls=%async_computation.1 | async-start | bytes 4194304 | tf_op jit(solution)/shard_map/all_to_all | solution.py:556
  95.3 3.5 %collective-permute-start.8 = (f32[24,48,128]{2,1,0:T(8,128)S(1)}, f32[24,48,128]{2,1,0:T(8,128)S(1)}, u32[]{:S(2)}, u32[]{:S(2)}) collective-permute-start(f32[24,48,128]{2,1,0:T(8,128)S(1)} %get-tuple-element.94), channel_id=1, source_target_pairs={{0,8},{8,16},{16,24},{1,9},{9,17},{17,25},{2,10},{10,18},{18,26},{... | collective-permute-start | bytes 1769480 | tf_op jit(solution)/shard_map/ppermute | solution.py:118
  98.7 5.7 %collective-permute-done.9.corner_r = f32[24,48,128]{2,1,0:T(8,128)S(1)} collective-permute-done((f32[24,48,128]{2,1,0:T(8,128)S(1)}, f32[24,48,128]{2,1,0:T(8,128)S(1)}, u32[]{:S(2)}, u32[]{:S(2)}) %collective-permute-start.9) | collective-permute-done | bytes 589856 | tf_op jit(solution)/shard_map/ppermute | solution.py:122
  106.8 25.0 %correlate.2 = (f32[24,176,128]{2,1,0:T(8,128)}, f32[32,176,128]{2,1,0:T(8,128)}, f32[24,176,128]{2,1,0:T(8,128)}) custom-call(s32[2,2]{1,0:T(2,128)S(1)} %copy-done.26, f32[32,24,128]{2,1,0:T(8,128)S(1)} %collective-permute-done.edge_l, f32[32,24,128]{2,1,0:T(8,128)S(1)} %collective-permute-done.1.edge_r, f32[8,32,16,128]{3,2,1,0:T(8,128)} %copy-done.4, ...), custom_call_target="tpu_custom_call" | custom-call | bytes 90000000 | tf_op jit(solution)/shard_map/correlate/pallas_call | solution.py:437
  131.8 4.4 %collective-permute-start.10 = (f32[24,176,128]{2,1,0:T(8,128)}, f32[24,176,128]{2,1,0:T(8,128)}, u32[]{:S(2)}, u32[]{:S(2)}) collective-permute-start(f32[24,176,128]{2,1,0:T(8,128)} %get-tuple-element.74), channel_id=1, source_target_pairs={{0,8},{8,16},{16,24},{1,9},{9,17},{17,25},{2,10},{10,18},{18,26},{... | collective-permute-start | bytes 6488072 | tf_op jit(solution)/shard_map/ppermute | solution.py:118
  140.7 3.5 %collective-permute-start.4 = (f32[32,24,128]{2,1,0:T(8,128)S(1)}, f32[32,24,128]{2,1,0:T(8,128)S(1)}, u32[]{:S(2)}, u32[]{:S(2)}) collective-permute-start(f32[32,24,128]{2,1,0:T(8,128)S(1)} %get-tuple-element.62), channel_id=1, source_target_pairs={{0,1},{1,2},{2,3},{3,4},{4,5},{5,6},{6,7},{8,9},{9,10},{10,11},{11... | collective-permute-start | bytes 1179656 | tf_op jit(solution)/shard_map/ppermute | solution.py:118
  145.5 4.9 %collective-permute-start.6 = (f32[8,24,16,128]{3,2,1,0:T(8,128)S(1)}, f32[8,24,16,128]{3,2,1,0:T(8,128)S(1)}, u32[]{:S(2)}, u32[]{:S(2)}) collective-permute-start(f32[8,24,16,128]{3,2,1,0:T(8,128)S(1)} %get-tuple-element.64), channel_id=1, source_target_pairs={{0,8},{8,16},{16,24},{1,9},{9,17},{17,25},{2,10},{10,18},{18,26},{... | collective-permute-start | bytes 4718600 | tf_op jit(solution)/shard_map/ppermute | solution.py:118
  150.4 9.2 %collective-permute-done.4.edge_l = f32[32,24,128]{2,1,0:T(8,128)S(1)} collective-permute-done((f32[32,24,128]{2,1,0:T(8,128)S(1)}, f32[32,24,128]{2,1,0:T(8,128)S(1)}, u32[]{:S(2)}, u32[]{:S(2)}) %collective-permute-start.4) | collective-permute-done | bytes 393248 | tf_op jit(solution)/shard_map/ppermute | solution.py:118
  159.6 4.2 %collective-permute-start.7 = (f32[8,24,16,128]{3,2,1,0:T(8,128)S(1)}, f32[8,24,16,128]{3,2,1,0:T(8,128)S(1)}, u32[]{:S(2)}, u32[]{:S(2)}) collective-permute-start(f32[8,24,16,128]{3,2,1,0:T(8,128)S(1)} %get-tuple-element.65), channel_id=1, source_target_pairs={{8,0},{16,8},{24,16},{9,1},{17,9},{25,17},{10,2},{18,10},{26,18},{... | collective-permute-start | bytes 4718600 | tf_op jit(solution)/shard_map/ppermute | solution.py:122
  173.0 10.3 %collective-permute-done.12.corner_l = f32[24,48,128]{2,1,0:T(8,128)S(1)} collective-permute-done((f32[24,48,128]{2,1,0:T(8,128)S(1)}, f32[24,48,128]{2,1,0:T(8,128)S(1)}, u32[]{:S(2)}, u32[]{:S(2)}) %collective-permute-start.12) | collective-permute-done | bytes 589856 | tf_op jit(solution)/shard_map/ppermute | solution.py:118
  183.3 3.9 %collective-permute-start.14 = (f32[32,24,128]{2,1,0:T(8,128)S(1)}, f32[32,24,128]{2,1,0:T(8,128)S(1)}, u32[]{:S(2)}, u32[]{:S(2)}) collective-permute-start(f32[32,24,128]{2,1,0:T(8,128)S(1)} %get-tuple-element.82), channel_id=1, source_target_pairs={{0,1},{1,2},{2,3},{3,4},{4,5},{5,6},{6,7},{8,9},{9,10},{10,11},{11... | collective-permute-start | bytes 1179656 | tf_op jit(solution)/shard_map/ppermute | solution.py:118
  189.5 25.1 %correlate.3 = (f32[24,176,128]{2,1,0:T(8,128)}, f32[32,176,128]{2,1,0:T(8,128)}, f32[24,176,128]{2,1,0:T(8,128)}) custom-call(s32[2,2]{1,0:T(2,128)S(1)} %copy-done.26, f32[32,24,128]{2,1,0:T(8,128)S(1)} %collective-permute-done.4.edge_l, f32[32,24,128]{2,1,0:T(8,128)S(1)} %collective-permute-done.5.edge_r, f32[8,32,16,128]{3,2,1,0:T(8,128)} %copy-done.3, ...), custom_call_target="tpu_custom_call" | custom-call | bytes 90000000 | tf_op jit(solution)/shard_map/correlate/pallas_call | solution.py:437
  218.9 4.6 %all-to-all-start.3 = ((f32[8,32,16,128]{3,2,1,0:T(8,128)}), f32[8,32,16,128]{3,2,1,0:T(8,128)}, u32[]{:S(2)}, u32[]{:S(2)}) async-start(f32[8,32,16,128]{3,2,1,0:T(8,128)} %copy-done.8), calls=%async_computation.3 | async-start | bytes 4194304 | tf_op jit(solution)/shard_map/all_to_all | solution.py:552
  228.0 22.0 %collective-permute-done.16.from_l = f32[24,176,128]{2,1,0:T(8,128)S(1)} collective-permute-done((f32[24,176,128]{2,1,0:T(8,128)}, f32[24,176,128]{2,1,0:T(8,128)S(1)}, u32[]{:S(2)}, u32[]{:S(2)}) %collective-permute-start.16) | collective-permute-done | bytes 2162720 | tf_op jit(solution)/shard_map/ppermute | solution.py:118
  250.0 4.3 %collective-permute-done.17.from_r = f32[24,176,128]{2,1,0:T(8,128)S(1)} collective-permute-done((f32[24,176,128]{2,1,0:T(8,128)}, f32[24,176,128]{2,1,0:T(8,128)S(1)}, u32[]{:S(2)}, u32[]{:S(2)}) %collective-permute-start.17) | collective-permute-done | bytes 2162720 | tf_op jit(solution)/shard_map/ppermute | solution.py:122
  254.4 4.2 %collective-permute-start.18 = (f32[32,24,128]{2,1,0:T(8,128)S(1)}, f32[32,24,128]{2,1,0:T(8,128)S(1)}, u32[]{:S(2)}, u32[]{:S(2)}) collective-permute-start(f32[32,24,128]{2,1,0:T(8,128)S(1)} %get-tuple-element.89), channel_id=1, source_target_pairs={{0,1},{1,2},{2,3},{3,4},{4,5},{5,6},{6,7},{8,9},{9,10},{10,11},{11... | collective-permute-start | bytes 1179656 | tf_op jit(solution)/shard_map/ppermute | solution.py:118
  259.8 5.5 %collective-permute-done.18.edge_l = f32[32,24,128]{2,1,0:T(8,128)S(1)} collective-permute-done((f32[32,24,128]{2,1,0:T(8,128)S(1)}, f32[32,24,128]{2,1,0:T(8,128)S(1)}, u32[]{:S(2)}, u32[]{:S(2)}) %collective-permute-start.18) | collective-permute-done | bytes 393248 | tf_op jit(solution)/shard_map/ppermute | solution.py:118
  269.0 9.0 %all-to-all-start.2 = ((f32[8,32,16,128]{3,2,1,0:T(8,128)}), f32[8,32,16,128]{3,2,1,0:T(8,128)S(1)}, u32[]{:S(2)}, u32[]{:S(2)}) async-start(f32[8,32,16,128]{3,2,1,0:T(8,128)} %copy-done.10), calls=%async_computation.2 | async-start | bytes 4194304 | tf_op jit(solution)/shard_map/all_to_all | solution.py:552
  281.4 40.5 %all-to-all-done.2.spread = f32[8,32,16,128]{3,2,1,0:T(8,128)S(1)} async-done(((f32[8,32,16,128]{3,2,1,0:T(8,128)}), f32[8,32,16,128]{3,2,1,0:T(8,128)S(1)}, u32[]{:S(2)}, u32[]{:S(2)}) %all-to-all-start.2) | async-done | bytes 2097184 | tf_op jit(solution)/shard_map/all_to_all | solution.py:552
  (107 shorter events, 71.6 us)
Async XLA Ops:
  4.1 53.7 %all-to-all-start = ((f32[8,32,16,128]{3,2,1,0:T(8,128)}), f32[8,32,16,128]{3,2,1,0:T(8,128)S(1)}, u32[]{:S(2)}, u32[]{:S(2)}) async-start(f32[8,32,16,128]{3,2,1,0:T(8,128)} %copy-done.9), calls=%async_computation | async-start | bytes 4194304 | tf_op jit(solution)/shard_map/all_to_all | solution.py:556
  58.7 25.4 %collective-permute-start.2 = (f32[8,24,16,128]{3,2,1,0:T(8,128)S(1)}, f32[8,24,16,128]{3,2,1,0:T(8,128)S(1)}, u32[]{:S(2)}, u32[]{:S(2)}) collective-permute-start(f32[8,24,16,128]{3,2,1,0:T(8,128)S(1)} %get-tuple-element.59), channel_id=1, source_target_pairs={{0,8},{8,16},{16,24},{1,9},{9,17},{17,25},{2,10},{10,18},{18,26},{... | collective-permute-start | bytes 4718600 | tf_op jit(solution)/shard_map/ppermute | solution.py:118
  63.6 21.7 %collective-permute-start.3 = (f32[8,24,16,128]{3,2,1,0:T(8,128)S(1)}, f32[8,24,16,128]{3,2,1,0:T(8,128)S(1)}, u32[]{:S(2)}, u32[]{:S(2)}) collective-permute-start(f32[8,24,16,128]{3,2,1,0:T(8,128)S(1)} %get-tuple-element.60), channel_id=1, source_target_pairs={{8,0},{16,8},{24,16},{9,1},{17,9},{25,17},{10,2},{18,10},{26,18},{... | collective-permute-start | bytes 4718600 | tf_op jit(solution)/shard_map/ppermute | solution.py:122
  65.5 18.6 %collective-permute-start = (f32[32,24,128]{2,1,0:T(8,128)S(1)}, f32[32,24,128]{2,1,0:T(8,128)S(1)}, u32[]{:S(2)}, u32[]{:S(2)}) collective-permute-start(f32[32,24,128]{2,1,0:T(8,128)S(1)} %get-tuple-element.57), channel_id=1, source_target_pairs={{0,1},{1,2},{2,3},{3,4},{4,5},{5,6},{6,7},{8,9},{9,10},{10,11},{11... | collective-permute-start | bytes 1179656 | tf_op jit(solution)/shard_map/ppermute | solution.py:118
  68.6 15.5 %collective-permute-start.1 = (f32[32,24,128]{2,1,0:T(8,128)S(1)}, f32[32,24,128]{2,1,0:T(8,128)S(1)}, u32[]{:S(2)}, u32[]{:S(2)}) collective-permute-start(f32[32,24,128]{2,1,0:T(8,128)S(1)} %get-tuple-element.58), channel_id=1, source_target_pairs={{1,0},{2,1},{3,2},{4,3},{5,4},{6,5},{7,6},{9,8},{10,9},{11,10},{12... | collective-permute-start | bytes 1179656 | tf_op jit(solution)/shard_map/ppermute | solution.py:122
  86.5 53.4 %all-to-all-start.1 = ((f32[8,32,16,128]{3,2,1,0:T(8,128)}), f32[8,32,16,128]{3,2,1,0:T(8,128)S(1)}, u32[]{:S(2)}, u32[]{:S(2)}) async-start(f32[8,32,16,128]{3,2,1,0:T(8,128)} %copy-done.7), calls=%async_computation.1 | async-start | bytes 4194304 | tf_op jit(solution)/shard_map/all_to_all | solution.py:556
  92.4 12.1 %collective-permute-start.9 = (f32[24,48,128]{2,1,0:T(8,128)S(1)}, f32[24,48,128]{2,1,0:T(8,128)S(1)}, u32[]{:S(2)}, u32[]{:S(2)}) collective-permute-start(f32[24,48,128]{2,1,0:T(8,128)S(1)} %get-tuple-element.93), channel_id=1, source_target_pairs={{8,0},{16,8},{24,16},{9,1},{17,9},{25,17},{10,2},{18,10},{26,18},{... | collective-permute-start | bytes 1769480 | tf_op jit(solution)/shard_map/ppermute | solution.py:122
  95.3 10.1 %collective-permute-start.8 = (f32[24,48,128]{2,1,0:T(8,128)S(1)}, f32[24,48,128]{2,1,0:T(8,128)S(1)}, u32[]{:S(2)}, u32[]{:S(2)}) collective-permute-start(f32[24,48,128]{2,1,0:T(8,128)S(1)} %get-tuple-element.94), channel_id=1, source_target_pairs={{0,8},{8,16},{16,24},{1,9},{9,17},{17,25},{2,10},{10,18},{18,26},{... | collective-permute-start | bytes 1769480 | tf_op jit(solution)/shard_map/ppermute | solution.py:118
  131.8 32.2 %collective-permute-start.10 = (f32[24,176,128]{2,1,0:T(8,128)}, f32[24,176,128]{2,1,0:T(8,128)}, u32[]{:S(2)}, u32[]{:S(2)}) collective-permute-start(f32[24,176,128]{2,1,0:T(8,128)} %get-tuple-element.74), channel_id=1, source_target_pairs={{0,8},{8,16},{16,24},{1,9},{9,17},{17,25},{2,10},{10,18},{18,26},{... | collective-permute-start | bytes 6488072 | tf_op jit(solution)/shard_map/ppermute | solution.py:118
  136.2 28.4 %collective-permute-start.11 = (f32[24,176,128]{2,1,0:T(8,128)}, f32[24,176,128]{2,1,0:T(8,128)}, u32[]{:S(2)}, u32[]{:S(2)}) collective-permute-start(f32[24,176,128]{2,1,0:T(8,128)} %get-tuple-element.75), channel_id=1, source_target_pairs={{8,0},{16,8},{24,16},{9,1},{17,9},{25,17},{10,2},{18,10},{26,18},{... | collective-permute-start | bytes 6488072 | tf_op jit(solution)/shard_map/ppermute | solution.py:122
  140.7 18.8 %collective-permute-start.4 = (f32[32,24,128]{2,1,0:T(8,128)S(1)}, f32[32,24,128]{2,1,0:T(8,128)S(1)}, u32[]{:S(2)}, u32[]{:S(2)}) collective-permute-start(f32[32,24,128]{2,1,0:T(8,128)S(1)} %get-tuple-element.62), channel_id=1, source_target_pairs={{0,1},{1,2},{2,3},{3,4},{4,5},{5,6},{6,7},{8,9},{9,10},{10,11},{11... | collective-permute-start | bytes 1179656 | tf_op jit(solution)/shard_map/ppermute | solution.py:118
  144.2 19.7 %collective-permute-start.5 = (f32[32,24,128]{2,1,0:T(8,128)S(1)}, f32[32,24,128]{2,1,0:T(8,128)S(1)}, u32[]{:S(2)}, u32[]{:S(2)}) collective-permute-start(f32[32,24,128]{2,1,0:T(8,128)S(1)} %get-tuple-element.63), channel_id=1, source_target_pairs={{1,0},{2,1},{3,2},{4,3},{5,4},{6,5},{7,6},{9,8},{10,9},{11,10},{12... | collective-permute-start | bytes 1179656 | tf_op jit(solution)/shard_map/ppermute | solution.py:122
  145.5 44.0 %collective-permute-start.6 = (f32[8,24,16,128]{3,2,1,0:T(8,128)S(1)}, f32[8,24,16,128]{3,2,1,0:T(8,128)S(1)}, u32[]{:S(2)}, u32[]{:S(2)}) collective-permute-start(f32[8,24,16,128]{3,2,1,0:T(8,128)S(1)} %get-tuple-element.64), channel_id=1, source_target_pairs={{0,8},{8,16},{16,24},{1,9},{9,17},{17,25},{2,10},{10,18},{18,26},{... | collective-permute-start | bytes 4718600 | tf_op jit(solution)/shard_map/ppermute | solution.py:118
  159.6 29.9 %collective-permute-start.7 = (f32[8,24,16,128]{3,2,1,0:T(8,128)S(1)}, f32[8,24,16,128]{3,2,1,0:T(8,128)S(1)}, u32[]{:S(2)}, u32[]{:S(2)}) collective-permute-start(f32[8,24,16,128]{3,2,1,0:T(8,128)S(1)} %get-tuple-element.65), channel_id=1, source_target_pairs={{8,0},{16,8},{24,16},{9,1},{17,9},{25,17},{10,2},{18,10},{26,18},{... | collective-permute-start | bytes 4718600 | tf_op jit(solution)/shard_map/ppermute | solution.py:122
  164.6 18.7 %collective-permute-start.12 = (f32[24,48,128]{2,1,0:T(8,128)S(1)}, f32[24,48,128]{2,1,0:T(8,128)S(1)}, u32[]{:S(2)}, u32[]{:S(2)}) collective-permute-start(f32[24,48,128]{2,1,0:T(8,128)S(1)} %get-tuple-element.76), channel_id=1, source_target_pairs={{0,8},{8,16},{16,24},{1,9},{9,17},{17,25},{2,10},{10,18},{18,26},{... | collective-permute-start | bytes 1769480 | tf_op jit(solution)/shard_map/ppermute | solution.py:118
  167.4 22.1 %collective-permute-start.13 = (f32[24,48,128]{2,1,0:T(8,128)S(1)}, f32[24,48,128]{2,1,0:T(8,128)S(1)}, u32[]{:S(2)}, u32[]{:S(2)}) collective-permute-start(f32[24,48,128]{2,1,0:T(8,128)S(1)} %get-tuple-element.77), channel_id=1, source_target_pairs={{8,0},{16,8},{24,16},{9,1},{17,9},{25,17},{10,2},{18,10},{26,18},{... | collective-permute-start | bytes 1769480 | tf_op jit(solution)/shard_map/ppermute | solution.py:122
  171.7 43.0 %collective-permute-start.15 = (f32[32,24,128]{2,1,0:T(8,128)S(1)}, f32[32,24,128]{2,1,0:T(8,128)S(1)}, u32[]{:S(2)}, u32[]{:S(2)}) collective-permute-start(f32[32,24,128]{2,1,0:T(8,128)S(1)} %get-tuple-element.81), channel_id=1, source_target_pairs={{1,0},{2,1},{3,2},{4,3},{5,4},{6,5},{7,6},{9,8},{10,9},{11,10},{12... | collective-permute-start | bytes 1179656 | tf_op jit(solution)/shard_map/ppermute | solution.py:122
  183.3 31.4 %collective-permute-start.14 = (f32[32,24,128]{2,1,0:T(8,128)S(1)}, f32[32,24,128]{2,1,0:T(8,128)S(1)}, u32[]{:S(2)}, u32[]{:S(2)}) collective-permute-start(f32[32,24,128]{2,1,0:T(8,128)S(1)} %get-tuple-element.82), channel_id=1, source_target_pairs={{0,1},{1,2},{2,3},{3,4},{4,5},{5,6},{6,7},{8,9},{9,10},{10,11},{11... | collective-permute-start | bytes 1179656 | tf_op jit(solution)/shard_map/ppermute | solution.py:118
  218.9 50.2 %all-to-all-start.3 = ((f32[8,32,16,128]{3,2,1,0:T(8,128)}), f32[8,32,16,128]{3,2,1,0:T(8,128)}, u32[]{:S(2)}, u32[]{:S(2)}) async-start(f32[8,32,16,128]{3,2,1,0:T(8,128)} %copy-done.8), calls=%async_computation.3 | async-start | bytes 4194304 | tf_op jit(solution)/shard_map/all_to_all | solution.py:552
  223.5 26.5 %collective-permute-start.16 = (f32[24,176,128]{2,1,0:T(8,128)}, f32[24,176,128]{2,1,0:T(8,128)S(1)}, u32[]{:S(2)}, u32[]{:S(2)}) collective-permute-start(f32[24,176,128]{2,1,0:T(8,128)} %get-tuple-element.87), channel_id=1, source_target_pairs={{0,8},{8,16},{16,24},{1,9},{9,17},{17,25},{2,10},{10,18},{18,26},{... | collective-permute-start | bytes 6488072 | tf_op jit(solution)/shard_map/ppermute | solution.py:118
  226.0 28.3 %collective-permute-start.17 = (f32[24,176,128]{2,1,0:T(8,128)}, f32[24,176,128]{2,1,0:T(8,128)S(1)}, u32[]{:S(2)}, u32[]{:S(2)}) collective-permute-start(f32[24,176,128]{2,1,0:T(8,128)} %get-tuple-element.88), channel_id=1, source_target_pairs={{8,0},{16,8},{24,16},{9,1},{17,9},{25,17},{10,2},{18,10},{26,18},{... | collective-permute-start | bytes 6488072 | tf_op jit(solution)/shard_map/ppermute | solution.py:122
  254.4 11.0 %collective-permute-start.18 = (f32[32,24,128]{2,1,0:T(8,128)S(1)}, f32[32,24,128]{2,1,0:T(8,128)S(1)}, u32[]{:S(2)}, u32[]{:S(2)}) collective-permute-start(f32[32,24,128]{2,1,0:T(8,128)S(1)} %get-tuple-element.89), channel_id=1, source_target_pairs={{0,1},{1,2},{2,3},{3,4},{4,5},{5,6},{6,7},{8,9},{9,10},{10,11},{11... | collective-permute-start | bytes 1179656 | tf_op jit(solution)/shard_map/ppermute | solution.py:118
  258.5 8.5 %collective-permute-start.19 = (f32[32,24,128]{2,1,0:T(8,128)S(1)}, f32[32,24,128]{2,1,0:T(8,128)S(1)}, u32[]{:S(2)}, u32[]{:S(2)}) collective-permute-start(f32[32,24,128]{2,1,0:T(8,128)S(1)} %get-tuple-element.90), channel_id=1, source_target_pairs={{1,0},{2,1},{3,2},{4,3},{5,4},{6,5},{7,6},{9,8},{10,9},{11,10},{12... | collective-permute-start | bytes 1179656 | tf_op jit(solution)/shard_map/ppermute | solution.py:122
  269.0 52.9 %all-to-all-start.2 = ((f32[8,32,16,128]{3,2,1,0:T(8,128)}), f32[8,32,16,128]{3,2,1,0:T(8,128)S(1)}, u32[]{:S(2)}, u32[]{:S(2)}) async-start(f32[8,32,16,128]{3,2,1,0:T(8,128)} %copy-done.10), calls=%async_computation.2 | async-start | bytes 4194304 | tf_op jit(solution)/shard_map/all_to_all | solution.py:552
  (30 other events, 281.7 us)
